TPU v7x, 32 devices: a whole 2x2x4 slice. The times are simulated.
32 devices in a mesh: dp: 16 (over z, y, x), tensor: 2 (over core).
Axes of the slice: x: 2, y: 2, z: 4, core: 2. Of those that a mesh axis runs over, the one named last changes fastest.
Arguments:
- text_input: bfloat16 [32, 512, 768], P(('dp', 'tensor')), may hold values from -6 to 6
- layout_input: bfloat16 [32, 512, 192], P(('dp', 'tensor')), may hold values from -6 to 6
- page_counts: int32 [32], P(('dp', 'tensor')), may hold values from 16 to 512, as said below
- text_joint: bfloat16 [768, 2304], replicated, may hold values from -0.21875 to 0.21875
- text_mixing: bfloat16 [768, 768], replicated, may hold values from -0.625 to 0.625
- text_norms: float32 [4, 768], replicated, may hold values from 0.1 to 1.9
- text_upward: bfloat16 [768, 3072], P(None, 'tensor'), may hold values from -0.21875 to 0.21875
- text_downward: bfloat16 [3072, 768], P('tensor'), may hold values from -0.109375 to 0.109375
- layout_joint: bfloat16 [192, 576], replicated, may hold values from -0.4375 to 0.4375
- layout_mixing: bfloat16 [192, 192], replicated, may hold values from -1.25 to 1.25
- layout_norms: float32 [4, 192], replicated, may hold values from 0.1 to 1.9
- layout_upward: bfloat16 [192, 768], P(None, 'tensor'), may hold values from -0.4375 to 0.4375
- layout_downward: bfloat16 [768, 192], P('tensor'), may hold values from -0.21875 to 0.21875
- text_cotangent: bfloat16 [32, 512, 768], P(('dp', 'tensor')), may hold values from -6 to 6
- layout_cotangent: bfloat16 [32, 512, 192], P(('dp', 'tensor')), may hold values from -6 to 6
Outputs:
- text_result: bfloat16 [32, 512, 768], P(('dp', 'tensor'))
- layout_result: bfloat16 [32, 512, 192], P(('dp', 'tensor'))
- text_gradient: float32 [32, 512, 768], P(('dp', 'tensor'))
- layout_gradient: float32 [32, 512, 192], P(('dp', 'tensor'))
- joint_text_gradient: float32 [768, 2304], replicated
- mixing_text_gradient: float32 [768, 768], replicated
- norms_text_gradient: float32 [4, 768], replicated
- upward_text_gradient: float32 [768, 3072], P(None, 'tensor')
- downward_text_gradient: float32 [3072, 768], P('tensor')
- joint_layout_gradient: float32 [192, 576], replicated
- mixing_layout_gradient: float32 [192, 192], replicated
- norms_layout_gradient: float32 [4, 192], replicated
- upward_layout_gradient: float32 [192, 768], P(None, 'tensor')
- downward_layout_gradient: float32 [768, 192], P('tensor')
Inputs may be any that keep to these rules, and one draw needn't show every extreme that they name: `page_counts`: keys of a page in slots below its count are live; some page has all 512 slots live; counts are spread over several powers of two.
All inputs are finite; a program needn't handle non-finite values.
Results may differ from a plain program's by a relative error of at most 0.015.
Values may be sent and summed in bfloat16 or wider, within the bound.
No kernel may reach another device: no remote copies, remote signals or barrier semaphores. Data moves between devices by JAX's collectives and lax.ppermute only.
A program may use at most 192 MiB of HBM per device.

v0:
```python
import math

import jax
import jax.numpy as jnp
from jax import lax
from jax.sharding import PartitionSpec as P

HEADS = 12


NEG_FILL = -1e30


def normalize(hidden, gain, shift):
    center = hidden - jnp.mean(hidden, axis=-1, keepdims=True)
    spread = jnp.mean(center * center, axis=-1, keepdims=True)
    return center * lax.rsqrt(spread + 1e-05) * gain + shift


def gelu_exact(value):
    return jax.nn.gelu(value, approximate=False)


def scores_of(queries, keys_in, scale):
    return jnp.einsum("qhd,khd->hqk", queries, keys_in, preferred_element_type=jnp.float32) * scale


def logits_pair(text_grid, layout_grid, count):
    slots = text_grid.shape[0]
    text_score = scores_of(text_grid[:, 0], text_grid[:, 1], 1.0 / math.sqrt(text_grid.shape[-1]))
    layout_score = scores_of(
        layout_grid[:, 0], layout_grid[:, 1], 1.0 / math.sqrt(layout_grid.shape[-1])
    )
    live = (jnp.arange(slots) < count)[None, None, :]
    return (
        jnp.where(live, text_score + layout_score, NEG_FILL),
        jnp.where(live, layout_score + text_score, NEG_FILL),
    )


def attend(logits, values):
    top = jnp.max(logits, axis=-1, keepdims=True)
    total = top + jnp.log(jnp.sum(jnp.exp(logits - top), axis=-1, keepdims=True))
    weights = jnp.exp(logits - total).astype(jnp.bfloat16)
    mixed = jnp.einsum("hqk,khd->qhd", weights, values, preferred_element_type=jnp.float32)
    return (mixed.astype(jnp.bfloat16), total)


def page_forward(items):
    text_grid, layout_grid, count = items
    text_logits, layout_logits = logits_pair(text_grid, layout_grid, count)
    text_mixed, text_total = attend(text_logits, text_grid[:, 2])
    layout_mixed, layout_total = attend(layout_logits, layout_grid[:, 2])
    return (text_mixed, layout_mixed, text_total, layout_total)


def probs_back(logits, total, values, upstream):
    probs = jnp.exp(logits - total)
    value_grad = jnp.einsum(
        "hqk,qhd->khd", probs.astype(jnp.bfloat16), upstream, preferred_element_type=jnp.float32
    )
    prob_grad = jnp.einsum("qhd,khd->hqk", upstream, values, preferred_element_type=jnp.float32)
    logit_grad = probs * (prob_grad - jnp.sum(prob_grad * probs, axis=-1, keepdims=True))
    return (logit_grad, value_grad)


def joint_grads(grid, score_grad, value_grad):
    scale = 1.0 / math.sqrt(grid.shape[-1])
    query_grad = (
        jnp.einsum("hqk,khd->qhd", score_grad, grid[:, 1], preferred_element_type=jnp.float32)
        * scale
    )
    key_grad = (
        jnp.einsum("hqk,qhd->khd", score_grad, grid[:, 0], preferred_element_type=jnp.float32)
        * scale
    )
    return jnp.stack([query_grad, key_grad, value_grad], axis=1).astype(jnp.bfloat16)


def page_backward(items):
    text_grid, layout_grid, count, text_total, layout_total, text_upper, layout_upper = items
    text_logits, layout_logits = logits_pair(text_grid, layout_grid, count)
    text_lgrad, text_vgrad = probs_back(text_logits, text_total, text_grid[:, 2], text_upper)
    layout_lgrad, layout_vgrad = probs_back(
        layout_logits, layout_total, layout_grid[:, 2], layout_upper
    )
    text_sgrad = text_lgrad.astype(jnp.bfloat16)
    layout_sgrad = (text_lgrad + layout_lgrad).astype(jnp.bfloat16)
    return (
        joint_grads(text_grid, text_sgrad, text_vgrad),
        joint_grads(layout_grid, layout_sgrad, layout_vgrad),
    )


def matmul(left, right):
    return jnp.dot(left, right, preferred_element_type=jnp.float32)


def shards(
    text_input,
    layout_input,
    page_counts,
    text_joint,
    text_mixing,
    text_norms,
    text_upward,
    text_downward,
    layout_joint,
    layout_mixing,
    layout_norms,
    layout_upward,
    layout_downward,
    text_cotangent,
    layout_cotangent,
):
    pages, slots, width_text = text_input.shape
    width_layout = layout_input.shape[2]
    text_rows = text_input.reshape(-1, width_text)
    layout_rows = layout_input.reshape(-1, width_layout)
    text_grid = (
        matmul(text_rows, text_joint).astype(jnp.bfloat16).reshape(pages, slots, 3, HEADS, -1)
    )
    layout_grid = (
        matmul(layout_rows, layout_joint).astype(jnp.bfloat16).reshape(pages, slots, 3, HEADS, -1)
    )
    text_mixed, layout_mixed, text_total, layout_total = lax.map(
        page_forward, (text_grid, layout_grid, page_counts)
    )
    text_mixed = text_mixed.reshape(-1, width_text)
    layout_mixed = layout_mixed.reshape(-1, width_layout)
    text_resid = text_rows.astype(jnp.float32) + matmul(text_mixed, text_mixing)
    layout_resid = layout_rows.astype(jnp.float32) + matmul(layout_mixed, layout_mixing)
    text_first, text_pull_one = jax.vjp(normalize, text_resid, text_norms[0], text_norms[1])
    layout_first, layout_pull_one = jax.vjp(
        normalize, layout_resid, layout_norms[0], layout_norms[1]
    )
    text_low = text_first.astype(jnp.bfloat16)
    layout_low = layout_first.astype(jnp.bfloat16)
    text_inputs, layout_inputs = (
        lax.all_gather(text_low, "tensor", axis=0, tiled=True),
        lax.all_gather(layout_low, "tensor", axis=0, tiled=True),
    )
    text_up_w, text_down_w, layout_up_w, layout_down_w = (
        text_upward,
        text_downward,
        layout_upward,
        layout_downward,
    )
    text_hidden = matmul(text_inputs, text_up_w)
    layout_hidden = matmul(layout_inputs, layout_up_w)
    text_active, text_gelu_pull = jax.vjp(gelu_exact, text_hidden)
    layout_active, layout_gelu_pull = jax.vjp(gelu_exact, layout_hidden)
    text_active = text_active.astype(jnp.bfloat16)
    layout_active = layout_active.astype(jnp.bfloat16)
    text_partial = matmul(text_active, text_down_w)
    layout_partial = matmul(layout_active, layout_down_w)
    text_feed, layout_feed = (
        lax.psum_scatter(text_partial, "tensor", scatter_dimension=0, tiled=True),
        lax.psum_scatter(layout_partial, "tensor", scatter_dimension=0, tiled=True),
    )
    text_out, text_pull_two = jax.vjp(
        normalize, text_first + text_feed, text_norms[2], text_norms[3]
    )
    layout_out, layout_pull_two = jax.vjp(
        normalize, layout_first + layout_feed, layout_norms[2], layout_norms[3]
    )
    text_result = text_out.astype(jnp.bfloat16).reshape(pages, slots, width_text)
    layout_result = layout_out.astype(jnp.bfloat16).reshape(pages, slots, width_layout)
    text_dsecond, text_dgain_two, text_dshift_two = text_pull_two(
        text_cotangent.reshape(-1, width_text).astype(jnp.float32)
    )
    layout_dsecond, layout_dgain_two, layout_dshift_two = layout_pull_two(
        layout_cotangent.reshape(-1, width_layout).astype(jnp.float32)
    )
    text_dfeed = text_dsecond.astype(jnp.bfloat16)
    layout_dfeed = layout_dsecond.astype(jnp.bfloat16)
    text_dfeed_all, layout_dfeed_all = (
        lax.all_gather(text_dfeed, "tensor", axis=0, tiled=True),
        lax.all_gather(layout_dfeed, "tensor", axis=0, tiled=True),
    )
    text_dhidden = text_gelu_pull(matmul(text_dfeed_all, text_down_w.T))[0].astype(jnp.bfloat16)
    layout_dhidden = layout_gelu_pull(matmul(layout_dfeed_all, layout_down_w.T))[0].astype(
        jnp.bfloat16
    )
    text_down_grad = matmul(text_active.T, text_dfeed_all)
    layout_down_grad = matmul(layout_active.T, layout_dfeed_all)
    text_up_grad = matmul(text_inputs.T, text_dhidden)
    layout_up_grad = matmul(layout_inputs.T, layout_dhidden)
    text_dinput = matmul(text_dhidden, text_up_w.T)
    layout_dinput = matmul(layout_dhidden, layout_up_w.T)
    text_dinput, layout_dinput = (
        lax.psum_scatter(text_dinput, "tensor", scatter_dimension=0, tiled=True),
        lax.psum_scatter(layout_dinput, "tensor", scatter_dimension=0, tiled=True),
    )
    text_up_grad, text_down_grad, layout_up_grad, layout_down_grad = (
        lax.psum(text_up_grad.astype(jnp.bfloat16), "dp").astype(jnp.float32),
        lax.psum(text_down_grad.astype(jnp.bfloat16), "dp").astype(jnp.float32),
        lax.psum(layout_up_grad.astype(jnp.bfloat16), "dp").astype(jnp.float32),
        lax.psum(layout_down_grad.astype(jnp.bfloat16), "dp").astype(jnp.float32),
    )
    text_dresid, text_dgain_one, text_dshift_one = text_pull_one(text_dsecond + text_dinput)
    layout_dresid, layout_dgain_one, layout_dshift_one = layout_pull_one(
        layout_dsecond + layout_dinput
    )
    text_datt = text_dresid.astype(jnp.bfloat16)
    layout_datt = layout_dresid.astype(jnp.bfloat16)
    text_mix_grad = matmul(text_mixed.T, text_datt)
    layout_mix_grad = matmul(layout_mixed.T, layout_datt)
    text_dmixed = (
        matmul(text_datt, text_mixing.T).astype(jnp.bfloat16).reshape(pages, slots, HEADS, -1)
    )
    layout_dmixed = (
        matmul(layout_datt, layout_mixing.T).astype(jnp.bfloat16).reshape(pages, slots, HEADS, -1)
    )
    text_djoint, layout_djoint = lax.map(
        page_backward,
        (text_grid, layout_grid, page_counts, text_total, layout_total, text_dmixed, layout_dmixed),
    )
    text_djoint = text_djoint.reshape(-1, 3 * width_text)
    layout_djoint = layout_djoint.reshape(-1, 3 * width_layout)
    text_joint_grad = matmul(text_rows.T, text_djoint)
    layout_joint_grad = matmul(layout_rows.T, layout_djoint)
    text_gradient = (text_dresid + matmul(text_djoint, text_joint.T)).reshape(
        pages, slots, width_text
    )
    layout_gradient = (layout_dresid + matmul(layout_djoint, layout_joint.T)).reshape(
        pages, slots, width_layout
    )
    text_norm_grad = jnp.stack([text_dgain_one, text_dshift_one, text_dgain_two, text_dshift_two])
    layout_norm_grad = jnp.stack(
        [layout_dgain_one, layout_dshift_one, layout_dgain_two, layout_dshift_two]
    )
    (
        text_joint_grad,
        text_mix_grad,
        text_norm_grad,
        layout_joint_grad,
        layout_mix_grad,
        layout_norm_grad,
    ) = lax.psum(
        (
            text_joint_grad,
            text_mix_grad,
            text_norm_grad,
            layout_joint_grad,
            layout_mix_grad,
            layout_norm_grad,
        ),
        ("dp", "tensor"),
    )
    return (
        text_result,
        layout_result,
        text_gradient,
        layout_gradient,
        text_joint_grad,
        text_mix_grad,
        text_norm_grad,
        text_up_grad,
        text_down_grad,
        layout_joint_grad,
        layout_mix_grad,
        layout_norm_grad,
        layout_up_grad,
        layout_down_grad,
    )


def solution(mesh):
    return jax.shard_map(
        shards,
        mesh=mesh,
        in_specs=(
            P(("dp", "tensor"), None, None),
            P(("dp", "tensor"), None, None),
            P(("dp", "tensor")),
            P(),
            P(),
            P(),
            P(None, "tensor"),
            P("tensor", None),
            P(),
            P(),
            P(),
            P(None, "tensor"),
            P("tensor", None),
            P(("dp", "tensor"), None, None),
            P(("dp", "tensor"), None, None),
        ),
        out_specs=(
            P(("dp", "tensor"), None, None),
            P(("dp", "tensor"), None, None),
            P(("dp", "tensor"), None, None),
            P(("dp", "tensor"), None, None),
            P(),
            P(),
            P(),
            P(None, "tensor"),
            P("tensor", None),
            P(),
            P(),
            P(),
            P(None, "tensor"),
            P("tensor", None),
        ),
        check_vma=False,
    )
```

profile of v0, /device:TPU:0, one launch (start us, length us, event | category | flops | bytes accessed | tf_op | source)
XLA Modules:
  0.0 606.4 jit_solution(1691573093866012901)
XLA Ops:
  9.2 4.5 convolution_convert_fusion
  18.0 7.8 %fusion.50 = f32[12,512,512]{1,2,0:T(8,128)} fusion(bf16[512,3,12,64]{0,3,2,1:T(8,128)(2,1)} %bitcast.190), kind=kOutput, calls=%fused_computation.103 | convolution fusion | flops 402653184 | bytes 14155776 | tf_op jit(solution)/shard_map/while/body/eval_jaxpr/qhd,khd->hqk/dot_general | solution.py:25
  26.9 6.8 %fusion.82 = (f32[12,512]{1,0:T(8,128)S(1)}, f32[12,512,512]{1,2,0:T(8,128)S(1)}) fusion(bf16[512,3,12,16]{0,3,2,1:T(8,128)(2,1)S(1)} %bitcast.203, f32[12,512,512]{1,2,0:T(8,128)} %fusion.50, pred[512]{0:T(512)(128)(4,1)S(1)} %iota_compare_fusion), kind=kOutput, calls=%fused_computation.171 | convolution fusion | flops 116385792 | bytes 25584128 | tf_op jit(solution)/shard_map/while/body/eval_jaxpr/qhd,khd->hqk/dot_general | solution.py:25
  38.2 9.4 %fusion.5 = bf16[12,512,512]{1,2,0:T(8,128)(2,1)} fusion(f32[12,512,512]{1,2,0:T(8,128)} %copy-done.1, f32[12,512]{1,0:T(8,128)S(1)} %log_add_fusion), kind=kLoop, calls=%fused_computation.11 | loop fusion | flops 6291456 | bytes 18898944 | tf_op jit(solution)/shard_map/while/body/eval_jaxpr/convert_element_type | solution.py:44
  63.7 4.8 multiply_convert_fusion.1
  70.9 19.8 %multiply_convert_fusion = (bf16[1024,1536]{1,0:T(8,128)(2,1)S(1)}, f32[1024,1536]{1,0:T(8,128)}, f32[1024,1536]{1,0:T(8,128)}) fusion(bf16[1024,768]{1,0:T(8,128)(2,1)} %all-gather.3.cloned.1.call-done, bf16[768,1536]{1,0:T(8,128)(2,1)} %param.21), kind=kOutput, calls=%fused_computation.14 | convolution fusion | flops 2518155264 | bytes 19660800 | tf_op jit(solution)/shard_map/dot_general | solution.py:96
  100.5 9.9 %reduce-scatter.5.cloned.1.call-done = f32[512,768]{1,0:T(8,128)} async-done(((f32[1024,768]{1,0:T(8,128)}), f32[512,768]{1,0:T(8,128)}) %reduce-scatter.5.cloned.1.call-update) | async-done | bytes 1572880 | tf_op jit(solution)/shard_map/reduce_scatter | solution.py:158
  118.3 12.3 %reduce-scatter.11.cloned.1.call-start = ((), (), s32[]{:S(2)}) async-start(), calls=%async_computation.9 | async-start | bytes 1179648 | tf_op jit(solution)/shard_map/reduce_scatter | solution.py:193
  141.8 9.9 %add_convert_fusion.1 = bf16[1024,1536]{1,0:T(8,128)(2,1)S(1)} fusion(f32[1024,1536]{1,0:T(8,128)} %get-tuple-element.151, f32[1024,1536]{1,0:T(8,128)} %get-tuple-element.164, bf16[1024,768]{1,0:T(8,128)(2,1)} %all-gather.5.cloned.1.call-done, bf16[1536,768]{1,0:T(8,128)(2,1)} %param.22), kind=kOutput, calls=%fused_computation.13 | convolution fusion | flops 2437939200 | bytes 19660800 | tf_op jit(solution)/shard_map/dot_general | solution.py:96
  153.4 4.3 fusion.87
  168.8 5.4 convolution_bitcast_fusion.3
  174.2 7.4 %fusion.62 = f32[12,512,512]{1,2,0:T(8,128)} fusion(bf16[512,12,16]{0,2,1:T(8,128)(2,1)S(1)} %bitcast.211, bf16[512,3,12,16]{0,3,2,1:T(8,128)(2,1)} %bitcast.205), kind=kOutput, calls=%fused_computation.131 | convolution fusion | flops 100663296 | bytes 12976128 | tf_op jit(solution)/shard_map/while/body/eval_jaxpr/qhd,khd->hqk/dot_general | solution.py:62
  199.5 12.8 %multiply_reduce_fusion.1 = (f32[12,512]{1,0:T(8,128)}, f32[12,512,512]{1,2,0:T(8,128)}) fusion(f32[12,512,512]{1,2,0:T(8,128)} %copy-done.1, f32[12,512]{1,0:T(8,128)} %copy-done.31, bf16[512,12,64]{0,2,1:T(8,128)(2,1)} %bitcast.197, bf16[512,3,12,64]{0,3,2,1:T(8,128)(2,1)} %bitcast.191), kind=kOutput, calls=%fused_computation.5 | convolution fusion | flops 412084224 | bytes 26796032 | tf_op jit(solution)/shard_map/while/body/eval_jaxpr/qhd,khd->hqk/dot_general | solution.py:62
  212.2 22.8 %fusion.43 = bf16[512,1,12,16]{0,3,2,1:T(8,128)(2,1)} fusion(f32[12,512,512]{1,2,0:T(8,128)} %fusion.62, f32[12,512,512]{1,2,0:T(8,128)} %get-tuple-element.169, f32[12,512,512]{1,2,0:T(8,128)} %copy-done.1, f32[12,512]{1,0:T(8,128)} %get-tuple-element.168, f32[12,512]{1,0:T(8,128)} %copy-done.31, bf16[512,3,12,16]{0,3,2,1:T(8,128)(2,1)} %bitcast.206), kind=kOutput, calls=%fused_computation.90 | convolution fusion | flops 129178112 | bytes 63406080 | tf_op jit(solution)/shard_map/while/body/eval_jaxpr/hqk,qhd->khd/dot_general | solution.py:74
  235.0 22.6 %fusion.37 = bf16[512,1,12,16]{0,3,2,1:T(8,128)(2,1)} fusion(f32[12,512,512]{1,2,0:T(8,128)} %fusion.62, f32[12,512,512]{1,2,0:T(8,128)} %get-tuple-element.169, f32[12,512,512]{1,2,0:T(8,128)} %copy-done.1, f32[12,512]{1,0:T(8,128)} %get-tuple-element.168, f32[12,512]{1,0:T(8,128)} %copy-done.31, bf16[512,3,12,16]{0,3,2,1:T(8,128)(2,1)} %bitcast.207), kind=kOutput, calls=%fused_computation.88 | convolution fusion | flops 129178112 | bytes 63406080 | tf_op jit(solution)/shard_map/while/body/eval_jaxpr/hqk,khd->qhd/dot_general | solution.py:70
  258.9 5.3 convolution_bitcast_fusion.1
  264.2 10.0 %fusion.2 = bf16[12,512,512]{1,2,0:T(8,128)(2,1)S(1)} fusion(f32[12,512,512]{1,2,0:T(8,128)} %get-tuple-element.169, f32[12,512,512]{1,2,0:T(8,128)} %copy-done.1, f32[12,512]{1,0:T(8,128)S(1)} %copy-done.42, f32[12,512]{1,0:T(8,128)S(1)} %copy-done.32), kind=kLoop, calls=%fused_computation.9 | loop fusion | flops 12582912 | bytes 31506432 | tf_op jit(solution)/shard_map/while/body/eval_jaxpr/convert_element_type | solution.py:87
  282.6 5.0 convolution_bitcast_fusion
  291.8 86.3 %all-reduce.8.cloned.1.call-done = (bf16[768,1536]{1,0:T(8,128)(2,1)}, bf16[1536,768]{1,0:T(8,128)(2,1)}, bf16[192,384]{1,0:T(8,128)(2,1)}, bf16[384,192]{0,1:T(8,128)(2,1)}) async-done(((bf16[768,1536]{1,0:T(8,128)(2,1)}, bf16[1536,768]{1,0:T(8,128)(2,1)}, bf16[192,384]{1,0:T(8,128)(2,1)}, bf16[384,192]{0,1:T(8,128)(2,1)}), (bf16[768,1536]{1,0:T(8,128)(2,1)}, bf16[1536,768]{1,0:T(8,128)(2,1)}, ...) | async-done | bytes 5013520 | tf_op jit(solution)/shard_map/psum | solution.py:196
  378.2 4.6 convert_element_type.188
  387.0 41.7 %all-reduce = (f32[4,768]{1,0:T(4,128)}, f32[4,192]{1,0:T(4,128)}) all-reduce(f32[4,768]{1,0:T(4,128)S(1)} %pad_maximum_fusion, f32[4,192]{1,0:T(4,128)} %pad_maximum_fusion.1), channel_id=1, replica_groups=mesh['dp'=16,'tensor'=2] {'dp','tensor'}, use_global_device_ids=true, to_apply=%region_30.31 | all-reduce | flops 3840 | bytes 30720 | tf_op jit(solution)/shard_map/psum | solution.py:240
  431.0 5.5 add_bitcast_fusion
  436.5 149.9 %all-reduce.6.cloned.1.call-done = (f32[768,2304]{0,1:T(8,128)}, f32[768,768]{1,0:T(8,128)}, f32[192,576]{1,0:T(8,128)}, f32[192,192]{1,0:T(8,128)}) async-done(((f32[768,2304]{0,1:T(8,128)}, f32[768,768]{1,0:T(8,128)}, f32[192,576]{1,0:T(8,128)}, f32[192,192]{1,0:T(8,128)}), (f32[768,2304]{0,1:T(8,128)}, f32[768,768]{1,0:T(8,128)}, f32[192,576]{1,0:T(8,128)}, ...) | async-done | bytes 10027024 | tf_op jit(solution)/shard_map/psum | solution.py:240
  586.4 8.0 %copy.53 = f32[768,2304]{1,0:T(8,128)} copy(f32[768,2304]{0,1:T(8,128)} %get-tuple-element.128) | data formatting | bytes 14155776
  (258 shorter events, 113.3 us)
Async XLA Ops:
  7.2 63.6 %all-gather.3.cloned.1.call-start = ((), (), s32[]{:S(2)}) async-start(), calls=%async_computation.4 | async-start | bytes 2359296 | tf_op jit(solution)/shard_map/all_gather | solution.py:140
  18.0 8.5 %copy-start.23 = (bf16[1,512,192]{1,2,0:T(8,128)(2,1)S(1)}, bf16[1,512,192]{1,2,0:T(8,128)(2,1)}, u32[]{:S(2)}) copy-start(bf16[1,512,192]{1,2,0:T(8,128)(2,1)} %param.16) | copy-start | bytes 589828
  18.0 8.5 %copy-start.28 = (bf16[192,576]{1,0:T(8,128)(2,1)S(1)}, bf16[192,576]{1,0:T(8,128)(2,1)}, u32[]{:S(2)}) copy-start(bf16[192,576]{1,0:T(8,128)(2,1)} %param.23) | copy-start | bytes 663556
  26.8 6.8 %copy-start.17 = (bf16[512,576]{0,1:T(8,128)(2,1)}, bf16[512,576]{0,1:T(8,128)(2,1)S(1)}, u32[]{:S(2)}) copy-start(bf16[512,576]{0,1:T(8,128)(2,1)S(1)} %convolution_convert_fusion.5) | copy-start | bytes 1769476
  38.2 9.4 %copy-start.31 = (f32[12,512]{1,0:T(8,128)}, f32[12,512]{1,0:T(8,128)S(1)}, u32[]{:S(2)}) copy-start(f32[12,512]{1,0:T(8,128)S(1)} %log_add_fusion) | copy-start | bytes 73732
  38.2 9.4 %copy-start.4 = (bf16[512,2304]{0,1:T(8,128)(2,1)S(1)}, bf16[512,2304]{0,1:T(8,128)(2,1)}, u32[]{:S(2)}) copy-start(bf16[512,2304]{0,1:T(8,128)(2,1)} %copy.43) | copy-start | bytes 7077892
  55.7 41.0 %reduce-scatter.7.cloned.1.call-start = ((), (), s32[]{:S(2)}) async-start(), calls=%async_computation.6 | async-start | bytes 1179648 | tf_op jit(solution)/shard_map/reduce_scatter | solution.py:159
  59.9 8.6 %copy-start.20 = (bf16[12,512,16]{1,2,0:T(8,128)(2,1)}, bf16[12,512,16]{1,2,0:T(8,128)(2,1)S(1)}, u32[]{:S(2)}) copy-start(bf16[12,512,16]{1,2,0:T(8,128)(2,1)S(1)} %convolution_convert_fusion.7) | copy-start | bytes 589828
  63.7 5.7 copy-start.39
  70.8 39.6 %reduce-scatter.5.cloned.1.call-start = ((), (), s32[]{:S(2)}) async-start(), calls=%async_computation.5 | async-start | bytes 4718592 | tf_op jit(solution)/shard_map/reduce_scatter | solution.py:158
  70.8 21.5 %copy-start.70 = (bf16[1536,768]{1,0:T(8,128)(2,1)S(1)}, bf16[1536,768]{1,0:T(8,128)(2,1)}, u32[]{:S(2)}) copy-start(bf16[1536,768]{1,0:T(8,128)(2,1)} %param.22) | copy-start | bytes 7077892
  96.7 45.1 %all-gather.5.cloned.1.call-start = ((), (), s32[]{:S(2)}) async-start(), calls=%async_computation.7 | async-start | bytes 2359296 | tf_op jit(solution)/shard_map/all_gather | solution.py:178
  118.3 44.1 %reduce-scatter.11.cloned.1.call-start = ((), (), s32[]{:S(2)}) async-start(), calls=%async_computation.9 | async-start | bytes 1179648 | tf_op jit(solution)/shard_map/reduce_scatter | solution.py:193
  141.7 47.9 %reduce-scatter.9.cloned.1.call-start = ((), (), s32[]{:S(2)}) async-start(), calls=%async_computation.8 | async-start | bytes 4718592 | tf_op jit(solution)/shard_map/reduce_scatter | solution.py:192
  141.8 11.6 %copy-start.71 = (bf16[768,1536]{1,0:T(8,128)(2,1)S(1)}, bf16[768,1536]{1,0:T(8,128)(2,1)}, u32[]{:S(2)}) copy-start(bf16[768,1536]{1,0:T(8,128)(2,1)} %param.21) | copy-start | bytes 7077892
  157.7 220.5 %all-reduce.8.cloned.1.call-start = ((), (), s32[]{:S(2)}) async-start(), calls=%async_computation.11 | async-start | bytes 10027008 | tf_op jit(solution)/shard_map/psum | solution.py:196
  167.2 7.0 %copy-start.47 = (f32[512]{0:T(512)}, f32[512]{0:T(512)S(1)}, u32[]{:S(2)}) copy-start(f32[512]{0:T(512)S(1)} %negate_multiply_fusion.2) | copy-start | bytes 6148
  174.2 7.4 %copy-start.72 = (bf16[1024,768]{1,0:T(8,128)(2,1)S(1)}, bf16[1024,768]{1,0:T(8,128)(2,1)}, u32[]{:S(2)}) copy-start(bf16[1024,768]{1,0:T(8,128)(2,1)} %all-gather.3.cloned.1.call-done) | copy-start | bytes 4718596
  174.2 7.4 %copy-start.77 = (bf16[1024,1536]{1,0:T(8,128)(2,1)S(1)}, bf16[1024,1536]{1,0:T(8,128)(2,1)}, u32[]{:S(2)}) copy-start(bf16[1024,1536]{1,0:T(8,128)(2,1)} %copy-done.76) | copy-start | bytes 9437188
  189.6 396.8 %all-reduce.6.cloned.1.call-start = ((), (), s32[]{:S(2)}) async-start(), calls=%async_computation.10 | async-start | bytes 20250624 | tf_op jit(solution)/shard_map/psum | solution.py:240
  194.3 85.3 %copy-start.65 = (f32[512]{0:T(512)}, f32[512]{0:T(512)S(1)}, u32[]{:S(2)}) copy-start(f32[512]{0:T(512)S(1)} %negate_multiply_fusion.4) | copy-start | bytes 6148
  258.9 18.9 %copy-start.16 = (bf16[512,3,12,16]{0,3,2,1:T(8,128)(2,1)}, bf16[512,3,12,16]{0,3,2,1:T(8,128)(2,1)S(1)}, u32[]{:S(2)}) copy-start(bf16[512,3,12,16]{0,3,2,1:T(8,128)(2,1)S(1)} %maximum_convert_fusion.1) | copy-start | bytes 1769476
  264.2 10.1 %copy-start.5 = (bf16[512,2304]{0,1:T(8,128)(2,1)S(1)}, bf16[512,2304]{0,1:T(8,128)(2,1)}, u32[]{:S(2)}) copy-start(bf16[512,2304]{0,1:T(8,128)(2,1)} %copy.43) | copy-start | bytes 7077892
  382.9 45.8 %copy-start.48 = (f32[512]{0:T(512)S(1)}, f32[512]{0:T(512)}, u32[]{:S(2)}) copy-start(f32[512]{0:T(512)} %copy-done.47) | copy-start | bytes 6148
  (64 other events, 187.5 us)
Sparse Core Ops, SparseCore 0:
  55.8 12.4 all-gather.2
  70.9 10.8 reduce-scatter.6
  96.8 13.5 reduce-scatter.4
  118.4 10.9 all-gather.4
  141.8 9.3 reduce-scatter.10
  157.8 12.0 reduce-scatter.8
  189.7 188.4 all-reduce.7
  385.7 200.6 all-reduce.5
where the time goes:
time: 616 us; the launch traced here: 606 us
  waiting for transfers between devices  246 us (40%)
  matrix products  188 us (31%)
  other arithmetic  58.9 us (10%)
  blocking collectives  45.9 us (7%)
  local copies, waits for them, and re-layouts  37.9 us (6%)
  between operations  16.1 us (3%)
  starting transfers between devices  12.9 us (2%)
    psum x1, waiting for transfers between devices, shards(): lax.psum((text_joint_grad, text_mix_grad, text_norm_grad, layout_joint_gr...  150 us
    dot_general x24, matrix products, matmul(): return jnp.dot(left, right, preferred_element_type=jnp.float32)  86.4 us
    psum x1, waiting for transfers between devices, shards(): lax.psum(text_up_grad.astype(jnp.bfloat16), 'dp').astype(jnp.float32)  86.3 us
    psum x1, blocking collectives, shards(): lax.psum((text_joint_grad, text_mix_grad, text_norm_grad, layout_joint_gr...  41.7 us
    unnamed x164, local copies, waits for them, and re-layouts  28.8 us
    dot_general x2, matrix products, joint_grads(): jnp.einsum('hqk,qhd->khd', score_grad, grid[:, 0], preferred_element_type...  24.8 us
    dot_general x2, matrix products, joint_grads(): jnp.einsum('hqk,khd->qhd', score_grad, grid[:, 1], preferred_element_type...  23.8 us
    dot_general x2, matrix products, probs_back(): jnp.einsum('qhd,khd->hqk', upstream, values, preferred_element_type=jnp.f...  20.2 us
  transfers between devices with their start and end apart: 8, of which 3 were waited for; matrix products, arithmetic and copies ran while one was open for 34% of the time, Pallas kernels for 0%

commit v1 on v0

v1 whole, which is shorter than its diff:
```python
import functools
import math

import jax
import jax.numpy as jnp
from jax import lax
from jax.experimental import pallas as pl
from jax.experimental.pallas import tpu as pltpu
from jax.sharding import PartitionSpec as P

HEADS = 12
NEG_FILL = -1e30
EPS = 1e-05
F32 = jnp.float32
BF16 = jnp.bfloat16
VMEM_SPEC = pl.BlockSpec(memory_space=pltpu.VMEM)
SMEM_SPEC = pl.BlockSpec(memory_space=pltpu.SMEM)
VMEM_LIMIT = 16 * 1024 * 1024


def nn(left, right):
    return lax.dot_general(left, right, (((1,), (0,)), ((), ())), preferred_element_type=F32)


def nt(left, right):
    return lax.dot_general(left, right, (((1,), (1,)), ((), ())), preferred_element_type=F32)


def tn(left, right):
    return lax.dot_general(left, right, (((0,), (0,)), ((), ())), preferred_element_type=F32)


def gelu_pair(hidden):
    below = 0.5 * (1.0 + lax.erf(hidden * math.sqrt(0.5)))
    bell = jnp.exp(-0.5 * hidden * hidden)
    return hidden * below, below + hidden * bell * (1.0 / math.sqrt(2.0 * math.pi))


def unit(hidden):
    center = hidden - jnp.mean(hidden, axis=-1, keepdims=True)
    spread = jnp.mean(center * center, axis=-1, keepdims=True)
    rate = lax.rsqrt(spread + EPS)
    return center * rate, rate


def unit_back(normed, rate, grad, gain):
    scaled = grad * gain
    return rate * (
        scaled
        - jnp.mean(scaled, axis=-1, keepdims=True)
        - normed * jnp.mean(scaled * normed, axis=-1, keepdims=True)
    )


def lane_masks(head, lane):
    base = (head // 8) * 8
    return (lane // 64) == (head % 2), (lane // 16) == (head - base)


PLAN_DOWN = ((1024, (0, 1, 2, 3)), (512, (2, 0, 1, 3)))
PLAN_UP = ((1152, (1, 2, 0, 3)), (576, (2, 0, 1, 3)))
PLAN_HALF = ((640, (0, 1, 2, 3)), (640, (1, 2, 0, 3)), (384, (2, 0, 1, 3)))


def pieces(plan, start, count):
    at, base = start, 0
    for rows, order in plan:
        leaf = rows // 8
        while base <= at < min(base + rows, start + count):
            which, offset = divmod(at - base, leaf)
            n = min(leaf - offset, start + count - at)
            yield at, n, base, leaf, which, offset, order
            at += n
        base += rows


def mask_of(sides, order):
    return sides[order[0]] * 4 + sides[order[1]] * 2 + sides[order[2]]


def spot_of(sides, plan, start, count):
    for at, n, base, leaf, which, offset, order in pieces(plan, start, count):
        row = base + offset + leaf * jnp.bitwise_xor(mask_of(sides, order), which)
        yield at - start, n, pl.multiple_of(row, math.gcd(math.gcd(base + offset, leaf), 64))


def place(out, sides, plan, start, value, columns=slice(None)):
    for at, n, row in spot_of(sides, plan, start, value.shape[0]):
        out[pl.ds(row, n), columns] = value[at:at + n, :]


def place_half(out, sides, plan, start, value, columns=slice(None)):
    half = sum(rows for rows, _ in plan)
    at = start
    while at < start + value.shape[0]:
        which, inner = divmod(at, half)
        count = min(half - inner, start + value.shape[0] - at)
        for off, n, row in spot_of(sides, plan, inner, count):
            there = pl.multiple_of(jnp.bitwise_xor(sides[4], which) * half + row, 16)
            out[pl.ds(there, n), columns] = value[at - start + off:at - start + off + n, :]
        at += count


def fetch(pairs, sems):
    copies = [pltpu.make_async_copy(src, dst, sems.at[i]) for i, (src, dst) in enumerate(pairs)]
    for copy in copies:
        copy.start()
    return copies


def front_kernel(
    count_ref, sides, text_any, layout_any, joint_t_any, joint_l_any, mix_t_any, mix_l_any,
    qkv_t, qkv_l, mixed_t, mixed_l, normed_t, normed_l, stats,
    text_ref, layout_ref, joint_t, joint_l, mix_t, mix_l, mix_acc, flipped, sems,
):
    slots, width_t = text_ref.shape
    width_l = layout_ref.shape[1]
    columns = [slice(j * width_t, (j + 1) * width_t) for j in range(3)]
    copies = fetch(
        [
            (layout_any.at[0], flipped), (joint_l_any, joint_l), (text_any.at[0], text_ref),
            *((joint_t_any.at[:, c], joint_t.at[:, c]) for c in columns),
            (mix_t_any, mix_t), (mix_l_any, mix_l),
        ],
        sems,
    )
    count = count_ref[0]
    mix_acc[...] = jnp.zeros_like(mix_acc)
    stats[...] = jnp.zeros_like(stats)
    copies[0].wait()
    copies[1].wait()
    layout_ref[...] = flipped[...].T
    for j in range(3):
        qkv_l[:, j * 256:j * 256 + width_l] = nn(
            layout_ref[...], joint_l[:, j * width_l:(j + 1) * width_l]
        ).astype(BF16)
        qkv_l[:, j * 256 + width_l:(j + 1) * 256] = jnp.zeros((slots, 256 - width_l), BF16)
    copies[2].wait()
    for j, c in enumerate(columns):
        copies[3 + j].wait()
        qkv_t[:, c] = nn(text_ref[...], joint_t[:, c]).astype(BF16)
    lane = lax.broadcasted_iota(jnp.int32, (slots, 128), 1)
    dead = lax.broadcasted_iota(jnp.int32, (slots, slots), 1) >= count

    def pair_step(pair, carry):
        spot = lambda start: pl.ds(pl.multiple_of(start, 128), 128)
        at_l = (pair // 4) * 128
        query_t, key_t, value_t = (qkv_t[:, spot(j * width_t + pair * 128)] for j in range(3))
        query_l, key_l, value_l = (qkv_l[:, spot(j * 256 + at_l)] for j in range(3))
        keys = jnp.concatenate([key_t, key_l], axis=1)
        values = jnp.concatenate([value_t, value_l], axis=1)
        for side in range(2):
            head = 2 * pair + side
            mask_t, mask_l = lane_masks(head, lane)
            queries = jnp.concatenate(
                [
                    jnp.where(mask_t, query_t * 0.125, 0),
                    jnp.where(mask_l, query_l * 0.25, 0),
                ],
                axis=1,
            ).astype(BF16)
            logits = jnp.where(dead, NEG_FILL, nt(queries, keys))
            top = jnp.max(logits, axis=1, keepdims=True)
            raised = jnp.exp(logits - top)
            mass = jnp.sum(raised, axis=1, keepdims=True)
            stats[...] = jnp.where(lane == head, top + jnp.log(mass), stats[...])
            out = nn(raised.astype(BF16), values) * (1.0 / mass)
            if side == 0:
                first = out[:, :128]
            else:
                mixed_t[:, spot(pair * 128)] = jnp.where(mask_t, out[:, :128], first).astype(BF16)
            mix_acc[:, spot(at_l)] = mix_acc[:, spot(at_l)] + jnp.where(mask_l, out[:, 128:], 0.0)
        return carry

    lax.fori_loop(0, HEADS // 2, pair_step, 0)
    mixed_l[...] = mix_acc[:, :width_l].astype(BF16)
    copies[6].wait()
    normed, rate = unit(text_ref[...].astype(F32) + nn(mixed_t[...], mix_t[...]))
    normed_t[...] = normed
    stats[...] = jnp.where(lane == 16, rate, stats[...])
    copies[7].wait()
    normed, rate = unit(layout_ref[...].astype(F32) + nn(mixed_l[...], mix_l[...]))
    normed_l[...] = normed
    stats[...] = jnp.where(lane == 17, rate, stats[...])


def column(stats, lane, which):
    return jnp.sum(jnp.where(lane == which, stats[...], 0.0), axis=1, keepdims=True)


ANY_SPEC = pl.BlockSpec(memory_space=pltpu.HBM)


def call(kernel, micros, outs, args, scratch=(), specs=None, aliases=None, limit=16):
    moved = sum(math.prod(a.shape) * a.dtype.itemsize for a in args)
    return pl.pallas_call(
        kernel,
        out_shape=[(pltpu.VMEM(s, d) if kept else jax.ShapeDtypeStruct(s, d)) for s, d, kept in outs],
        in_specs=specs or [VMEM_SPEC] * len(args),
        out_specs=[VMEM_SPEC] * len(outs),
        scratch_shapes=list(scratch),
        input_output_aliases=aliases or {},
        compiler_params=pltpu.CompilerParams(vmem_limit_bytes=limit * 1024 * 1024),
        cost_estimate=pl.CostEstimate(flops=int(micros * 1.1e9), bytes_accessed=moved, transcendentals=0),
    )(*args)


def front(count, sides, text, layout, joint_t, joint_l, mix_t, mix_l):
    _, s, wt = text.shape
    wl = layout.shape[1]
    return call(
        front_kernel,
        12,
        [
            ((s, 3 * wt), BF16, True), ((s, 768), BF16, True), ((s, wt), BF16, True), ((s, wl), BF16, True),
            ((s, wt), F32, True), ((s, wl), F32, True), ((s, 128), F32, True),
        ],
        (count, sides, text, layout, joint_t, joint_l, mix_t, mix_l),
        [
            pltpu.VMEM((s, wt), BF16), pltpu.VMEM((s, wl), BF16), pltpu.VMEM((wt, 3 * wt), BF16),
            pltpu.VMEM((wl, 3 * wl), BF16), pltpu.VMEM((wt, wt), BF16), pltpu.VMEM((wl, wl), BF16),
            pltpu.VMEM((s, 256), F32), pltpu.VMEM((wl, s), BF16), pltpu.SemaphoreType.DMA((8,)),
        ],
        [SMEM_SPEC] * 2 + [ANY_SPEC] * 6,
        limit=56,
    )


def feed_kernel(
    sides, normed_t, normed_l, norms_t, norms_l, cot_t, cot_l,
    up_t0, up_t1, down_t0, down_t1, up_l0, up_l1, down_l0, down_l1,
    result_t, result_l, second_t, second_l, dfeed_t, dfeed_l, low_t, low_l,
    act_t0, act_t1, slope_t0, slope_t1, act_l0, act_l1, slope_l0, slope_l1,
    dnorm_t, dnorm_l, down_far,
):
    step = 512
    cuts = [slice(at, at + step) for at in range(0, up_t0.shape[1], step)]
    first_t = normed_t[...] * norms_t[0:1, :] + norms_t[1:2, :]
    low_t[...] = first_t.astype(BF16)
    first_l = normed_l[...] * norms_l[0:1, :] + norms_l[1:2, :]
    low_l[...] = first_l.astype(BF16)
    for up, act, slope in ((up_t0, act_t0, slope_t0), (up_t1, act_t1, slope_t1)):
        for cut in cuts:
            active, rise = gelu_pair(nn(low_t[...], up[:, cut]))
            act[:, cut] = active.astype(BF16)
            slope[:, cut] = rise.astype(BF16)
    for up, act, slope in ((up_l0, act_l0, slope_l0), (up_l1, act_l1, slope_l1)):
        active, rise = gelu_pair(nn(low_l[...], up[...]))
        act[...] = active.astype(BF16)
        slope[...] = rise.astype(BF16)
    summed_l = first_l + nt(act_l0[...], down_l0[...]) + nt(act_l1[...], down_l1[...])
    summed_t = normed_t[...] * norms_t[0:1, :] + norms_t[1:2, :] + (
        nn(act_t0[...], down_t0[...]) + nn(act_t1[...], down_t1[...])
    )
    for summed, norms, cot, result, second, dfeed, dnorm in (
        (summed_t, norms_t, cot_t, result_t, second_t, dfeed_t, dnorm_t),
        (summed_l, norms_l, cot_l, result_l, second_l, dfeed_l, dnorm_l),
    ):
        normed, rate = unit(summed)
        value = (normed * norms[2:3, :] + norms[3:4, :]).astype(BF16)
        result[...] = value if result is result_t else value.T
        grad = (cot[0] if cot is cot_t else cot[0].T).astype(F32)
        dnorm[0:1, :] = jnp.sum(grad * normed, axis=0, keepdims=True)
        dnorm[1:2, :] = jnp.sum(grad, axis=0, keepdims=True)
        back = unit_back(normed, rate, grad, norms[2:3, :])
        second[...] = back
        dfeed[...] = back.astype(BF16)
    down_kernel(sides, act_t1, dfeed_t, down_far)


def feed(sides, normed_t, normed_l, norms_t, norms_l, cot_t, cot_l, weights):
    s, wt = normed_t.shape
    wl = normed_l.shape[1]
    ht, hl = weights[0].shape[1], weights[4].shape[1]
    return call(
        feed_kernel,
        16,
        [((s, wt), BF16, False), ((wl, s), BF16, False)]
        + [((s, wt), F32, True), ((s, wl), F32, True)]
        + [((s, wt), BF16, True), ((s, wl), BF16, True)] * 2
        + [((s, ht), BF16, True)] * 4
        + [((s, hl), BF16, True)] * 4
        + [((2, wt), F32, True), ((2, wl), F32, True), ((ht, wt), BF16, False)],
        (sides, normed_t, normed_l, norms_t, norms_l, cot_t, cot_l) + tuple(weights),
        specs=[SMEM_SPEC] + [VMEM_SPEC] * 14,
        limit=16,
    )


def down_kernel(sides, act, dfeed, out):
    step = 512
    for start in range(0, act.shape[1], step):
        place(out, sides, PLAN_DOWN, start, tn(act[:, start:start + step], dfeed[...]).astype(BF16))


def up_body(
    sides, dfeed_t, dfeed_l, low_t, low_l, down_t, down_l, slope_t, slope_l, act_l, up_t, up_l, prev_t, prev_l,
    grads, dfirst_t, dfirst_l, dhid,
):
    wt = low_t.shape[1]
    wl = low_l.shape[1]
    for start in range(0, down_t.shape[0], wt):
        at = slice(start, start + wt)
        dhid[:, at] = (nt(dfeed_t[...], down_t[at, :]) * slope_t[:, at].astype(F32)).astype(BF16)
        place(grads, sides, PLAN_UP, start, tn(low_t[...], dhid[:, at]).astype(BF16))
    dfirst_t[...] = prev_t[...] + nt(dhid[...], up_t[...])
    base = down_t.shape[0]
    hl = down_l.shape[1]
    dhidden = (nn(dfeed_l[...], down_l[...]) * slope_l[...].astype(F32)).astype(BF16)
    lower = tn(act_l[...], dfeed_l[...]).astype(BF16)
    packed = jnp.concatenate([tn(low_l[...], dhidden).astype(BF16), lower[:wl, :], lower[wl:, :]], axis=1)
    place(grads, sides, PLAN_UP, base, packed)
    dfirst_l[...] = prev_l[...] + nt(dhidden, up_l[...])


def up_kernel(*refs):
    up_body(*refs)


def up_down_kernel(*refs):
    sides, act_t, refs = refs[0], refs[1], refs[2:]
    down_kernel(sides, act_t, refs[0], refs[13])
    up_body(sides, *refs[:13], *refs[14:])


def up_grad(sides, act_t, *args):
    dfeed_t, dfeed_l, low_t, low_l, down_t = args[:5]
    s, wt = low_t.shape
    wl = low_l.shape[1]
    ht = down_t.shape[0]
    outs = [((ht + wl, wt), BF16, False), ((s, wt), F32, True), ((s, wl), F32, True)]
    scratch = [pltpu.VMEM((s, ht), BF16)]
    if act_t is None:
        specs = [SMEM_SPEC] + [VMEM_SPEC] * len(args)
        return call(up_kernel, 5, outs, (sides,) + args, scratch, specs)
    specs = [SMEM_SPEC] + [VMEM_SPEC] * (len(args) + 1)
    return call(up_down_kernel, 8, [((ht, wt), BF16, False)] + outs, (sides, act_t) + args, scratch, specs)


def turn_kernel(
    sides, mixed_t, mixed_l, normed_t, normed_l, stats, dfirst_t, dfirst_l, norms_t, norms_l, dnorm_t, dnorm_l, mix_t, mix_l,
    grads, dtext, dlayout, dmix_t, dmix_l, mix_low,
):
    slots, wt = mixed_t.shape
    wl = mixed_l.shape[1]
    base = 4 * wt
    lane = lax.broadcasted_iota(jnp.int32, (slots, 128), 1)
    norm_row = base + wl
    kept = []
    for n, (first, normed, norms, dnorm, width, mixed, mix, dmix) in enumerate((
        (dfirst_t, normed_t, norms_t, dnorm_t, wt, mixed_t, mix_t, dmix_t),
        (dfirst_l, normed_l, norms_l, dnorm_l, wl, mixed_l, mix_l, dmix_l),
    )):
        grad = first[...]
        unitv = normed[...]
        gain_grad = jnp.sum(grad * unitv, axis=0, keepdims=True)
        shift_grad = jnp.sum(grad, axis=0, keepdims=True)
        rows = jnp.concatenate([gain_grad, shift_grad, dnorm[0:2, :]], axis=0)
        kept.append(jnp.concatenate(
            [rows.astype(BF16), jnp.zeros((12, width), BF16)], axis=0
        ) if width == wt else jnp.concatenate(
            [jnp.concatenate([rows.astype(BF16), jnp.zeros((4, wt - width), BF16)], axis=1), jnp.zeros((44, wt), BF16)],
            axis=0,
        ))
        resid = unit_back(unitv, column(stats, lane, 16 + n), grad, norms[0:1, :])
        low = resid.astype(BF16)
        if n == 0:
            dtext[...] = resid
            place_half(grads, sides, PLAN_HALF, 3 * wt, tn(mixed[...], low).astype(BF16))
            dmix[...] = nt(low, mix[...]).astype(BF16)
        else:
            dlayout[...] = resid
            mix_low[...] = tn(mixed[...], low).astype(BF16)
            dmix[:, :wl] = nt(low, mix[...]).astype(BF16)
            dmix[:, wl:] = jnp.zeros((slots, 256 - wl), BF16)
    place_half(grads, sides, PLAN_HALF, norm_row, jnp.concatenate(kept, axis=0))


def turn(*args):
    s, wt = args[1].shape
    wl = args[2].shape[1]
    rows = 4 * wt + wl + 64
    return call(
        turn_kernel,
        4,
        [
            ((rows, wt), BF16, True), ((s, wt), F32, True), ((s, wl), F32, True), ((s, wt), BF16, True),
            ((s, 256), BF16, True), ((wl, wl), BF16, True),
        ],
        args,
        specs=[SMEM_SPEC] + [VMEM_SPEC] * (len(args) - 1),
    )


def pairs_kernel(lo, hi, fresh, count_ref, qkv_t, qkv_l, stats, dmix_t, dmix_l, *refs):
    djoint_t, acc_l = refs[-2:]
    slots, wt = dmix_t.shape
    count = count_ref[0]
    if fresh:
        acc_l[...] = jnp.zeros_like(acc_l)
    lane = lax.broadcasted_iota(jnp.int32, (slots, 128), 1)
    dead = lax.broadcasted_iota(jnp.int32, (slots, slots), 1) >= count

    def pair_step(pair, carry):
        spot = lambda start: pl.ds(pl.multiple_of(start, 128), 128)
        at_l = (pair // 4) * 128
        query_t, key_t, value_t = (qkv_t[:, spot(j * wt + pair * 128)] for j in range(3))
        query_l, key_l, value_l = (qkv_l[:, spot(j * 256 + at_l)] for j in range(3))
        upper_t = dmix_t[:, spot(pair * 128)]
        upper_l = dmix_l[:, spot(at_l)]
        keys = jnp.concatenate([key_t, key_l], axis=1)
        values = jnp.concatenate([value_t, value_l], axis=1)
        kept = None
        for side in range(2):
            head = 2 * pair + side
            mask_t, mask_l = lane_masks(head, lane)
            queries = jnp.concatenate(
                [
                    jnp.where(mask_t, query_t * 0.125, 0),
                    jnp.where(mask_l, query_l * 0.25, 0),
                ],
                axis=1,
            ).astype(BF16)
            logits = jnp.where(dead, NEG_FILL, nt(queries, keys))
            probs = jnp.exp(logits - column(stats, lane, head))
            own_t = jnp.where(mask_t, upper_t, 0).astype(BF16)
            own_l = jnp.where(mask_l, upper_l, 0).astype(BF16)
            grad_t = nt(own_t, value_t)
            grad_s = nt(jnp.concatenate([own_t, own_l], axis=1), values)
            score_t = (probs * (grad_t - jnp.sum(grad_t * probs, axis=1, keepdims=True))).astype(BF16)
            score_l = (probs * (grad_s - jnp.sum(grad_s * probs, axis=1, keepdims=True))).astype(BF16)
            dvalue = tn(probs.astype(BF16), jnp.concatenate([upper_t, upper_l], axis=1))
            dquery_t = nn(score_t, key_t) * 0.125
            dkey_t = tn(score_t, query_t) * 0.125
            dquery_l = nn(score_l, key_l) * 0.25
            dkey_l = tn(score_l, query_l) * 0.25
            if side == 0:
                kept = (dquery_t, dkey_t, dvalue[:, :128])
            else:
                for j, (old, new) in enumerate(zip(kept, (dquery_t, dkey_t, dvalue[:, :128]))):
                    djoint_t[:, spot(j * wt + pair * 128)] = jnp.where(mask_t, new, old).astype(BF16)
            for j, part in enumerate((dquery_l, dkey_l, dvalue[:, 128:])):
                at = spot(j * 256 + at_l)
                acc_l[:, at] = acc_l[:, at] + jnp.where(mask_l, part, 0.0)
        return carry

    lax.fori_loop(lo, hi, pair_step, 0)


def pairs(lo, hi, prev, *args):
    s, wt = args[4].shape
    outs = [((s, 3 * wt), BF16, True), ((s, 768), F32, True)]
    n = len(args)
    return call(
        functools.partial(pairs_kernel, lo, hi, prev is None),
        3 * (hi - lo),
        outs,
        args + tuple(prev or ()),
        specs=[SMEM_SPEC] + [VMEM_SPEC] * (n - 1 + (2 if prev else 0)),
        aliases={n: 0, n + 1: 1} if prev else None,
    )


def close_kernel(
    sides, text_ref, layout_ref, djoint_t, acc_l, joint_t, joint_l, mix_low, part_ref, dtext_in, dlayout_in,
    grads, dtext, dlayout, djoint_l,
):
    wt = text_ref.shape[2]
    wl = layout_ref.shape[1]
    base = 4 * wt

    for j in range(3):
        place_half(
            grads, sides, PLAN_HALF, j * wt, tn(text_ref[0], djoint_t[:, j * wt:(j + 1) * wt]).astype(BF16)
        )
    for j in range(3):
        djoint_l[:, j * wl:(j + 1) * wl] = acc_l[:, j * 256:j * 256 + wl].astype(BF16)
    low = jnp.concatenate([nn(layout_ref[0], djoint_l[...]).astype(BF16), mix_low[...]], axis=1)
    place_half(grads, sides, PLAN_HALF, base, low)
    dtext[...] = dtext_in[...] + nt(djoint_t[...], joint_t[...])
    dlayout[...] = (dlayout_in[...] + nt(djoint_l[...], joint_l[...])).T


def close(*args):
    text, layout = args[1:3]
    _, s, wt = text.shape
    wl = layout.shape[1]
    return call(
        close_kernel,
        5,
        [(args[8].shape, BF16, True), ((s, wt), F32, False), ((wl, s), F32, False)],
        args,
        [pltpu.VMEM((s, 3 * wl), BF16)],
        specs=[SMEM_SPEC] + [VMEM_SPEC] * (len(args) - 1),
        aliases={8: 0},
    )


AXES = ("dp", "tensor")


def swap(value, bit, many):
    dp, tensor = many
    pairs = []
    for d in range(dp):
        for t in range(tensor):
            to = (d, t ^ 1) if bit < 0 else (d ^ (1 << bit), t)
            pairs.append((d * tensor + t, to[0] * tensor + to[1]))
    return lax.ppermute(value, AXES, pairs)


def cut_of(value, base, rows):
    return lax.slice_in_dim(value, base, base + rows, axis=0)


def tie(values, *others):
    got = lax.optimization_barrier((tuple(values), tuple(others)))
    return got[0]


class Stream:
    def __init__(self, plan, own, got, many):
        self.plan, self.many = plan, many
        self.keep, self.send, base = [], [], 0
        for rows, _ in plan:
            half = rows // 2
            self.keep.append(cut_of(own, base, half) + cut_of(got, base, half))
            self.send.append(cut_of(own, base + half, half) + cut_of(got, base + half, half))
            base += rows

    def reduce(self, step):
        got = [swap(v, order[step], self.many) for v, (_, order) in zip(self.send, self.plan)]
        keep, send = [], []
        for k, g in zip(self.keep, got):
            if step < 2:
                half = k.shape[0] // 2
                keep.append(cut_of(k, 0, half) + cut_of(g, 0, half))
                send.append(cut_of(k, half, half) + cut_of(g, half, half))
            else:
                keep.append(k + g)
        self.keep, self.send = keep, send

    def cross(self):
        whole = jnp.concatenate(self.keep, axis=0)
        whole = whole + swap(whole, self.plan[0][1][3], self.many)
        base, keep = 0, []
        for k in self.keep:
            keep.append(cut_of(whole, base, k.shape[0]))
            base += k.shape[0]
        self.keep = keep

    def spread(self, step):
        got = [swap(v, order[step], self.many) for v, (_, order) in zip(self.keep, self.plan)]
        if step:
            self.keep = [jnp.concatenate([k, g], axis=0) for k, g in zip(self.keep, got)]
        else:
            self.keep = [(k, g) for k, g in zip(self.keep, got)]

    def flat(self):
        return [part for pair in self.keep for part in pair]


def read_rows(parts, sides, plan, start, count):
    bases = {}
    base = 0
    for i, (rows, _) in enumerate(plan):
        bases[base] = i
        base += rows
    for at, n, base, leaf, which, offset, order in pieces(plan, start, count):
        pair = parts[2 * bases[base]], parts[2 * bases[base] + 1]
        rel = jnp.bitwise_xor(mask_of(sides, order), which)
        row = pl.multiple_of(jnp.bitwise_and(rel, 3) * leaf + offset, math.gcd(math.gcd(leaf, offset), 64))
        yield at - start, n, pair, rel < 4, row


def move(parts, sides, plan, start, count, write):
    for at, n, pair, low, row in read_rows(parts, sides, plan, start, count):
        for ref, here in zip(pair, (low, jnp.logical_not(low))):

            @pl.when(here)
            def _(ref=ref, at=at, n=n, row=row):
                write(at, n, ref[pl.ds(row, n), :].astype(F32))


def put(out, column, width):
    def write(at, n, value):
        out[at:at + n, column:column + width] = value[:, :width]

    return write


def open_down_kernel(sides, *refs):
    parts, out = refs[:-1], refs[-1]
    move(parts, sides, PLAN_DOWN, 0, out.shape[0], put(out, 0, out.shape[1]))


def open_up_kernel(sides, *refs):
    parts, (up_t, up_l, down_l) = refs[:-3], refs[-3:]
    wt, hidden = up_t.shape
    wl, hl = up_l.shape
    for column in range(0, hidden, wt):
        move(parts, sides, PLAN_UP, column, wt, put(up_t, column, wt))

    def low(at, n, value):
        up_l[at:at + n, :] = value[:, :hl]
        down_l[at:at + n, :] = value[:, hl:hl + wl]
        down_l[wl + at:wl + at + n, :] = value[:, hl + wl:]

    move(parts, sides, PLAN_UP, hidden, wl, low)


def open_half_kernel(sides, *refs):
    count = 2 * len(PLAN_HALF)
    own, other, (joint_t, mix_t, norm_t, joint_l, mix_l, norm_l) = refs[:count], refs[count:2 * count], refs[2 * count:]
    wt, wl = mix_t.shape[0], mix_l.shape[0]
    half = sum(rows for rows, _ in PLAN_HALF)

    def low(at, n, value):
        joint_l[at:at + n, :] = value[:, :3 * wl]
        mix_l[at:at + n, :] = value[:, 3 * wl:]

    def norm(out, width):
        def write(at, n, value):
            out[...] = value[:4, :width]

        return write

    fields = [(j * wt, wt, put(joint_t, j * wt, wt)) for j in range(3)]
    fields += [(3 * wt, wt, put(mix_t, 0, wt)), (4 * wt, wl, low)]
    fields += [(4 * wt + wl, 16, norm(norm_t, wt)), (4 * wt + wl + 16, 16, norm(norm_l, wl))]
    for core in range(2):

        @pl.when(sides[4] == core)
        def _():
            for which in range(2):
                parts = own if which == core else other
                for start, rows, write in fields:
                    lo, hi = max(start, which * half), min(start + rows, (which + 1) * half)
                    if lo < hi:
                        move(
                            parts, sides, PLAN_HALF, lo - which * half, hi - lo,
                            lambda at, n, value, shift=lo - start, write=write: write(at + shift, n, value),
                        )


def open_up(kernel, micros, outs, sides, parts):
    return call(
        kernel, micros, [(shape, F32, False) for shape in outs], (sides,) + tuple(parts),
        specs=[SMEM_SPEC] + [VMEM_SPEC] * len(parts),
    )


def shards(
    many, text_input, layout_input, page_counts, text_joint, text_mixing, text_norms, text_upward, text_downward,
    layout_joint, layout_mixing, layout_norms, layout_upward, layout_downward, text_cotangent, layout_cotangent,
):
    dp, tensor = many
    wt, wl = text_input.shape[2], layout_input.shape[2]
    layout_flip = layout_input.swapaxes(1, 2)
    halves = tensor == 2 and dp == 16
    own = (text_upward, text_downward, layout_upward, layout_downward.T)
    if halves:
        far = tuple(swap(w, -1, many) for w in own)
    else:
        whole = [
            lax.all_gather(w, "tensor", axis=axis, tiled=True) for w, axis in zip(own, (1, 0, 1, 1))
        ]
        cut = lambda w, axis, i: lax.slice_in_dim(w, i * (w.shape[axis] // 2), (i + 1) * (w.shape[axis] // 2), axis=axis)
        own = tuple(cut(w, axis, 0) for w, axis in zip(whole, (1, 0, 1, 1)))
        far = tuple(cut(w, axis, 1) for w, axis in zip(whole, (1, 0, 1, 1)))
    place_bits = lax.axis_index("dp").astype(jnp.int32)
    sides = jnp.stack([(place_bits >> b) & 1 for b in range(4)] + [lax.axis_index("tensor").astype(jnp.int32) & 1])
    if not halves:
        sides = jnp.zeros_like(sides)
    (
        qkv_t, qkv_l, mixed_t, mixed_l, normed_t, normed_l, stats,
    ) = front(page_counts, sides, text_input, layout_flip, text_joint, layout_joint, text_mixing, layout_mixing)
    up_t0, down_t0, up_l0, down_l0 = own
    up_t1, down_t1, up_l1, down_l1 = far
    (
        result_t, result_l, second_t, second_l, dfeed_t, dfeed_l, low_t, low_l,
        act_t0, act_t1, slope_t0, slope_t1, act_l0, act_l1, slope_l0, slope_l1, dnorm_t, dnorm_l, down_far,
    ) = feed(
        sides, normed_t, normed_l, text_norms, layout_norms, text_cotangent, layout_cotangent.swapaxes(1, 2),
        (own[0], far[0], own[1], far[1], own[2], far[2], own[3], far[3]),
    )
    down_got = swap(down_far, -1, many) if halves else None
    down_own, up_far, dfirst_t, dfirst_l = up_grad(
        sides, act_t0,
        dfeed_t, dfeed_l, low_t, low_l, down_t1, down_l1, slope_t1, slope_l1, act_l1, up_t1, up_l1, second_t, second_l
    )
    if halves:
        up_got = swap(up_far, -1, many)
        down = Stream(PLAN_DOWN, down_own, down_got, many)
        dfirst_t, = tie([dfirst_t], *down.send)
    up_own, dfirst_t, dfirst_l = up_grad(
        sides, None,
        dfeed_t, dfeed_l, low_t, low_l, down_t0, down_l0, slope_t0, slope_l0, act_l0, up_t0, up_l0, dfirst_t, dfirst_l
    )
    if halves:
        up = Stream(PLAN_UP, up_own, up_got, many)
        dfirst_t, = tie([dfirst_t], *up.send)
    grads, dtext, dlayout, dmix_t, dmix_l, mix_low = turn(
        sides, mixed_t, mixed_l, normed_t, normed_l, stats, dfirst_t, dfirst_l, text_norms, layout_norms, dnorm_t, dnorm_l,
        text_mixing, layout_mixing,
    )
    state = None
    for lo in range(0, HEADS // 2, 2):
        if halves and lo == 2:
            down.reduce(0)
            dmix_t, = tie([dmix_t], *down.send)
        if halves and lo == 4:
            up.reduce(0)
            down.reduce(1)
            dmix_t, = tie([dmix_t], *up.send, *down.send)
        state = pairs(lo, lo + 2, state, page_counts, qkv_t, qkv_l, stats, dmix_t, dmix_l)
    if halves:
        up.reduce(1)
        down.reduce(2)
        state = tie(state, *up.send, *down.keep)
    grads, dtext, dlayout = close(
        sides, text_input, layout_flip, state[0], state[1], text_joint, layout_joint, mix_low, grads, dtext, dlayout
    )

    def unpack_up(packed, hidden, hl):
        text_part = jnp.concatenate([packed[i * wt:(i + 1) * wt] for i in range(hidden // wt)], axis=1)
        low_part = packed[hidden:]
        return text_part, low_part[:, :hl], jnp.concatenate([low_part[:, hl:hl + wl], low_part[:, hl + wl:]], axis=0)

    if halves:
        rows = grads.shape[0] // 2
        half = Stream(PLAN_HALF, cut_of(grads, 0, rows), swap(cut_of(grads, rows, rows), -1, many), many)
        down.cross()
        up.reduce(2)
        up.cross()
        for step in range(3):
            half.reduce(step)
        half.cross()
        for stream in (down, up, half):
            for step in (2, 1, 0):
                stream.spread(step)
        own_parts = half.flat()
        far_parts = [swap(part, -1, many) for part in own_parts]
        ht, hl = text_upward.shape[1], layout_upward.shape[1]
        down_grad_t, = open_up(open_down_kernel, 3, [(ht, wt)], sides, down.flat())
        up_grad_t, up_grad_l, down_grad_l = open_up(
            open_up_kernel, 3, [(wt, ht), (wl, hl), (hl, wl)], sides, up.flat()
        )
        joint_t, mix_t, norm_t, joint_l, mix_l, norm_l = open_up(
            open_half_kernel, 5, [(wt, 3 * wt), (wt, wt), (4, wt), (wl, 3 * wl), (wl, wl), (4, wl)],
            sides, own_parts + far_parts,
        )
    else:
        hidden = down_own.shape[0]
        parts = [unpack_up(up, hidden, up_l0.shape[1]) for up in (up_own, up_far)]
        joined = [
            jnp.concatenate([parts[0][0], parts[1][0]], axis=1),
            jnp.concatenate([down_own, down_far], axis=0),
            jnp.concatenate([parts[0][1], parts[1][1]], axis=1),
            jnp.concatenate([parts[0][2], parts[1][2]], axis=0),
        ]
        up_grad_t, down_grad_t, up_grad_l, down_grad_l = (
            lax.psum(lax.psum_scatter(g, "tensor", scatter_dimension=axis, tiled=True), "dp")
            for g, axis in zip(joined, (1, 0, 1, 0))
        )
        grads = lax.psum(grads, AXES).astype(F32)
        low = grads[4 * wt:4 * wt + wl]
        rows = 4 * wt + wl
        joint_t, mix_t = jnp.concatenate([grads[j * wt:(j + 1) * wt] for j in range(3)], axis=1), grads[3 * wt:4 * wt]
        norm_t, norm_l = grads[rows:rows + 4], grads[rows + 16:rows + 20, :wl]
        joint_l, mix_l = low[:, :3 * wl], low[:, 3 * wl:]
    return (
        result_t[None],
        result_l.T[None],
        dtext[None],
        dlayout.T[None],
        joint_t,
        mix_t,
        norm_t,
        up_grad_t.astype(F32),
        down_grad_t.astype(F32),
        joint_l,
        mix_l,
        norm_l,
        up_grad_l.astype(F32),
        down_grad_l.astype(F32),
    )


def solution(mesh):
    many = (mesh.shape["dp"], mesh.shape["tensor"])
    pages = P(("dp", "tensor"), None, None)
    columns, rows = P(None, "tensor"), P("tensor", None)
    return jax.shard_map(
        functools.partial(shards, many),
        mesh=mesh,
        in_specs=(
            pages, pages, P(("dp", "tensor")), P(), P(), P(), columns, rows, P(), P(), P(), columns, rows, pages, pages,
        ),
        out_specs=(
            pages, pages, pages, pages, P(), P(), P(), columns, rows, P(), P(), P(), columns, rows,
        ),
        check_vma=False,
    )
```

time: 616 us -> 282 us (0.46)
  matrix products: 188 us -> 0 us
  waiting for transfers between devices: 246 us -> 123 us
  Pallas kernels: 0 us -> 83.2 us
  other arithmetic: 58.9 us -> 2.31 us
  blocking collectives: 45.9 us -> 0 us
  starting transfers between devices: 12.9 us -> 56.6 us
  local copies, waits for them, and re-layouts: 37.9 us -> 10.2 us
  between operations: 16.1 us -> 2.25 us
    psum x2 -> x0, waiting for transfers between devices: 236 us -> none  [the longest x1 150 us: shards(): lax.psum((text_joint_grad, text_mix_grad, text_norm_grad, layout_joint_gr...]
    dot_general x36 -> x0, matrix products: 188 us -> none  [the longest x24 86.4 us: matmul(): return jnp.dot(left, right, preferred_element_type=jnp.float32)]
    ppermute x0 -> x58, waiting for transfers between devices: none -> 123 us  [swap(): return lax.ppermute(value, AXES, pairs)]
    pallas_call x0 -> x12, Pallas kernels: none -> 83.2 us  [call(): pl.pallas_call(kernel, out_shape=[pltpu.VMEM(s, d) if kept else jax.Shape...]
    ppermute x0 -> x58, starting transfers between devices: none -> 56.6 us  [swap(): return lax.ppermute(value, AXES, pairs)]
    psum x1 -> x0, blocking collectives: 41.7 us -> none  [shards(): lax.psum((text_joint_grad, text_mix_grad, text_norm_grad, layout_joint_gr...]
    convert_element_type x12 -> x0, other arithmetic: 33.1 us -> none  [the longest x1 10 us: page_backward(): text_sgrad = text_lgrad.astype(jnp.bfloat16)]
    reduce_sum x16 -> x0, other arithmetic: 23.7 us -> none  [the longest x7 14 us: normalize(): return center * lax.rsqrt(spread + 1e-05) * gain + shift]
  transfers between devices with their start and end apart: 8 -> 58, of which waited for: 3 -> 20; matrix products, arithmetic and copies ran while one was open for 34% -> 1% of each run, Pallas kernels for 0% -> 20%
where the time goes in v1:
time: 282 us; the launch traced here: 278 us
  waiting for transfers between devices  123 us (44%)
  Pallas kernels  83.2 us (30%)
  starting transfers between devices  56.6 us (20%)
  local copies, waits for them, and re-layouts  10.2 us (4%)
    ppermute x58, waiting for transfers between devices, swap(): return lax.ppermute(value, AXES, pairs)  123 us
    pallas_call x12, Pallas kernels, call(): pl.pallas_call(kernel, out_shape=[pltpu.VMEM(s, d) if kept else jax.Shape...  83.2 us
    ppermute x58, starting transfers between devices, swap(): return lax.ppermute(value, AXES, pairs)  56.6 us
    unnamed x57, local copies, waits for them, and re-layouts  9.36 us
  transfers between devices with their start and end apart: 58, of which 20 were waited for; matrix products, arithmetic and copies ran while one was open for 1% of the time, Pallas kernels for 20%

profile of v1, /device:TPU:0, one launch (start us, length us, event | category | flops | bytes accessed | tf_op | source)
XLA Modules:
  0.0 277.8 jit_solution(2773536187085326461)
XLA Ops:
  3.1 14.4 %shard_map.254 = (bf16[512,2304]{1,0:T(8,128)(2,1)S(1)}, bf16[512,768]{1,0:T(8,128)(2,1)S(1)}, bf16[512,768]{1,0:T(8,128)(2,1)S(1)}, bf16[512,192]{1,0:T(8,128)(...) custom-call(s32[1]{0:T(128)S(6)} %copy.40.count_ref, s32[5]{0:T(128)} %stack.23.sides.refs_0_, ...), custom_call_target="tpu_custom_call" | custom-call | flops 13200000000 | bytes 5996568 | tf_op jit(solution)/shard_map/pallas_call | solution.py:196
  25.0 14.1 %shard_map.255 = (bf16[512,768]{1,0:T(8,128)(2,1)}, bf16[192,512]{1,0:T(8,128)(2,1)}, f32[512,768]{1,0:T(8,128)S(1)}, f32[512,192]{1,0:T(8,128)S(1)}, bf16[512,7...) custom-call(s32[5]{0:T(128)S(1)} %copy-done, ...), custom_call_target="tpu_custom_call" | custom-call | flops 17600000000 | bytes 12991508 | tf_op jit(solution)/shard_map/pallas_call | solution.py:196
  39.5 8.5 %shard_map.256 = (bf16[1536,768]{1,0:T(8,128)(2,1)S(1)}, bf16[1728,768]{1,0:T(8,128)(2,1)S(1)}, f32[512,768]{1,0:T(8,128)S(1)}, f32[512,192]{1,0:T(8,128)S(1)}) custom-call(s32[5]{0:T(128)S(1)} %copy-done, bf16[512,1536]{1,0:T(8,128)(2,1)S(1)} %get-tuple-element.92.refs_1_, bf16[512,768]{1,0:T(8,128)(2,1)S(1)} %get-tuple-element.85.refs_2_.refs_1_, ...), custom_call_target="tpu_custom_call" | custom-call | flops 8800000000 | bytes 12877844 | tf_op jit(solution)/shard_map/pallas_call | solution.py:196
  53.1 5.1 %shard_map.257 = (bf16[1728,768]{1,0:T(8,128)(2,1)S(1)}, f32[512,768]{1,0:T(8,128)S(1)}, f32[512,192]{1,0:T(8,128)S(1)}) custom-call(s32[5]{0:T(128)S(1)} %copy-done, bf16[512,768]{1,0:T(8,128)(2,1)S(1)} %get-tuple-element.85.refs_2_.refs_1_, bf16[512,192]{1,0:T(8,128)(2,1)S(1)} %get-tuple-element.86.refs_3_.refs_2_, ...), custom_call_target="tpu_custom_call" | custom-call | flops 5500000256 | bytes 11304980 | tf_op jit(solution)/shard_map/pallas_call | solution.py:196
  65.9 9.2 %collective-permute-done.11 = bf16[128,768]{1,0:T(8,128)(2,1)S(1)} collective-permute-done((bf16[128,768]{1,0:T(8,128)(2,1)S(1)}, bf16[128,768]{1,0:T(8,128)(2,1)S(1)}, u32[]{:S(2)}, u32[]{:S(2)}) %collective-permute-start.11) | collective-permute-done | bytes 196640 | tf_op jit(solution)/shard_map/ppermute | solution.py:509
  76.7 6.3 %shard_map.259 = (bf16[512,2304]{1,0:T(8,128)(2,1)S(1)}, f32[512,768]{1,0:T(8,128)S(1)}) custom-call(s32[1]{0:T(128)S(6)} %copy.40.count_ref, bf16[512,2304]{1,0:T(8,128)(2,1)S(1)} %get-tuple-element.80.qkv_t, bf16[512,768]{1,0:T(8,128)(2,1)S(1)} %copy-done.23, f32[512,128]{1,0:T(8,128)S(1)} %copy-done.25, bf16[512,768]{1,0:T(8,128)(2,1)S(1)} %get-tuple-element.112.dmix_t, ...), custom_call_target="tpu_custom_call" | custom-call | flops 6600000000 | bytes 4456452 | tf_op jit(solution)/shard_map/pallas_call | solution.py:196
  86.1 5.8 %shard_map.260 = (bf16[512,2304]{1,0:T(8,128)(2,1)S(1)}, f32[512,768]{1,0:T(8,128)S(1)}) custom-call(s32[1]{0:T(128)S(6)} %copy.40.count_ref, bf16[512,2304]{1,0:T(8,128)(2,1)S(1)} %get-tuple-element.80.qkv_t, bf16[512,768]{1,0:T(8,128)(2,1)S(1)} %copy-done.23, f32[512,128]{1,0:T(8,128)S(1)} %copy-done.25, ...), custom_call_target="tpu_custom_call", output_to_operand_aliasing={{0}: (6, {}), {1}: (7, {})} | custom-call | flops 6600000000 | bytes 8388612 | tf_op jit(solution)/shard_map/pallas_call | solution.py:196
  94.8 6.0 %shard_map.261 = (bf16[512,2304]{1,0:T(8,128)(2,1)S(1)}, f32[512,768]{1,0:T(8,128)S(1)}) custom-call(s32[1]{0:T(128)S(6)} %copy.40.count_ref, bf16[512,2304]{1,0:T(8,128)(2,1)S(1)} %get-tuple-element.80.qkv_t, bf16[512,768]{1,0:T(8,128)(2,1)S(1)} %copy-done.23, f32[512,128]{1,0:T(8,128)S(1)} %copy-done.25, ...), custom_call_target="tpu_custom_call", output_to_operand_aliasing={{0}: (6, {}), {1}: (7, {})} | custom-call | flops 6600000000 | bytes 8388612 | tf_op jit(solution)/shard_map/pallas_call | solution.py:196
  100.8 6.0 %collective-permute-done.14 = bf16[128,768]{1,0:T(8,128)(2,1)S(1)} collective-permute-done((bf16[128,768]{1,0:T(8,128)(2,1)S(1)}, bf16[128,768]{1,0:T(8,128)(2,1)S(1)}, u32[]{:S(2)}, u32[]{:S(2)}) %collective-permute-start.14) | collective-permute-done | bytes 196640 | tf_op jit(solution)/shard_map/ppermute | solution.py:509
  106.9 6.2 %shard_map.262 = (bf16[3328,768]{1,0:T(8,128)(2,1)S(1)}, f32[512,768]{1,0:T(8,128)}, f32[192,512]{1,0:T(8,128)}) custom-call(s32[5]{0:T(128)S(1)} %copy-done, bf16[1,512,768]{2,1,0:T(8,128)(2,1)S(1)} %copy-done.8, bf16[1,192,512]{2,1,0:T(8,128)(2,1)S(1)} %bitcast.18, ...), custom_call_target="tpu_custom_call", output_to_operand_aliasing={{0}: (8, {})} | custom-call | flops 5500000256 | bytes 15826964 | tf_op jit(solution)/shard_map/pallas_call | solution.py:196
  117.1 12.8 %collective-permute-done.51 = bf16[192,768]{1,0:T(8,128)(2,1)S(1)} collective-permute-done((bf16[192,768]{1,0:T(8,128)(2,1)S(1)}, bf16[192,768]{1,0:T(8,128)(2,1)S(1)}, u32[]{:S(2)}, u32[]{:S(2)}) %collective-permute-start.51) | collective-permute-done | bytes 294944 | tf_op jit(solution)/shard_map/ppermute | solution.py:509
  130.7 4.1 %collective-permute-done.55 = bf16[64,768]{1,0:T(8,128)(2,1)S(1)} collective-permute-done((bf16[64,768]{1,0:T(8,128)(2,1)S(1)}, bf16[64,768]{1,0:T(8,128)(2,1)S(1)}, u32[]{:S(2)}, u32[]{:S(2)}) %collective-permute-start.55) | collective-permute-done | bytes 98336 | tf_op jit(solution)/shard_map/ppermute | solution.py:509
  139.5 9.1 %collective-permute-done.23 = bf16[192,768]{1,0:T(8,128)(2,1)S(1)} collective-permute-done((bf16[192,768]{1,0:T(8,128)(2,1)S(1)}, bf16[192,768]{1,0:T(8,128)(2,1)S(1)}, u32[]{:S(2)}, u32[]{:S(2)}) %collective-permute-start.23) | collective-permute-done | bytes 294944 | tf_op jit(solution)/shard_map/ppermute | solution.py:509
  153.0 10.5 %collective-permute-done.24 = bf16[96,768]{1,0:T(8,128)(2,1)S(1)} collective-permute-done((bf16[96,768]{1,0:T(8,128)(2,1)S(1)}, bf16[96,768]{1,0:T(8,128)(2,1)S(1)}, u32[]{:S(2)}, u32[]{:S(2)}) %collective-permute-start.24) | collective-permute-done | bytes 147488 | tf_op jit(solution)/shard_map/ppermute | solution.py:509
  175.4 3.1 %collective-permute-start.19 = (bf16[80,768]{1,0:T(8,128)(2,1)S(1)}, bf16[80,768]{1,0:T(8,128)(2,1)S(1)}, u32[]{:S(2)}, u32[]{:S(2)}) collective-permute-start(bf16[80,768]{1,0:T(8,128)(2,1)S(1)} %slice_add_fusion.34), channel_id=1, source_target_pairs={{0,8},{1,9},{2,10},{3,11},{4,12},{5,13},{6,14},{7,15},{8,0},{9,1},... | collective-permute-start | bytes 368648 | tf_op jit(solution)/shard_map/ppermute | solution.py:509
  178.5 6.2 %collective-permute-done.19 = bf16[80,768]{1,0:T(8,128)(2,1)S(1)} collective-permute-done((bf16[80,768]{1,0:T(8,128)(2,1)S(1)}, bf16[80,768]{1,0:T(8,128)(2,1)S(1)}, u32[]{:S(2)}, u32[]{:S(2)}) %collective-permute-start.19) | collective-permute-done | bytes 122912 | tf_op jit(solution)/shard_map/ppermute | solution.py:509
  189.3 6.7 %collective-permute-done.26 = bf16[208,768]{1,0:T(8,128)(2,1)S(1)} collective-permute-done((bf16[208,768]{1,0:T(8,128)(2,1)S(1)}, bf16[208,768]{1,0:T(8,128)(2,1)S(1)}, u32[]{:S(2)}, u32[]{:S(2)}) %collective-permute-start.26) | collective-permute-done | bytes 319520 | tf_op jit(solution)/shard_map/ppermute | solution.py:509
  201.4 9.7 %collective-permute-done.27 = bf16[80,768]{1,0:T(8,128)(2,1)S(1)} collective-permute-done((bf16[80,768]{1,0:T(8,128)(2,1)S(1)}, bf16[80,768]{1,0:T(8,128)(2,1)S(1)}, u32[]{:S(2)}, u32[]{:S(2)}) %collective-permute-start.27) | collective-permute-done | bytes 122912 | tf_op jit(solution)/shard_map/ppermute | solution.py:509
  214.9 17.3 %collective-permute-done.33 = bf16[48,768]{1,0:T(8,128)(2,1)S(1)} collective-permute-done((bf16[48,768]{1,0:T(8,128)(2,1)S(1)}, bf16[48,768]{1,0:T(8,128)(2,1)S(1)}, u32[]{:S(2)}, u32[]{:S(2)}) %collective-permute-start.33) | collective-permute-done | bytes 73760 | tf_op jit(solution)/shard_map/ppermute | solution.py:509
  236.3 16.1 %collective-permute-done.34 = bf16[96,768]{1,0:T(8,128)(2,1)S(1)} collective-permute-done((bf16[96,768]{1,0:T(8,128)(2,1)S(1)}, bf16[96,768]{1,0:T(8,128)(2,1)S(1)}, u32[]{:S(2)}, u32[]{:S(2)}) %collective-permute-start.34) | collective-permute-done | bytes 147488 | tf_op jit(solution)/shard_map/ppermute | solution.py:509
  257.6 3.6 %collective-permute-done.32.refs_3_ = bf16[320,768]{1,0:T(8,128)(2,1)S(1)} collective-permute-done((bf16[320,768]{1,0:T(8,128)(2,1)S(1)}, bf16[320,768]{1,0:T(8,128)(2,1)S(1)}, u32[]{:S(2)}, u32[]{:S(2)}) %collective-permute-start.32) | collective-permute-done | bytes 491552 | tf_op jit(solution)/shard_map/ppermute | solution.py:509
  261.2 3.3 %shard_map.265 = f32[1536,768]{1,0:T(8,128)} custom-call(s32[5]{0:T(128)S(1)} %copy-done, bf16[512,768]{1,0:T(8,128)(2,1)S(1)} %pad_maximum_fusion.1.refs_0_, bf16[512,768]{1,0:T(8,128)(2,1)S(1)} %collective-permute-done.54.refs_1_, bf16[256,768]{1,0:T(8,128)(2,1)S(1)} %pad_maximum_fusion.7.refs_2_, bf16[256,768]{1,0:T(8,128)(2,1)S(1)} %collective-permute-done.57.refs_3_), custom_call_target="tpu_custom_call" | custom-call | flops 3300000000 | bytes 2359316 | tf_op jit(solution)/shard_map/pallas_call | solution.py:196
  265.0 3.6 %shard_map.264 = (f32[768,1536]{1,0:T(8,128)}, f32[192,384]{1,0:T(8,128)}, f32[384,192]{1,0:T(8,128)S(1)}) custom-call(s32[5]{0:T(128)S(1)} %copy-done, bf16[576,768]{1,0:T(8,128)(2,1)S(1)} %pad_maximum_fusion.refs_0_, bf16[576,768]{1,0:T(8,128)(2,1)S(1)} %collective-permute-done.47.refs_1_, bf16[288,768]{1,0:T(8,128)(2,1)S(1)} %pad_maximum_fusion.5.refs_2_, ...), custom_call_target="tpu_custom_call" | custom-call | flops 3300000000 | bytes 2654228 | tf_op jit(solution)/shard_map/pallas_call | solution.py:196
  270.5 7.2 %shard_map.263 = (f32[768,2304]{1,0:T(8,128)}, f32[768,768]{1,0:T(8,128)}, f32[4,768]{1,0:T(4,128)}, f32[192,576]{1,0:T(8,128)}, f32[192,192]{1,0:T(8,128)}, /*index=5*/f32[4,192]{1,0:T(4,128)}) custom-call(s32[5]{0:T(128)S(1)} %copy-done, bf16[320,768]{1,0:T(8,128)(2,1)S(1)} %pad_maximum_fusion.2.refs_0_, ...), custom_call_target="tpu_custom_call" | custom-call | flops 5500000256 | bytes 5111828 | tf_op jit(solution)/shard_map/pallas_call | solution.py:196
  (216 shorter events, 80.7 us)
Async XLA Ops:
  0.6 19.9 %collective-permute-start = (bf16[768,1536]{1,0:T(8,128)(2,1)}, bf16[768,1536]{1,0:T(8,128)(2,1)}, u32[]{:S(2)}, u32[]{:S(2)}) collective-permute-start(bf16[768,1536]{1,0:T(8,128)(2,1)} %refs_10_.1), channel_id=1, source_target_pairs={{0,1},{1,0},{2,3},{3,2},{4,5},{5,4},{6,7},{7,6},{8,9},{9,8},{10,11... | collective-permute-start | bytes 7077896 | tf_op jit(solution)/shard_map/ppermute | solution.py:509
  1.2 19.4 %collective-permute-start.1 = (bf16[1536,768]{1,0:T(8,128)(2,1)}, bf16[1536,768]{1,0:T(8,128)(2,1)}, u32[]{:S(2)}, u32[]{:S(2)}) collective-permute-start(bf16[1536,768]{1,0:T(8,128)(2,1)} %refs_5_.1), channel_id=1, source_target_pairs={{0,1},{1,0},{2,3},{3,2},{4,5},{5,4},{6,7},{7,6},{8,9},{9,8},{10,11... | collective-permute-start | bytes 7077896 | tf_op jit(solution)/shard_map/ppermute | solution.py:509
  1.2 19.3 %collective-permute-start.3 = (bf16[192,384]{1,0:T(8,128)(2,1)}, bf16[192,384]{1,0:T(8,128)(2,1)S(1)}, u32[]{:S(2)}, u32[]{:S(2)}) collective-permute-start(bf16[192,384]{1,0:T(8,128)(2,1)} %bitcast.19), channel_id=1, source_target_pairs={{0,1},{1,0},{2,3},{3,2},{4,5},{5,4},{6,7},{7,6},{8,9},{9,8},{10,11... | collective-permute-start | bytes 442376 | tf_op jit(solution)/shard_map/ppermute | solution.py:509
  1.7 18.8 %collective-permute-start.2 = (bf16[192,384]{1,0:T(8,128)(2,1)}, bf16[192,384]{1,0:T(8,128)(2,1)S(1)}, u32[]{:S(2)}, u32[]{:S(2)}) collective-permute-start(bf16[192,384]{1,0:T(8,128)(2,1)} %refs_11_.1), channel_id=1, source_target_pairs={{0,1},{1,0},{2,3},{3,2},{4,5},{5,4},{6,7},{7,6},{8,9},{9,8},{10,11... | collective-permute-start | bytes 442376 | tf_op jit(solution)/shard_map/ppermute | solution.py:509
  51.5 33.2 %collective-permute-start.6 = (bf16[512,768]{1,0:T(8,128)(2,1)S(1)}, bf16[512,768]{1,0:T(8,128)(2,1)S(1)}, u32[]{:S(2)}, u32[]{:S(2)}) collective-permute-start(bf16[512,768]{1,0:T(8,128)(2,1)S(1)} %get-tuple-element.165), channel_id=1, source_target_pairs={{0,2},{1,3},{2,0},{3,1},{4,6},{5,7},{6,4},{7,5},{8,10},{9,11},{10,... | collective-permute-start | bytes 2359304 | tf_op jit(solution)/shard_map/ppermute | solution.py:509
  58.4 24.6 %collective-permute-start.9 = (bf16[288,768]{1,0:T(8,128)(2,1)S(1)}, bf16[288,768]{1,0:T(8,128)(2,1)S(1)}, u32[]{:S(2)}, u32[]{:S(2)}) collective-permute-start(bf16[288,768]{1,0:T(8,128)(2,1)S(1)} %get-tuple-element.159), channel_id=1, source_target_pairs={{0,8},{1,9},{2,10},{3,11},{4,12},{5,13},{6,14},{7,15},{8,0},{9,1},... | collective-permute-start | bytes 1327112 | tf_op jit(solution)/shard_map/ppermute | solution.py:509
  59.3 32.7 %collective-permute-start.8 = (bf16[576,768]{1,0:T(8,128)(2,1)S(1)}, bf16[576,768]{1,0:T(8,128)(2,1)S(1)}, u32[]{:S(2)}, u32[]{:S(2)}) collective-permute-start(bf16[576,768]{1,0:T(8,128)(2,1)S(1)} %get-tuple-element.161), channel_id=1, source_target_pairs={{0,4},{1,5},{2,6},{3,7},{4,0},{5,1},{6,2},{7,3},{8,12},{9,13},{10,... | collective-permute-start | bytes 2654216 | tf_op jit(solution)/shard_map/ppermute | solution.py:509
  113.3 22.2 %collective-permute-start.16 = (bf16[1664,768]{1,0:T(8,128)(2,1)S(1)}, bf16[1664,768]{1,0:T(8,128)(2,1)S(1)}, u32[]{:S(2)}, u32[]{:S(2)}) collective-permute-start(bf16[1664,768]{1,0:T(8,128)(2,1)S(1)} %slice.328), channel_id=1, source_target_pairs={{0,1},{1,0},{2,3},{3,2},{4,5},{5,4},{6,7},{7,6},{8,9},{9,8},{10,11... | collective-permute-start | bytes 7667720 | tf_op jit(solution)/shard_map/ppermute | solution.py:509
  116.6 18.8 %collective-permute-start.42 = (bf16[144,768]{1,0:T(8,128)(2,1)S(1)}, bf16[144,768]{1,0:T(8,128)(2,1)S(1)}, u32[]{:S(2)}, u32[]{:S(2)}) collective-permute-start(bf16[144,768]{1,0:T(8,128)(2,1)S(1)} %slice_add_fusion.24), channel_id=1, source_target_pairs={{0,2},{1,3},{2,0},{3,1},{4,6},{5,7},{6,4},{7,5},{8,10},{9,11},{10,... | collective-permute-start | bytes 663560 | tf_op jit(solution)/shard_map/ppermute | solution.py:509
  130.7 54.2 %collective-permute-start.52 = (bf16[128,768]{1,0:T(8,128)(2,1)S(1)}, bf16[128,768]{1,0:T(8,128)(2,1)S(1)}, u32[]{:S(2)}, u32[]{:S(2)}) collective-permute-start(bf16[128,768]{1,0:T(8,128)(2,1)S(1)} %slice.450), channel_id=1, source_target_pairs={{0,8},{1,9},{2,10},{3,11},{4,12},{5,13},{6,14},{7,15},{8,0},{9,1},... | collective-permute-start | bytes 589832 | tf_op jit(solution)/shard_map/ppermute | solution.py:509
  134.9 51.7 %collective-permute-start.56 = (bf16[128,768]{1,0:T(8,128)(2,1)S(1)}, bf16[128,768]{1,0:T(8,128)(2,1)S(1)}, u32[]{:S(2)}, u32[]{:S(2)}) collective-permute-start(bf16[128,768]{1,0:T(8,128)(2,1)S(1)} %pad_maximum_fusion.15), channel_id=1, source_target_pairs={{0,2},{1,3},{2,0},{3,1},{4,6},{5,7},{6,4},{7,5},{8,10},{9,11},{10,... | collective-permute-start | bytes 589832 | tf_op jit(solution)/shard_map/ppermute | solution.py:509
  138.8 25.7 %collective-permute-start.20 = (bf16[320,768]{1,0:T(8,128)(2,1)S(1)}, bf16[320,768]{1,0:T(8,128)(2,1)S(1)}, u32[]{:S(2)}, u32[]{:S(2)}) collective-permute-start(bf16[320,768]{1,0:T(8,128)(2,1)S(1)} %get-tuple-element.153), channel_id=1, source_target_pairs={{0,4},{1,5},{2,6},{3,7},{4,0},{5,1},{6,2},{7,3},{8,12},{9,13},{10,... | collective-permute-start | bytes 1474568 | tf_op jit(solution)/shard_map/ppermute | solution.py:509
  148.6 17.4 %collective-permute-start.17 = (bf16[320,768]{1,0:T(8,128)(2,1)S(1)}, bf16[320,768]{1,0:T(8,128)(2,1)S(1)}, u32[]{:S(2)}, u32[]{:S(2)}) collective-permute-start(bf16[320,768]{1,0:T(8,128)(2,1)S(1)} %get-tuple-element.155), channel_id=1, source_target_pairs={{0,2},{1,3},{2,0},{3,1},{4,6},{5,7},{6,4},{7,5},{8,10},{9,11},{10,... | collective-permute-start | bytes 1474568 | tf_op jit(solution)/shard_map/ppermute | solution.py:509
  163.5 24.4 %collective-permute-start.45 = (bf16[144,768]{1,0:T(8,128)(2,1)S(1)}, bf16[144,768]{1,0:T(8,128)(2,1)S(1)}, u32[]{:S(2)}, u32[]{:S(2)}) collective-permute-start(bf16[144,768]{1,0:T(8,128)(2,1)S(1)} %slice.448), channel_id=1, source_target_pairs={{0,2},{1,3},{2,0},{3,1},{4,6},{5,7},{6,4},{7,5},{8,10},{9,11},{10,... | collective-permute-start | bytes 663560 | tf_op jit(solution)/shard_map/ppermute | solution.py:509
  186.6 47.8 %collective-permute-start.57 = (bf16[256,768]{1,0:T(8,128)(2,1)S(1)}, bf16[256,768]{1,0:T(8,128)(2,1)S(1)}, u32[]{:S(2)}, u32[]{:S(2)}) collective-permute-start(bf16[256,768]{1,0:T(8,128)(2,1)S(1)} %pad_maximum_fusion.7.refs_2_), channel_id=1, source_target_pairs={{0,8},{1,9},{2,10},{3,11},{4,12},{5,13},{6,14},{7,15},{8,0},{9,1},... | collective-permute-start | bytes 1179656 | tf_op jit(solution)/shard_map/ppermute | solution.py:509
  187.9 24.7 %collective-permute-start.46 = (bf16[288,768]{1,0:T(8,128)(2,1)S(1)}, bf16[288,768]{1,0:T(8,128)(2,1)S(1)}, u32[]{:S(2)}, u32[]{:S(2)}) collective-permute-start(bf16[288,768]{1,0:T(8,128)(2,1)S(1)} %pad_maximum_fusion.4), channel_id=1, source_target_pairs={{0,8},{1,9},{2,10},{3,11},{4,12},{5,13},{6,14},{7,15},{8,0},{9,1},... | collective-permute-start | bytes 1327112 | tf_op jit(solution)/shard_map/ppermute | solution.py:509
  201.1 32.8 %collective-permute-start.31 = (bf16[160,768]{1,0:T(8,128)(2,1)S(1)}, bf16[160,768]{1,0:T(8,128)(2,1)S(1)}, u32[]{:S(2)}, u32[]{:S(2)}) collective-permute-start(bf16[160,768]{1,0:T(8,128)(2,1)S(1)} %pad_maximum_fusion.13), channel_id=1, source_target_pairs={{0,8},{1,9},{2,10},{3,11},{4,12},{5,13},{6,14},{7,15},{8,0},{9,1},... | collective-permute-start | bytes 737288 | tf_op jit(solution)/shard_map/ppermute | solution.py:509
  211.1 22.9 %collective-permute-start.28 = (bf16[160,768]{1,0:T(8,128)(2,1)S(1)}, bf16[160,768]{1,0:T(8,128)(2,1)S(1)}, u32[]{:S(2)}, u32[]{:S(2)}) collective-permute-start(bf16[160,768]{1,0:T(8,128)(2,1)S(1)} %pad_maximum_fusion.12), channel_id=1, source_target_pairs={{0,4},{1,5},{2,6},{3,7},{4,0},{5,1},{6,2},{7,3},{8,12},{9,13},{10,... | collective-permute-start | bytes 737288 | tf_op jit(solution)/shard_map/ppermute | solution.py:509
  212.7 41.4 %collective-permute-start.47 = (bf16[576,768]{1,0:T(8,128)(2,1)S(1)}, bf16[576,768]{1,0:T(8,128)(2,1)S(1)}, u32[]{:S(2)}, u32[]{:S(2)}) collective-permute-start(bf16[576,768]{1,0:T(8,128)(2,1)S(1)} %pad_maximum_fusion.refs_0_), channel_id=1, source_target_pairs={{0,4},{1,5},{2,6},{3,7},{4,0},{5,1},{6,2},{7,3},{8,12},{9,13},{10,... | collective-permute-start | bytes 2654216 | tf_op jit(solution)/shard_map/ppermute | solution.py:509
  213.4 18.7 %collective-permute-start.33 = (bf16[48,768]{1,0:T(8,128)(2,1)S(1)}, bf16[48,768]{1,0:T(8,128)(2,1)S(1)}, u32[]{:S(2)}, u32[]{:S(2)}) collective-permute-start(bf16[48,768]{1,0:T(8,128)(2,1)S(1)} %slice.443), channel_id=1, source_target_pairs={{0,4},{1,5},{2,6},{3,7},{4,0},{5,1},{6,2},{7,3},{8,12},{9,13},{10,... | collective-permute-start | bytes 221192 | tf_op jit(solution)/shard_map/ppermute | solution.py:509
  232.1 21.8 %collective-permute-start.54 = (bf16[512,768]{1,0:T(8,128)(2,1)S(1)}, bf16[512,768]{1,0:T(8,128)(2,1)S(1)}, u32[]{:S(2)}, u32[]{:S(2)}) collective-permute-start(bf16[512,768]{1,0:T(8,128)(2,1)S(1)} %pad_maximum_fusion.1.refs_0_), channel_id=1, source_target_pairs={{0,2},{1,3},{2,0},{3,1},{4,6},{5,7},{6,4},{7,5},{8,10},{9,11},{10,... | collective-permute-start | bytes 2359304 | tf_op jit(solution)/shard_map/ppermute | solution.py:509
  234.0 19.9 %collective-permute-start.50 = (bf16[288,768]{1,0:T(8,128)(2,1)S(1)}, bf16[288,768]{1,0:T(8,128)(2,1)S(1)}, u32[]{:S(2)}, u32[]{:S(2)}) collective-permute-start(bf16[288,768]{1,0:T(8,128)(2,1)S(1)} %pad_maximum_fusion.5.refs_2_), channel_id=1, source_target_pairs={{0,8},{1,9},{2,10},{3,11},{4,12},{5,13},{6,14},{7,15},{8,0},{9,1},... | collective-permute-start | bytes 1327112 | tf_op jit(solution)/shard_map/ppermute | solution.py:509
  234.1 18.3 %collective-permute-start.34 = (bf16[96,768]{1,0:T(8,128)(2,1)S(1)}, bf16[96,768]{1,0:T(8,128)(2,1)S(1)}, u32[]{:S(2)}, u32[]{:S(2)}) collective-permute-start(bf16[96,768]{1,0:T(8,128)(2,1)S(1)} %pad_maximum_fusion.16), channel_id=1, source_target_pairs={{0,2},{1,3},{2,0},{3,1},{4,6},{5,7},{6,4},{7,5},{8,10},{9,11},{10,... | collective-permute-start | bytes 442376 | tf_op jit(solution)/shard_map/ppermute | solution.py:509
  234.4 23.2 %collective-permute-start.29 = (bf16[320,768]{1,0:T(8,128)(2,1)S(1)}, bf16[320,768]{1,0:T(8,128)(2,1)S(1)}, u32[]{:S(2)}, u32[]{:S(2)}) collective-permute-start(bf16[320,768]{1,0:T(8,128)(2,1)S(1)} %pad_maximum_fusion.2.refs_0_), channel_id=1, source_target_pairs={{0,2},{1,3},{2,0},{3,1},{4,6},{5,7},{6,4},{7,5},{8,10},{9,11},{10,... | collective-permute-start | bytes 1474568 | tf_op jit(solution)/shard_map/ppermute | solution.py:509
  (62 other events, 588.0 us)

commit v2 on v1

v2 whole, which is shorter than its diff:
```python
import functools
import math

import jax
import jax.numpy as jnp
from jax import lax
from jax.experimental import pallas as pl
from jax.experimental.pallas import tpu as pltpu
from jax.sharding import PartitionSpec as P

HEADS = 12
NEG_FILL = -1e30
EPS = 1e-05
F32 = jnp.float32
BF16 = jnp.bfloat16
VMEM_SPEC = pl.BlockSpec(memory_space=pltpu.VMEM)
SMEM_SPEC = pl.BlockSpec(memory_space=pltpu.SMEM)
SCALE = 1.0


def nn(left, right):
    return lax.dot_general(left, right, (((1,), (0,)), ((), ())), preferred_element_type=F32)


def nt(left, right):
    return lax.dot_general(left, right, (((1,), (1,)), ((), ())), preferred_element_type=F32)


def tn(left, right):
    return lax.dot_general(left, right, (((0,), (0,)), ((), ())), preferred_element_type=F32)


def gelu_pair(hidden):
    below = 0.5 * (1.0 + lax.erf(hidden * math.sqrt(0.5)))
    bell = jnp.exp(-0.5 * hidden * hidden)
    return hidden * below, below + hidden * bell * (1.0 / math.sqrt(2.0 * math.pi))


def unit(hidden):
    center = hidden - jnp.mean(hidden, axis=-1, keepdims=True)
    spread = jnp.mean(center * center, axis=-1, keepdims=True)
    rate = lax.rsqrt(spread + EPS)
    return center * rate, rate


def unit_back(normed, rate, grad, gain):
    scaled = grad * gain
    return rate * (
        scaled
        - jnp.mean(scaled, axis=-1, keepdims=True)
        - normed * jnp.mean(scaled * normed, axis=-1, keepdims=True)
    )


def lane_masks(head, lane):
    base = (head // 8) * 8
    return (lane // 64) == (head % 2), (lane // 16) == (head - base)


ORDERS = (((0, 2, 1, 3), (1, 0, 2, 3)), ((1, 2, 0, 3), (2, 0, 1, 3)), ((0, 2, 1, 3), (2, 0, 1, 3)), ((0, 1, 2, 3), (1, 0, 2, 3)))
FIELDS_DOWN = ((("down", 0, 192),),)
FIELDS_UP = ((("left", 0, 96), ("right", 0, 96), ("low", 0, 32)),)
FIELDS_HALF = (
    (("query", 0, 32), ("key", 0, 32), ("value", 0, 16), ("mix", 0, 16), ("low", 0, 16)),
    (("query", 256, 16), ("key", 256, 16), ("value", 128, 32), ("mix", 128, 32)),
)
PLANS = (FIELDS_DOWN, FIELDS_UP, FIELDS_HALF)
HALF_ROWS = {"query": 384, "key": 384, "value": 384, "mix": 384, "low": 128}
EVENTS = (
    "B2", "D.core", "B3", "U.core", "turn", "p0", "p1", "D0.0", "p2", "U0.0", "D0.1", "close", "in", "D0.2",
    "U0.1", "A.core", "U0.2", "D0.3", "A1.0", "A0.0", "A1.1", "U0.3", "D0.4", "A0.1", "A1.2", "U0.4", "A0.2",
    "D0.5", "A1.3", "A0.3", "A1.4", "U0.5", "A0.4", "D0.6", "oD", "A1.5", "A0.5", "A1.6", "A0.6", "U0.6",
    "oU",
)


def leaf_of(fields):
    return sum(n for _, _, n in fields)


def streams_of(plan):
    base = 0
    first = sum(len(p) for p in PLANS[:PLANS.index(plan)])
    for i, fields in enumerate(plan):
        yield first + i, base, leaf_of(fields), fields
        base += 8 * leaf_of(fields)


def rows_of(plan):
    return sum(8 * leaf_of(fields) for fields in plan)


def sides_of(dp, tensor):
    bits = [(dp >> b) & 1 for b in range(4)]
    values = [tensor & 1]
    for orders in ORDERS:
        values += [bits[o[0]] * 4 + bits[o[1]] * 2 + bits[o[2]] for o in orders]
    return jnp.stack(values)


def place(out, sides, core, plan, field, value, start=0, shift=0, columns=slice(None)):
    for number, base, leaf, fields in streams_of(plan):
        mask = sides[1 + 2 * number + core]
        inner = 0
        for name, first, n in fields:
            if name == field:
                for l in range(8):
                    at = first + l * n - start
                    if 0 <= at < value.shape[0]:
                        row = shift + base + inner + leaf * jnp.bitwise_xor(mask, l)
                        row = pl.multiple_of(row, math.gcd(math.gcd(base + inner, leaf), 16))
                        out[pl.ds(row, n), columns] = value[at:at + n, :]
            inner += n


def place_half(out, sides, field, value):
    half = HALF_ROWS[field]
    for core in range(2):
        shift = jnp.bitwise_xor(sides[0], core) * rows_of(FIELDS_HALF)
        place(out, sides, core, FIELDS_HALF, field, value[core * half:(core + 1) * half, :], 0, shift)


def fetch(pairs, sems):
    copies = [pltpu.make_async_copy(src, dst, sems.at[i]) for i, (src, dst) in enumerate(pairs)]
    for copy in copies:
        copy.start()
    return copies


def front_kernel(
    count_ref, sides, text_any, layout_any, joint_t_any, joint_l_any, mix_t_any, mix_l_any,
    qkv_t, qkv_l, mixed_t, mixed_l, normed_t, normed_l, stats,
    text_ref, layout_ref, joint_t, joint_l, mix_t, mix_l, mix_acc, flipped, sems,
):
    slots, width_t = text_ref.shape
    width_l = layout_ref.shape[1]
    columns = [slice(j * width_t, (j + 1) * width_t) for j in range(3)]
    copies = fetch(
        [
            (layout_any.at[0], flipped), (joint_l_any, joint_l), (text_any.at[0], text_ref),
            *((joint_t_any.at[:, c], joint_t.at[:, c]) for c in columns),
            (mix_t_any, mix_t), (mix_l_any, mix_l),
        ],
        sems,
    )
    count = count_ref[0]
    mix_acc[...] = jnp.zeros_like(mix_acc)
    stats[...] = jnp.zeros_like(stats)
    copies[0].wait()
    copies[1].wait()
    layout_ref[...] = flipped[...].T
    for j in range(3):
        qkv_l[:, j * 256:j * 256 + width_l] = nn(
            layout_ref[...], joint_l[:, j * width_l:(j + 1) * width_l]
        ).astype(BF16)
        qkv_l[:, j * 256 + width_l:(j + 1) * 256] = jnp.zeros((slots, 256 - width_l), BF16)
    copies[2].wait()
    for j, c in enumerate(columns):
        copies[3 + j].wait()
        qkv_t[:, c] = nn(text_ref[...], joint_t[:, c]).astype(BF16)
    lane = lax.broadcasted_iota(jnp.int32, (slots, 128), 1)
    dead = lax.broadcasted_iota(jnp.int32, (slots, slots), 1) >= count

    def pair_step(pair, carry):
        spot = lambda start: pl.ds(pl.multiple_of(start, 128), 128)
        at_l = (pair // 4) * 128
        query_t, key_t, value_t = (qkv_t[:, spot(j * width_t + pair * 128)] for j in range(3))
        query_l, key_l, value_l = (qkv_l[:, spot(j * 256 + at_l)] for j in range(3))
        keys = jnp.concatenate([key_t, key_l], axis=1)
        values = jnp.concatenate([value_t, value_l], axis=1)
        for side in range(2):
            head = 2 * pair + side
            mask_t, mask_l = lane_masks(head, lane)
            queries = jnp.concatenate(
                [
                    jnp.where(mask_t, query_t * 0.125, 0),
                    jnp.where(mask_l, query_l * 0.25, 0),
                ],
                axis=1,
            ).astype(BF16)
            logits = jnp.where(dead, NEG_FILL, nt(queries, keys))
            top = jnp.max(logits, axis=1, keepdims=True)
            raised = jnp.exp(logits - top)
            mass = jnp.sum(raised, axis=1, keepdims=True)
            stats[...] = jnp.where(lane == head, top + jnp.log(mass), stats[...])
            out = nn(raised.astype(BF16), values) * (1.0 / mass)
            if side == 0:
                first = out[:, :128]
            else:
                mixed_t[:, spot(pair * 128)] = jnp.where(mask_t, out[:, :128], first).astype(BF16)
            mix_acc[:, spot(at_l)] = mix_acc[:, spot(at_l)] + jnp.where(mask_l, out[:, 128:], 0.0)
        return carry

    lax.fori_loop(0, HEADS // 2, pair_step, 0)
    mixed_l[...] = mix_acc[:, :width_l].astype(BF16)
    copies[6].wait()
    normed, rate = unit(text_ref[...].astype(F32) + nn(mixed_t[...], mix_t[...]))
    normed_t[...] = normed
    stats[...] = jnp.where(lane == 16, rate, stats[...])
    copies[7].wait()
    normed, rate = unit(layout_ref[...].astype(F32) + nn(mixed_l[...], mix_l[...]))
    normed_l[...] = normed
    stats[...] = jnp.where(lane == 17, rate, stats[...])


def column(stats, lane, which):
    return jnp.sum(jnp.where(lane == which, stats[...], 0.0), axis=1, keepdims=True)


ANY_SPEC = pl.BlockSpec(memory_space=pltpu.HBM)


def call(kernel, micros, outs, args, scratch=(), specs=None, aliases=None, limit=16, out_specs=None):
    moved = sum(math.prod(a.shape) * a.dtype.itemsize for a in args)
    return pl.pallas_call(
        kernel,
        out_shape=[(pltpu.VMEM(s, d) if kept else jax.ShapeDtypeStruct(s, d)) for s, d, kept in outs],
        in_specs=specs or [VMEM_SPEC] * len(args),
        out_specs=out_specs or [VMEM_SPEC] * len(outs),
        scratch_shapes=list(scratch),
        input_output_aliases=aliases or {},
        compiler_params=pltpu.CompilerParams(vmem_limit_bytes=limit * 1024 * 1024),
        cost_estimate=pl.CostEstimate(flops=int(micros * SCALE * 1.1e9), bytes_accessed=moved, transcendentals=0),
    )(*args)


def front(count, sides, text, layout, joint_t, joint_l, mix_t, mix_l):
    _, s, wt = text.shape
    wl = layout.shape[1]
    return call(
        front_kernel,
        12,
        [
            ((s, 3 * wt), BF16, True), ((s, 768), BF16, True), ((s, wt), BF16, True), ((s, wl), BF16, True),
            ((s, wt), F32, True), ((s, wl), F32, True), ((s, 128), F32, True),
        ],
        (count, sides, text, layout, joint_t, joint_l, mix_t, mix_l),
        [
            pltpu.VMEM((s, wt), BF16), pltpu.VMEM((s, wl), BF16), pltpu.VMEM((wt, 3 * wt), BF16),
            pltpu.VMEM((wl, 3 * wl), BF16), pltpu.VMEM((wt, wt), BF16), pltpu.VMEM((wl, wl), BF16),
            pltpu.VMEM((s, 256), F32), pltpu.VMEM((wl, s), BF16), pltpu.SemaphoreType.DMA((8,)),
        ],
        [SMEM_SPEC] * 2 + [ANY_SPEC] * 6,
        limit=56,
    )


def feed_kernel(
    sides, normed_t, normed_l, norms_t, norms_l, *refs,
):
    far_refs, refs = refs[:10], refs[10:]
    (
        result_t, result_l, second_t, second_l, dfeed_t, dfeed_l, low_t, low_l,
        act_t0, act_t1, slope_t0, slope_t1, act_l0, act_l1, slope_l0, slope_l1,
        dnorm_t, dnorm_l, down_far,
    ) = refs[:19]
    cot_t, cot_l, up_t0, up_t1, down_t0, down_t1, up_l0, up_l1, down_l0, down_l1 = far_refs
    step = 512
    cuts = [slice(at, at + step) for at in range(0, up_t0.shape[1], step)]
    first_t = normed_t[...] * norms_t[0:1, :] + norms_t[1:2, :]
    low_t[...] = first_t.astype(BF16)
    first_l = normed_l[...] * norms_l[0:1, :] + norms_l[1:2, :]
    low_l[...] = first_l.astype(BF16)
    for up, act, slope in ((up_t0, act_t0, slope_t0), (up_t1, act_t1, slope_t1)):
        for cut in cuts:
            active, rise = gelu_pair(nn(low_t[...], up[:, cut]))
            act[:, cut] = active.astype(BF16)
            slope[:, cut] = rise.astype(BF16)
    for up, act, slope in ((up_l0, act_l0, slope_l0), (up_l1, act_l1, slope_l1)):
        active, rise = gelu_pair(nn(low_l[...], up[...]))
        act[...] = active.astype(BF16)
        slope[...] = rise.astype(BF16)
    summed_l = first_l + nt(act_l0[...], down_l0[...]) + nt(act_l1[...], down_l1[...])
    summed_t = normed_t[...] * norms_t[0:1, :] + norms_t[1:2, :] + (
        nn(act_t0[...], down_t0[...]) + nn(act_t1[...], down_t1[...])
    )
    for summed, norms, cot, result, second, dfeed, dnorm in (
        (summed_t, norms_t, cot_t, result_t, second_t, dfeed_t, dnorm_t),
        (summed_l, norms_l, cot_l, result_l, second_l, dfeed_l, dnorm_l),
    ):
        normed, rate = unit(summed)
        value = (normed * norms[2:3, :] + norms[3:4, :]).astype(BF16)
        result[...] = value if result is result_t else value.T
        grad = (cot[0] if cot is cot_t else cot[0].T).astype(F32)
        dnorm[0:1, :] = jnp.sum(grad * normed, axis=0, keepdims=True)
        dnorm[1:2, :] = jnp.sum(grad, axis=0, keepdims=True)
        back = unit_back(normed, rate, grad, norms[2:3, :])
        second[...] = back
        dfeed[...] = back.astype(BF16)
    down_kernel(sides, 1, act_t1, dfeed_t, down_far)


def feed(sides, normed_t, normed_l, norms_t, norms_l, cot_t, cot_l, weights):
    s, wt = normed_t.shape
    wl = normed_l.shape[1]
    ht, hl = weights[0].shape[1], weights[4].shape[1]
    return call(
        feed_kernel,
        16,
        [((s, wt), BF16, False), ((wl, s), BF16, False)]
        + [((s, wt), F32, True), ((s, wl), F32, True)]
        + [((s, wt), BF16, True), ((s, wl), BF16, True)] * 2
        + [((s, ht), BF16, True)] * 4
        + [((s, hl), BF16, True)] * 4
        + [((2, wt), F32, True), ((2, wl), F32, True), ((ht, wt), BF16, False)],
        (sides, normed_t, normed_l, norms_t, norms_l, cot_t, cot_l) + tuple(weights),
        specs=[SMEM_SPEC] + [VMEM_SPEC] * 14,
        limit=16,
    )


def down_kernel(sides, far, act, dfeed, out):
    core = jnp.bitwise_xor(sides[0], far)
    step = 768
    for start in range(0, act.shape[1], step):
        place(out, sides, core, FIELDS_DOWN, "down", tn(act[:, start:start + step], dfeed[...]).astype(BF16), start)


def up_body(
    sides, far, dfeed_t, dfeed_l, low_t, low_l, down_t, down_l, slope_t, slope_l, act_l, up_t, up_l, prev_t, prev_l,
    grads, dfirst_t, dfirst_l, dhid,
):
    wt = low_t.shape[1]
    wl = low_l.shape[1]
    core = jnp.bitwise_xor(sides[0], far)
    for start in range(0, down_t.shape[0], wt):
        at = slice(start, start + wt)
        dhid[:, at] = (nt(dfeed_t[...], down_t[at, :]) * slope_t[:, at].astype(F32)).astype(BF16)
        field = "right" if start else "left"
        place(grads, sides, core, FIELDS_UP, field, tn(low_t[...], dhid[:, at]).astype(BF16))
    dfirst_t[...] = prev_t[...] + nt(dhid[...], up_t[...])
    hl = down_l.shape[1]
    dhidden = (nn(dfeed_l[...], down_l[...]) * slope_l[...].astype(F32)).astype(BF16)
    lower = tn(act_l[...], dfeed_l[...]).astype(BF16)
    packed = jnp.concatenate([tn(low_l[...], dhidden).astype(BF16), lower[:wl, :], lower[wl:, :]], axis=1)
    place(grads, sides, core, FIELDS_UP, "low", jnp.concatenate([packed, jnp.zeros((64, wt), BF16)], axis=0))
    dfirst_l[...] = prev_l[...] + nt(dhidden, up_l[...])


def up_kernel(sides, *refs):
    up_body(sides, 0, *refs)


def up_down_kernel(*refs):
    sides, act_t, refs = refs[0], refs[1], refs[2:]
    down_kernel(sides, 0, act_t, refs[0], refs[13])
    up_body(sides, 1, *refs[:13], *refs[14:])


def up_grad(sides, act_t, *args):
    dfeed_t, dfeed_l, low_t, low_l, down_t = args[:5]
    s, wt = low_t.shape
    wl = low_l.shape[1]
    ht = down_t.shape[0]
    outs = [((ht + wl + 64, wt), BF16, False), ((s, wt), F32, True), ((s, wl), F32, True)]
    scratch = [pltpu.VMEM((s, ht), BF16)]
    if act_t is None:
        specs = [SMEM_SPEC] + [VMEM_SPEC] * len(args)
        return call(up_kernel, 5, outs, (sides,) + args, scratch, specs)
    specs = [SMEM_SPEC] + [VMEM_SPEC] * (len(args) + 1)
    return call(up_down_kernel, 8, [((ht, wt), BF16, False)] + outs, (sides, act_t) + args, scratch, specs)


def turn_kernel(
    sides, mixed_t, mixed_l, normed_t, normed_l, stats, dfirst_t, dfirst_l, norms_t, norms_l, dnorm_t, dnorm_l, mix_t, mix_l,
    grads, dtext, dlayout, dmix_t, dmix_l, mix_low, norm_low, djoint_t, acc_l,
):
    slots, wt = mixed_t.shape
    wl = mixed_l.shape[1]
    acc_l[...] = jnp.zeros_like(acc_l)
    djoint_t[...] = jnp.zeros_like(djoint_t)
    lane = lax.broadcasted_iota(jnp.int32, (slots, 128), 1)
    kept = []
    for n, (first, normed, norms, dnorm, width, mixed, mix, dmix) in enumerate((
        (dfirst_t, normed_t, norms_t, dnorm_t, wt, mixed_t, mix_t, dmix_t),
        (dfirst_l, normed_l, norms_l, dnorm_l, wl, mixed_l, mix_l, dmix_l),
    )):
        grad = first[...]
        unitv = normed[...]
        gain_grad = jnp.sum(grad * unitv, axis=0, keepdims=True)
        shift_grad = jnp.sum(grad, axis=0, keepdims=True)
        rows = jnp.concatenate([gain_grad, shift_grad, dnorm[0:2, :]], axis=0)
        kept.append(jnp.concatenate(
            [rows.astype(BF16), jnp.zeros((12, width), BF16)], axis=0
        ) if width == wt else jnp.concatenate(
            [jnp.concatenate([rows.astype(BF16), jnp.zeros((4, wt - width), BF16)], axis=1), jnp.zeros((44, wt), BF16)],
            axis=0,
        ))
        resid = unit_back(unitv, column(stats, lane, 16 + n), grad, norms[0:1, :])
        low = resid.astype(BF16)
        if n == 0:
            dtext[...] = resid
            place_half(grads, sides, "mix", tn(mixed[...], low).astype(BF16))
            dmix[...] = nt(low, mix[...]).astype(BF16)
        else:
            dlayout[...] = resid
            mix_low[...] = tn(mixed[...], low).astype(BF16)
            dmix[:, :wl] = nt(low, mix[...]).astype(BF16)
            dmix[:, wl:] = jnp.zeros((slots, 256 - wl), BF16)
    norm_low[...] = jnp.concatenate(kept, axis=0)


def turn(*args):
    s, wt = args[1].shape
    wl = args[2].shape[1]
    rows = 4 * wt + wl + 64
    return call(
        turn_kernel,
        4,
        [
            ((rows, wt), BF16, True), ((s, wt), F32, True), ((s, wl), F32, True), ((s, wt), BF16, True),
            ((s, 256), BF16, True), ((wl, wl), BF16, True), ((64, wt), BF16, True), ((s, 3 * wt), BF16, True),
            ((s, 768), F32, True),
        ],
        args,
        specs=[SMEM_SPEC] + [VMEM_SPEC] * (len(args) - 1),
    )


def pairs_kernel(span_ref, count_ref, qkv_t, qkv_l, stats, dmix_t, dmix_l, djoint_in, acc_in, djoint_t, acc_l):
    slots, wt = dmix_t.shape
    count = count_ref[0]
    lane = lax.broadcasted_iota(jnp.int32, (slots, 128), 1)
    dead = lax.broadcasted_iota(jnp.int32, (slots, slots), 1) >= count

    def pair_step(pair, carry):
        spot = lambda start: pl.ds(pl.multiple_of(start, 128), 128)
        at_l = (pair // 4) * 128
        query_t, key_t, value_t = (qkv_t[:, spot(j * wt + pair * 128)] for j in range(3))
        query_l, key_l, value_l = (qkv_l[:, spot(j * 256 + at_l)] for j in range(3))
        upper_t = dmix_t[:, spot(pair * 128)]
        upper_l = dmix_l[:, spot(at_l)]
        keys = jnp.concatenate([key_t, key_l], axis=1)
        values = jnp.concatenate([value_t, value_l], axis=1)
        kept = None
        for side in range(2):
            head = 2 * pair + side
            mask_t, mask_l = lane_masks(head, lane)
            queries = jnp.concatenate(
                [
                    jnp.where(mask_t, query_t * 0.125, 0),
                    jnp.where(mask_l, query_l * 0.25, 0),
                ],
                axis=1,
            ).astype(BF16)
            logits = jnp.where(dead, NEG_FILL, nt(queries, keys))
            probs = jnp.exp(logits - column(stats, lane, head))
            own_t = jnp.where(mask_t, upper_t, 0).astype(BF16)
            own_l = jnp.where(mask_l, upper_l, 0).astype(BF16)
            grad_t = nt(own_t, value_t)
            grad_s = nt(jnp.concatenate([own_t, own_l], axis=1), values)
            score_t = (probs * (grad_t - jnp.sum(grad_t * probs, axis=1, keepdims=True))).astype(BF16)
            score_l = (probs * (grad_s - jnp.sum(grad_s * probs, axis=1, keepdims=True))).astype(BF16)
            dvalue = tn(probs.astype(BF16), jnp.concatenate([upper_t, upper_l], axis=1))
            dquery_t = nn(score_t, key_t) * 0.125
            dkey_t = tn(score_t, query_t) * 0.125
            dquery_l = nn(score_l, key_l) * 0.25
            dkey_l = tn(score_l, query_l) * 0.25
            if side == 0:
                kept = (dquery_t, dkey_t, dvalue[:, :128])
            else:
                for j, (old, new) in enumerate(zip(kept, (dquery_t, dkey_t, dvalue[:, :128]))):
                    djoint_t[:, spot(j * wt + pair * 128)] = jnp.where(mask_t, new, old).astype(BF16)
            for j, part in enumerate((dquery_l, dkey_l, dvalue[:, 128:])):
                at = spot(j * 256 + at_l)
                acc_l[:, at] = acc_l[:, at] + jnp.where(mask_l, part, 0.0)
        return carry

    lax.fori_loop(span_ref[0], span_ref[1], pair_step, 0)


def pairs(lo, hi, prev, *args):
    s, wt = args[4].shape
    span = jnp.array([lo, hi], jnp.int32)
    return call(
        pairs_kernel,
        3 * (hi - lo),
        [((s, 3 * wt), BF16, True), ((s, 768), F32, True)],
        (span,) + args + tuple(prev),
        specs=[SMEM_SPEC] * 2 + [VMEM_SPEC] * 7,
        aliases={7: 0, 8: 1},
    )


def close_kernel(
    sides, text_ref, layout_ref, djoint_t, acc_l, mix_low, norm_low, part_ref,
    grads, djoint_l,
):
    wt = text_ref.shape[2]
    wl = layout_ref.shape[1]
    for j, field in enumerate(("query", "key", "value")):
        place_half(grads, sides, field, tn(text_ref[0], djoint_t[:, j * wt:(j + 1) * wt]).astype(BF16))
    for j in range(3):
        djoint_l[:, j * wl:(j + 1) * wl] = acc_l[:, j * 256:j * 256 + wl].astype(BF16)
    low = jnp.concatenate([nn(layout_ref[0], djoint_l[...]).astype(BF16), mix_low[...]], axis=1)
    place_half(grads, sides, "low", jnp.concatenate([low, norm_low[...]], axis=0))


def close(*args):
    text, layout = args[1:3]
    _, s, wt = text.shape
    wl = layout.shape[1]
    return call(
        close_kernel,
        3,
        [(args[7].shape, BF16, True), ((s, 3 * wl), BF16, True)],
        args,
        specs=[SMEM_SPEC] + [VMEM_SPEC] * (len(args) - 1),
        aliases={7: 0},
    )


def inputs_kernel(djoint_t, djoint_l, joint_t, joint_l, dtext_in, dlayout_in, dtext, dlayout):
    dtext[...] = dtext_in[...] + nt(djoint_t[...], joint_t[...])
    dlayout[...] = (dlayout_in[...] + nt(djoint_l[...], joint_l[...])).T


def input_grads(*args):
    s, wt = args[4].shape
    wl = args[5].shape[1]
    return call(inputs_kernel, 3, [((s, wt), F32, False), ((wl, s), F32, False)], args)


AXES = ("dp", "tensor")


def swap(value, bits, many):
    dp, tensor = many
    pairs = []
    for d in range(dp):
        for t in range(tensor):
            to = (d, t ^ 1) if bits == -1 else (d ^ (1 << bits[t]), t)
            pairs.append((d * tensor + t, to[0] * tensor + to[1]))
    return lax.ppermute(value, AXES, pairs)


def cut_of(value, base, rows):
    return lax.slice_in_dim(value, base, base + rows, axis=0)


def tie(values, *others):
    got = lax.optimization_barrier((tuple(values), tuple(others)))
    return got[0]


class Stream:
    def __init__(self, fields, orders, many):
        self.half, self.orders, self.many = 4 * leaf_of(fields), orders, many

    def launch(self, phase, value):
        bits = tuple(order[min(phase, 6 - phase)] for order in self.orders)
        self.flying = swap(value, bits, self.many)
        return [value]

    def begin(self, own, got, base):
        half = self.half
        self.keep = cut_of(own, base, half) + cut_of(got, base, half)
        return self.launch(0, cut_of(own, base + half, half) + cut_of(got, base + half, half))

    def finish(self, phase, token):
        got, = tie([self.flying], *token)
        keep = self.keep
        if phase < 2:
            half = keep.shape[0] // 2
            self.keep = cut_of(keep, 0, half) + cut_of(got, 0, half)
            return self.launch(phase + 1, cut_of(keep, half, half) + cut_of(got, half, half))
        if phase == 6:
            self.keep = (keep, got)
            return [got]
        self.keep = keep + got if phase < 4 else jnp.concatenate([keep, got], axis=0)
        return self.launch(phase + 1, self.keep)


def unplace(parts, sides, core, plan, field, out, half=0):
    for i, (number, _, leaf, fields) in enumerate(streams_of(plan)):
        mask = sides[1 + 2 * number + core]
        inner = 0
        for name, first, n in fields:
            if name == field:
                for side in range(2):
                    part = parts[2 * i + side]

                    def copy(r, carry, first=first, n=n, inner=inner, part=part, mask=mask, side=side, leaf=leaf):
                        row = core * half + first + n * jnp.bitwise_xor(mask, 4 * side + r)
                        source = pl.ds(pl.multiple_of(inner + r * leaf, 16), n)
                        out[pl.ds(pl.multiple_of(row, 16), n), :] = part[source, :].astype(F32)
                        return carry

                    lax.fori_loop(0, 4, copy, 0)
            inner += n


def stage(refs, sems, fill):
    flying = []
    for i, (field, out, columns, buffer) in enumerate(refs):
        fill(field, buffer)
        copy = pltpu.make_async_copy(buffer, out.at[:, columns], sems.at[i])
        copy.start()
        flying.append(copy)
    return flying


def open_down_kernel(sides, *refs):
    parts, (out, buffer, sems) = refs[:-3], refs[-3:]
    unplace(parts, sides, sides[0], FIELDS_DOWN, "down", buffer)
    copy = pltpu.make_async_copy(buffer, out, sems.at[0])
    copy.start()
    copy.wait()


def open_up_kernel(sides, *refs):
    parts, (up_t, up_l, down_l, left, right, low, sems) = refs[:-7], refs[-7:]
    wt = up_t.shape[0]
    wl, hl = up_l.shape
    fill = functools.partial(unplace, parts, sides, sides[0], FIELDS_UP)
    flying = stage(
        [("left", up_t, slice(0, wt), left), ("right", up_t, slice(wt, 2 * wt), right)], sems, fill
    )
    fill("low", low)
    up_l[...] = low[:wl, :hl]
    down_l[:wl, :] = low[:wl, hl:hl + wl]
    down_l[wl:, :] = low[:wl, hl + wl:]
    for copy in flying:
        copy.wait()


def open_half_kernel(sides, *refs):
    count = 2 * len(FIELDS_HALF)
    own, other, refs = refs[:count], refs[count:2 * count], refs[2 * count:]
    joint_t, mix_t, joint_l, mix_l, norm_t, norm_l, *buffers, low, sems = refs
    wt, wl = mix_t.shape[0], mix_l.shape[0]

    def fill(field, out):
        for parts, core in ((own, sides[0]), (other, 1 - sides[0])):
            unplace(parts, sides, core, FIELDS_HALF, field, out, HALF_ROWS[field])

    outs = [(field, joint_t, slice(j * wt, (j + 1) * wt)) for j, field in enumerate(("query", "key", "value"))]
    flying = stage([(*o, b) for o, b in zip(outs + [("mix", mix_t, slice(0, wt))], buffers)], sems, fill)
    fill("low", low)
    joint_l[...] = low[:wl, :3 * wl]
    mix_l[...] = low[:wl, 3 * wl:]
    norm_t[...] = low[wl:wl + 4, :]
    norm_l[...] = low[wl + 16:wl + 20, :wl]
    for copy in flying:
        copy.wait()


def open_up(kernel, micros, direct, outs, buffers, sides, token, parts):
    if token:
        parts = [tie([parts[0]], *token)[0], *parts[1:]]
    return call(
        kernel, micros, [(shape, F32, False) for shape in outs], (sides,) + tuple(parts),
        [pltpu.VMEM(shape, F32) for shape in buffers] + [pltpu.SemaphoreType.DMA((4,))],
        [SMEM_SPEC] + [VMEM_SPEC] * len(parts), limit=24,
        out_specs=[ANY_SPEC] * direct + [VMEM_SPEC] * (len(outs) - direct),
    )


def shards(
    many, text_input, layout_input, page_counts, text_joint, text_mixing, text_norms, text_upward, text_downward,
    layout_joint, layout_mixing, layout_norms, layout_upward, layout_downward, text_cotangent, layout_cotangent,
):
    dp, tensor = many
    wt, wl = text_input.shape[2], layout_input.shape[2]
    layout_flip = layout_input.swapaxes(1, 2)
    halves = tensor == 2 and dp == 16
    own = (text_upward, text_downward, layout_upward, layout_downward.T)
    if halves:
        far = tuple(swap(w, -1, many) for w in own)
    else:
        whole = [
            lax.all_gather(w, "tensor", axis=axis, tiled=True) for w, axis in zip(own, (1, 0, 1, 1))
        ]
        cut = lambda w, axis, i: lax.slice_in_dim(w, i * (w.shape[axis] // 2), (i + 1) * (w.shape[axis] // 2), axis=axis)
        own = tuple(cut(w, axis, 0) for w, axis in zip(whole, (1, 0, 1, 1)))
        far = tuple(cut(w, axis, 1) for w, axis in zip(whole, (1, 0, 1, 1)))
    sides = sides_of(lax.axis_index("dp").astype(jnp.int32), lax.axis_index("tensor").astype(jnp.int32))
    if not halves:
        sides = jnp.zeros_like(sides)
    (
        qkv_t, qkv_l, mixed_t, mixed_l, normed_t, normed_l, stats,
    ) = front(page_counts, sides, text_input, layout_flip, text_joint, layout_joint, text_mixing, layout_mixing)
    up_t0, down_t0, up_l0, down_l0 = own
    up_t1, down_t1, up_l1, down_l1 = far
    (
        result_t, result_l, second_t, second_l, dfeed_t, dfeed_l, low_t, low_l,
        act_t0, act_t1, slope_t0, slope_t1, act_l0, act_l1, slope_l0, slope_l1, dnorm_t, dnorm_l, down_far,
    ) = feed(
        sides, normed_t, normed_l, text_norms, layout_norms, text_cotangent, layout_cotangent.swapaxes(1, 2),
        (own[0], far[0], own[1], far[1], own[2], far[2], own[3], far[3]),
    )
    run = {"token": [dfeed_t], "state": None, "first": (second_t, second_l)}
    streams = {
        "%s%d" % (name, number - first): Stream(fields, ORDERS[number], many)
        for name, plan in zip("DUA", PLANS)
        for first in [sum(len(p) for p in PLANS[:PLANS.index(plan)])]
        for number, _, _, fields in streams_of(plan)
    }
    got = {}
    if halves:
        got["D"] = swap(down_far, -1, many)

    def held(value):
        return tie([value], *run["token"])[0]

    def far_grads():
        down_own, up_far, *run["first"] = up_grad(
            sides, act_t0, held(dfeed_t),
            dfeed_l, low_t, low_l, down_t1, down_l1, slope_t1, slope_l1, act_l1, up_t1, up_l1, *run["first"]
        )
        run["down_own"], run["up_far"], run["token"] = down_own, up_far, [run["first"][0]]
        if halves:
            got["U"] = swap(up_far, -1, many)

    def own_grads():
        run["up_own"], *run["first"] = up_grad(
            sides, None, held(dfeed_t),
            dfeed_l, low_t, low_l, down_t0, down_l0, slope_t0, slope_l0, act_l0, up_t0, up_l0, *run["first"]
        )
        run["token"] = [run["first"][0]]

    def turn_back():
        run["grads"], run["dtext"], run["dlayout"], run["dmix_t"], run["dmix_l"], run["mix_low"], run["norm_low"], *run["state"] = turn(
            sides, mixed_t, mixed_l, normed_t, normed_l, stats, held(run["first"][0]), run["first"][1], text_norms,
            layout_norms, dnorm_t, dnorm_l, text_mixing, layout_mixing,
        )
        run["token"] = [run["dmix_t"]]

    def pair_grads(lo, hi):
        run["state"] = pairs(
            lo, hi, run["state"], page_counts, qkv_t, qkv_l, stats, held(run["dmix_t"]), run["dmix_l"]
        )
        run["token"] = [run["state"][1]]

    def close_up():
        state = run["state"]
        run["grads"], run["djoint_l"] = close(
            sides, text_input, layout_flip, state[0], held(state[1]), run["mix_low"], run["norm_low"], run["grads"],
        )
        run["token"] = [run["djoint_l"]]
        if halves:
            rows = run["grads"].shape[0] // 2
            run["half_own"] = cut_of(run["grads"], 0, rows)
            got["A"] = swap(cut_of(run["grads"], rows, rows), -1, many)

    def inputs_up():
        run["dtext"], run["dlayout"] = input_grads(
            run["state"][0], held(run["djoint_l"]), text_joint, layout_joint, run["dtext"], run["dlayout"]
        )
        run["token"] = [run["dlayout"]]

    ht, hl = text_upward.shape[1], layout_upward.shape[1]

    def parts_of(name, plan):
        return [part for i in range(len(plan)) for part in streams["%s%d" % (name, i)].keep]

    def open_down():
        run["down"] = open_up(open_down_kernel, 3, 1, [(ht, wt)], [(ht, wt)], sides, run["token"], parts_of("D", FIELDS_DOWN))
        run["token"] = list(run["down"])

    def open_upper():
        run["up"] = open_up(
            open_up_kernel, 3, 1, [(wt, ht), (wl, hl), (hl, wl)], [(wt, wt)] * 2 + [(256, wt)], sides, run["token"], parts_of("U", FIELDS_UP)
        )
        run["token"] = list(run["up"])

    kernels = {
        "B2": far_grads, "B3": own_grads, "turn": turn_back, "p0": lambda: pair_grads(0, 2),
        "p1": lambda: pair_grads(2, 4), "p2": lambda: pair_grads(4, 6), "close": close_up, "in": inputs_up,
    }
    opens = {"oD": open_down, "oU": open_upper}
    owns = {"D": ("down_own", FIELDS_DOWN), "U": ("up_own", FIELDS_UP), "A": ("half_own", FIELDS_HALF)}
    for event in EVENTS if halves else [e for e in EVENTS if e in kernels]:
        if event in kernels:
            kernels[event]()
        elif event in opens:
            opens[event]()
        else:
            name, step = event.split(".")
            if step == "core":
                here, = tie([got[name]], *run["token"])
                own_of, plan = owns[name]
                run["token"], base = [], 0
                for i, fields in enumerate(plan):
                    run["token"] += streams["%s%d" % (name, i)].begin(run[own_of], here, base)
                    base += 8 * leaf_of(fields)
            else:
                run["token"] = streams[name].finish(int(step), run["token"])
    grads, dtext, dlayout = run["grads"], run["dtext"], run["dlayout"]
    down_own, up_own, up_far = run["down_own"], run["up_own"], run["up_far"]

    if halves:
        own_parts = parts_of("A", FIELDS_HALF)
        far_parts = [swap(part, -1, many) for part in own_parts]
        down_grad_t, = run["down"]
        up_grad_t, up_grad_l, down_grad_l = run["up"]
        joint_t, mix_t, joint_l, mix_l, norm_t, norm_l = open_up(
            open_half_kernel, 4, 2, [(wt, 3 * wt), (wt, wt), (wl, 3 * wl), (wl, wl), (4, wt), (4, wl)],
            [(wt, wt)] * 4 + [(256, wt)], sides, [], own_parts + far_parts,
        )
    else:
        def parts(packed, plan, shift=0):
            return [
                cut_of(packed, shift + base + i * 4 * leaf, 4 * leaf)
                for _, base, leaf, _ in streams_of(plan) for i in range(2)
            ]

        hidden, wide = down_own.shape[0], up_l0.shape[1]
        downs = [
            open_up(open_down_kernel, 3, 1, [(hidden, wt)], [(hidden, wt)], sides, [], parts(p, FIELDS_DOWN))[0]
            for p in (down_own, down_far)
        ]
        ups = [
            open_up(
                open_up_kernel, 3, 1, [(wt, hidden), (wl, wide), (wide, wl)], [(wt, wt)] * 2 + [(256, wt)], sides, [],
                parts(p, FIELDS_UP),
            )
            for p in (up_own, up_far)
        ]
        joined = [
            jnp.concatenate([ups[0][0], ups[1][0]], axis=1),
            jnp.concatenate(downs, axis=0),
            jnp.concatenate([ups[0][1], ups[1][1]], axis=1),
            jnp.concatenate([ups[0][2], ups[1][2]], axis=0),
        ]
        up_grad_t, down_grad_t, up_grad_l, down_grad_l = (
            lax.psum(lax.psum_scatter(g, "tensor", scatter_dimension=axis, tiled=True), "dp")
            for g, axis in zip(joined, (1, 0, 1, 0))
        )
        rows = grads.shape[0] // 2
        joint_t, mix_t, joint_l, mix_l, norm_t, norm_l = lax.psum(open_up(
            open_half_kernel, 4, 2, [(wt, 3 * wt), (wt, wt), (wl, 3 * wl), (wl, wl), (4, wt), (4, wl)],
            [(wt, wt)] * 4 + [(256, wt)], sides, [],
            parts(grads, FIELDS_HALF) + parts(grads, FIELDS_HALF, rows),
        ), AXES)
    return (
        result_t[None],
        result_l.T[None],
        dtext[None],
        dlayout.T[None],
        joint_t,
        mix_t,
        norm_t,
        up_grad_t.astype(F32),
        down_grad_t.astype(F32),
        joint_l,
        mix_l,
        norm_l,
        up_grad_l.astype(F32),
        down_grad_l.astype(F32),
    )


def solution(mesh):
    many = (mesh.shape["dp"], mesh.shape["tensor"])
    pages = P(("dp", "tensor"), None, None)
    columns, rows = P(None, "tensor"), P("tensor", None)
    return jax.shard_map(
        functools.partial(shards, many),
        mesh=mesh,
        in_specs=(
            pages, pages, P(("dp", "tensor")), P(), P(), P(), columns, rows, P(), P(), P(), columns, rows, pages, pages,
        ),
        out_specs=(
            pages, pages, pages, pages, P(), P(), P(), columns, rows, P(), P(), P(), columns, rows,
        ),
        check_vma=False,
    )
```

time: 282 us -> 219 us (0.78)
  waiting for transfers between devices: 123 us -> 83.8 us
  starting transfers between devices: 56.6 us -> 34.4 us
    ppermute x58 -> x39, waiting for transfers between devices: 123 us -> 83.8 us  [swap(): return lax.ppermute(value, AXES, pairs)]
    ppermute x58 -> x39, starting transfers between devices: 56.6 us -> 34.4 us  [swap(): return lax.ppermute(value, AXES, pairs)]
    pallas_call x12 -> x13, Pallas kernels: 83.2 us -> 83.4 us  [call(): pl.pallas_call(kernel, out_shape=[pltpu.VMEM(s, d) if kept else jax.Shape...]
  transfers between devices with their start and end apart: 58 -> 39, of which waited for: 20 -> 16; matrix products, arithmetic and copies ran while one was open for 1% -> 2% of each run, Pallas kernels for 20% -> 28%
where the time goes in v2:
time: 219 us; the launch traced here: 215 us
  waiting for transfers between devices  83.8 us (38%)
  Pallas kernels  83.4 us (38%)
  starting transfers between devices  34.4 us (16%)
  local copies, waits for them, and re-layouts  9.19 us (4%)
  other arithmetic  2.3 us (1%)
    ppermute x39, waiting for transfers between devices, swap(): return lax.ppermute(value, AXES, pairs)  83.8 us
    pallas_call x13, Pallas kernels, call(): pl.pallas_call(kernel, out_shape=[pltpu.VMEM(s, d) if kept else jax.Shape...  83.4 us
    ppermute x39, starting transfers between devices, swap(): return lax.ppermute(value, AXES, pairs)  34.4 us
    unnamed x57, local copies, waits for them, and re-layouts  8.42 us
  transfers between devices with their start and end apart: 39, of which 16 were waited for; matrix products, arithmetic and copies ran while one was open for 2% of the time, Pallas kernels for 28%

profile of v2, /device:TPU:0, one launch (start us, length us, event | category | flops | bytes accessed | tf_op | source)
XLA Modules:
  0.0 215.1 jit_solution(1675634177403752031)
XLA Ops:
  3.1 14.3 %shard_map.281 = (bf16[512,2304]{1,0:T(8,128)(2,1)S(1)}, bf16[512,768]{1,0:T(8,128)(2,1)S(1)}, bf16[512,768]{1,0:T(8,128)(2,1)S(1)}, bf16[512,192]{1,0:T(8,128)(...) custom-call(s32[1]{0:T(128)S(6)} %copy.47.count_ref, s32[9]{0:T(128)} %stack.30.sides.refs_0_, ...), custom_call_target="tpu_custom_call" | custom-call | flops 13200000000 | bytes 5996584 | tf_op jit(solution)/shard_map/pallas_call | solution.py:215
  24.9 13.3 %shard_map.282 = (bf16[512,768]{1,0:T(8,128)(2,1)}, bf16[192,512]{1,0:T(8,128)(2,1)}, f32[512,768]{1,0:T(8,128)S(1)}, f32[512,192]{1,0:T(8,128)S(1)}, bf16[512,7...) custom-call(s32[9]{0:T(128)S(1)} %copy-done, ...), custom_call_target="tpu_custom_call" | custom-call | flops 17600000000 | bytes 12991524 | tf_op jit(solution)/shard_map/pallas_call | solution.py:215
  38.7 8.5 %shard_map.283 = (bf16[1536,768]{1,0:T(8,128)(2,1)S(1)}, bf16[1792,768]{1,0:T(8,128)(2,1)S(1)}, f32[512,768]{1,0:T(8,128)S(1)}, f32[512,192]{1,0:T(8,128)S(1)}) custom-call(s32[9]{0:T(128)S(1)} %copy-done, bf16[512,1536]{1,0:T(8,128)(2,1)S(1)} %get-tuple-element.124.refs_1_, bf16[512,768]{1,0:T(8,128)(2,1)S(1)} %get-tuple-element.138.refs_2_.refs_0_, ...), custom_call_target="tpu_custom_call" | custom-call | flops 8800000000 | bytes 12877860 | tf_op jit(solution)/shard_map/pallas_call | solution.py:215
  47.6 3.0 %collective-permute-start.6 = (bf16[768,768]{1,0:T(8,128)(2,1)S(1)}, bf16[768,768]{1,0:T(8,128)(2,1)S(1)}, u32[]{:S(2)}, u32[]{:S(2)}) collective-permute-start(bf16[768,768]{1,0:T(8,128)(2,1)S(1)} %get-tuple-element.235), channel_id=1, source_target_pairs={{0,2},{1,5},{2,0},{3,7},{4,6},{5,1},{6,4},{7,3},{8,10},{9,13},{10,... | collective-permute-start | bytes 3538952 | tf_op jit(solution)/shard_map/ppermute | solution.py:534
  50.6 5.1 %shard_map.284 = (bf16[1792,768]{1,0:T(8,128)(2,1)S(1)}, f32[512,768]{1,0:T(8,128)S(1)}, f32[512,192]{1,0:T(8,128)S(1)}) custom-call(s32[9]{0:T(128)S(1)} %copy-done, bf16[512,768]{1,0:T(8,128)(2,1)S(1)} %get-tuple-element.138.refs_2_.refs_0_, bf16[512,192]{1,0:T(8,128)(2,1)S(1)} %get-tuple-element.126.refs_3_.refs_1_, ...), custom_call_target="tpu_custom_call" | custom-call | flops 5500000256 | bytes 11304996 | tf_op jit(solution)/shard_map/pallas_call | solution.py:215
  58.3 2.9 %shard_map.285 = (bf16[3328,768]{1,0:T(8,128)(2,1)S(1)}, f32[512,768]{1,0:T(8,128)S(1)}, f32[512,192]{1,0:T(8,128)S(1)}, bf16[512,768]{1,0:T(8,128)(2,1)S(1)}, b...) custom-call(s32[9]{0:T(128)S(1)} %copy-done, ...), custom_call_target="tpu_custom_call" | custom-call | flops 4400000000 | bytes 6453796 | tf_op jit(solution)/shard_map/pallas_call | solution.py:215
  61.2 6.8 %shard_map.286 = (bf16[512,2304]{1,0:T(8,128)(2,1)S(1)}, f32[512,768]{1,0:T(8,128)S(1)}) custom-call(s32[2]{0:T(128)S(1)} %iota_multiply_fusion.span_ref, s32[1]{0:T(128)S(6)} %copy.47.count_ref, bf16[512,2304]{1,0:T(8,128)(2,1)S(1)} %get-tuple-element.118.qkv_t, bf16[512,768]{1,0:T(8,128)(2,1)S(1)} %copy-done.23, ...), custom_call_target="tpu_custom_call", output_to_operand_aliasing={{0}: (7, {}), {1}: (8, {})} | custom-call | flops 6600000000 | bytes 8388620 | tf_op jit(solution)/shard_map/pallas_call | solution.py:215
  68.0 6.3 %shard_map.287 = (bf16[512,2304]{1,0:T(8,128)(2,1)S(1)}, f32[512,768]{1,0:T(8,128)S(1)}) custom-call(s32[2]{0:T(128)S(1)} %copy-done.18, s32[1]{0:T(128)S(6)} %copy.47.count_ref, bf16[512,2304]{1,0:T(8,128)(2,1)S(1)} %get-tuple-element.118.qkv_t, bf16[512,768]{1,0:T(8,128)(2,1)S(1)} %copy-done.23, ...), custom_call_target="tpu_custom_call", output_to_operand_aliasing={{0}: (7, {}), {1}: (8, {})} | custom-call | flops 6600000000 | bytes 8388620 | tf_op jit(solution)/shard_map/pallas_call | solution.py:215
  76.1 6.5 %shard_map.288 = (bf16[512,2304]{1,0:T(8,128)(2,1)S(1)}, f32[512,768]{1,0:T(8,128)S(1)}) custom-call(s32[2]{0:T(128)S(1)} %copy-done.17, s32[1]{0:T(128)S(6)} %copy.47.count_ref, bf16[512,2304]{1,0:T(8,128)(2,1)S(1)} %get-tuple-element.118.qkv_t, bf16[512,768]{1,0:T(8,128)(2,1)S(1)} %copy-done.23, ...), custom_call_target="tpu_custom_call", output_to_operand_aliasing={{0}: (7, {}), {1}: (8, {})} | custom-call | flops 6600000000 | bytes 8388620 | tf_op jit(solution)/shard_map/pallas_call | solution.py:215
  84.5 2.8 %shard_map.289 = (bf16[3328,768]{1,0:T(8,128)(2,1)S(1)}, bf16[512,576]{1,0:T(8,128)(2,1)S(1)}) custom-call(s32[9]{0:T(128)S(1)} %copy-done, bf16[1,512,768]{2,1,0:T(8,128)(2,1)S(1)} %copy-done.8, bf16[1,192,512]{2,1,0:T(8,128)(2,1)S(1)} %bitcast.19, bf16[512,2304]{1,0:T(8,128)(2,1)S(1)} %get-tuple-element.163.djoint_t, ...), custom_call_target="tpu_custom_call", output_to_operand_aliasing={{0}: (7, {})} | custom-call | flops 3300000000 | bytes 10199076 | tf_op jit(solution)/shard_map/pallas_call | solution.py:215
  90.3 3.5 %shard_map.290 = (f32[512,768]{1,0:T(8,128)}, f32[192,512]{1,0:T(8,128)}) custom-call(bf16[512,2304]{1,0:T(8,128)(2,1)S(1)} %get-tuple-element.163.djoint_t, bf16[512,576]{1,0:T(8,128)(2,1)S(1)} %get-tuple-element.171.djoint_l, bf16[768,2304]{1,0:T(8,128)(2,1)S(1)} %copy-done.1, bf16[192,576]{1,0:T(8,128)(2,1)S(1)} %copy-done.9, ...), custom_call_target="tpu_custom_call" | custom-call | flops 3300000000 | bytes 8675328 | tf_op jit(solution)/shard_map/pallas_call | solution.py:215
  96.0 5.7 %collective-permute-done.10 = bf16[448,768]{1,0:T(8,128)(2,1)S(1)} collective-permute-done((bf16[448,768]{1,0:T(8,128)(2,1)S(1)}, bf16[448,768]{1,0:T(8,128)(2,1)S(1)}, u32[]{:S(2)}, u32[]{:S(2)}) %collective-permute-start.10) | collective-permute-done | bytes 688160 | tf_op jit(solution)/shard_map/ppermute | solution.py:534
  105.5 2.6 %collective-permute-start.14 = (bf16[192,768]{1,0:T(8,128)(2,1)S(1)}, bf16[192,768]{1,0:T(8,128)(2,1)S(1)}, u32[]{:S(2)}, u32[]{:S(2)}) collective-permute-start(bf16[192,768]{1,0:T(8,128)(2,1)S(1)} %fusion.1), channel_id=1, source_target_pairs={{0,16},{1,17},{2,18},{3,19},{4,20},{5,21},{6,22},{7,23},{8,24},{9,... | collective-permute-start | bytes 884744 | tf_op jit(solution)/shard_map/ppermute | solution.py:534
  109.2 10.4 %collective-permute-done.14 = bf16[192,768]{1,0:T(8,128)(2,1)S(1)} collective-permute-done((bf16[192,768]{1,0:T(8,128)(2,1)S(1)}, bf16[192,768]{1,0:T(8,128)(2,1)S(1)}, u32[]{:S(2)}, u32[]{:S(2)}) %collective-permute-start.14) | collective-permute-done | bytes 294944 | tf_op jit(solution)/shard_map/ppermute | solution.py:534
  121.8 5.0 %collective-permute-done.12 = bf16[448,768]{1,0:T(8,128)(2,1)S(1)} collective-permute-done((bf16[448,768]{1,0:T(8,128)(2,1)S(1)}, bf16[448,768]{1,0:T(8,128)(2,1)S(1)}, u32[]{:S(2)}, u32[]{:S(2)}) %collective-permute-start.12) | collective-permute-done | bytes 688160 | tf_op jit(solution)/shard_map/ppermute | solution.py:534
  129.0 9.5 %collective-permute-done.18 = bf16[224,768]{1,0:T(8,128)(2,1)S(1)} collective-permute-done((bf16[224,768]{1,0:T(8,128)(2,1)S(1)}, bf16[224,768]{1,0:T(8,128)(2,1)S(1)}, u32[]{:S(2)}, u32[]{:S(2)}) %collective-permute-start.18) | collective-permute-done | bytes 344096 | tf_op jit(solution)/shard_map/ppermute | solution.py:534
  141.2 8.5 %collective-permute-done.21 = bf16[224,768]{1,0:T(8,128)(2,1)S(1)} collective-permute-done((bf16[224,768]{1,0:T(8,128)(2,1)S(1)}, bf16[224,768]{1,0:T(8,128)(2,1)S(1)}, u32[]{:S(2)}, u32[]{:S(2)}) %collective-permute-start.21) | collective-permute-done | bytes 344096 | tf_op jit(solution)/shard_map/ppermute | solution.py:534
  153.8 12.0 %collective-permute-done.24 = bf16[96,768]{1,0:T(8,128)(2,1)S(1)} collective-permute-done((bf16[96,768]{1,0:T(8,128)(2,1)S(1)}, bf16[96,768]{1,0:T(8,128)(2,1)S(1)}, u32[]{:S(2)}, u32[]{:S(2)}) %collective-permute-start.24) | collective-permute-done | bytes 147488 | tf_op jit(solution)/shard_map/ppermute | solution.py:534
  168.7 3.7 %collective-permute-done.28 = bf16[96,768]{1,0:T(8,128)(2,1)S(1)} collective-permute-done((bf16[96,768]{1,0:T(8,128)(2,1)S(1)}, bf16[96,768]{1,0:T(8,128)(2,1)S(1)}, u32[]{:S(2)}, u32[]{:S(2)}) %collective-permute-start.28) | collective-permute-done | bytes 147488 | tf_op jit(solution)/shard_map/ppermute | solution.py:534
  177.4 3.1 %shard_map.291 = f32[1536,768]{1,0:T(8,128)} custom-call(s32[9]{0:T(128)S(1)} %copy-done, bf16[768,768]{1,0:T(8,128)(2,1)S(1)} %pad_maximum_fusion.1.refs_0_, bf16[768,768]{1,0:T(8,128)(2,1)S(1)} %collective-permute-done.31.refs_1_), custom_call_target="tpu_custom_call" | custom-call | flops 3300000000 | bytes 2359332 | tf_op jit(solution)/shard_map/pallas_call | solution.py:215
  180.6 5.2 %collective-permute-done.29 = bf16[224,768]{1,0:T(8,128)(2,1)S(1)} collective-permute-done((bf16[224,768]{1,0:T(8,128)(2,1)S(1)}, bf16[224,768]{1,0:T(8,128)(2,1)S(1)}, u32[]{:S(2)}, u32[]{:S(2)}) %collective-permute-start.29) | collective-permute-done | bytes 344096 | tf_op jit(solution)/shard_map/ppermute | solution.py:534
  187.9 15.3 %collective-permute-done.33.refs_3_ = bf16[384,768]{1,0:T(8,128)(2,1)} collective-permute-done((bf16[384,768]{1,0:T(8,128)(2,1)S(1)}, bf16[384,768]{1,0:T(8,128)(2,1)}, u32[]{:S(2)}, u32[]{:S(2)}) %collective-permute-start.33) | collective-permute-done | bytes 589856 | tf_op jit(solution)/shard_map/ppermute | solution.py:534
  203.8 3.7 %shard_map.293 = (f32[768,1536]{1,0:T(8,128)}, f32[192,384]{1,0:T(8,128)}, f32[384,192]{1,0:T(8,128)S(1)}) custom-call(s32[9]{0:T(128)S(1)} %copy-done, bf16[896,768]{1,0:T(8,128)(2,1)S(1)} %pad_maximum_fusion.refs_0_, bf16[896,768]{1,0:T(8,128)(2,1)S(1)} %collective-permute-done.38.refs_1_), custom_call_target="tpu_custom_call" | custom-call | flops 3300000000 | bytes 2752548 | tf_op jit(solution)/shard_map/pallas_call | solution.py:215
  208.4 6.5 %shard_map.292 = (f32[768,2304]{1,0:T(8,128)}, f32[768,768]{1,0:T(8,128)}, f32[192,576]{1,0:T(8,128)}, f32[192,192]{1,0:T(8,128)}, f32[4,768]{1,0:T(4,128)}, /*index=5*/f32[4,192]{1,0:T(4,128)}) custom-call(s32[9]{0:T(128)S(1)} %copy-done, bf16[448,768]{1,0:T(8,128)(2,1)S(1)} %pad_maximum_fusion.3.refs_0_, ...), custom_call_target="tpu_custom_call" | custom-call | flops 4400000000 | bytes 5111844 | tf_op jit(solution)/shard_map/pallas_call | solution.py:215
  (155 shorter events, 48.7 us)
Async XLA Ops:
  0.6 19.8 %collective-permute-start = (bf16[768,1536]{1,0:T(8,128)(2,1)}, bf16[768,1536]{1,0:T(8,128)(2,1)}, u32[]{:S(2)}, u32[]{:S(2)}) collective-permute-start(bf16[768,1536]{1,0:T(8,128)(2,1)} %refs_9_.1), channel_id=1, source_target_pairs={{0,1},{1,0},{2,3},{3,2},{4,5},{5,4},{6,7},{7,6},{8,9},{9,8},{10,11... | collective-permute-start | bytes 7077896 | tf_op jit(solution)/shard_map/ppermute | solution.py:534
  1.2 19.3 %collective-permute-start.1 = (bf16[1536,768]{1,0:T(8,128)(2,1)}, bf16[1536,768]{1,0:T(8,128)(2,1)}, u32[]{:S(2)}, u32[]{:S(2)}) collective-permute-start(bf16[1536,768]{1,0:T(8,128)(2,1)} %refs_4_.3), channel_id=1, source_target_pairs={{0,1},{1,0},{2,3},{3,2},{4,5},{5,4},{6,7},{7,6},{8,9},{9,8},{10,11... | collective-permute-start | bytes 7077896 | tf_op jit(solution)/shard_map/ppermute | solution.py:534
  1.2 19.2 %collective-permute-start.2 = (bf16[192,384]{1,0:T(8,128)(2,1)}, bf16[192,384]{1,0:T(8,128)(2,1)S(1)}, u32[]{:S(2)}, u32[]{:S(2)}) collective-permute-start(bf16[192,384]{1,0:T(8,128)(2,1)} %refs_10_.1), channel_id=1, source_target_pairs={{0,1},{1,0},{2,3},{3,2},{4,5},{5,4},{6,7},{7,6},{8,9},{9,8},{10,11... | collective-permute-start | bytes 442376 | tf_op jit(solution)/shard_map/ppermute | solution.py:534
  1.7 18.8 %collective-permute-start.3 = (bf16[192,384]{1,0:T(8,128)(2,1)}, bf16[192,384]{1,0:T(8,128)(2,1)S(1)}, u32[]{:S(2)}, u32[]{:S(2)}) collective-permute-start(bf16[192,384]{1,0:T(8,128)(2,1)} %bitcast.20), channel_id=1, source_target_pairs={{0,1},{1,0},{2,3},{3,2},{4,5},{5,4},{6,7},{7,6},{8,9},{9,8},{10,11... | collective-permute-start | bytes 442376 | tf_op jit(solution)/shard_map/ppermute | solution.py:534
  47.6 26.7 %collective-permute-start.6 = (bf16[768,768]{1,0:T(8,128)(2,1)S(1)}, bf16[768,768]{1,0:T(8,128)(2,1)S(1)}, u32[]{:S(2)}, u32[]{:S(2)}) collective-permute-start(bf16[768,768]{1,0:T(8,128)(2,1)S(1)} %get-tuple-element.235), channel_id=1, source_target_pairs={{0,2},{1,5},{2,0},{3,7},{4,6},{5,1},{6,4},{7,3},{8,10},{9,13},{10,... | collective-permute-start | bytes 3538952 | tf_op jit(solution)/shard_map/ppermute | solution.py:534
  56.1 26.5 %collective-permute-start.8 = (bf16[896,768]{1,0:T(8,128)(2,1)S(1)}, bf16[896,768]{1,0:T(8,128)(2,1)S(1)}, u32[]{:S(2)}, u32[]{:S(2)}) collective-permute-start(bf16[896,768]{1,0:T(8,128)(2,1)S(1)} %get-tuple-element.233), channel_id=1, source_target_pairs={{0,4},{1,9},{2,6},{3,11},{4,0},{5,13},{6,2},{7,15},{8,12},{9,1},{1... | collective-permute-start | bytes 4128776 | tf_op jit(solution)/shard_map/ppermute | solution.py:534
  87.5 15.6 %collective-permute-start.9 = (bf16[1664,768]{1,0:T(8,128)(2,1)S(1)}, bf16[1664,768]{1,0:T(8,128)(2,1)S(1)}, u32[]{:S(2)}, u32[]{:S(2)}) collective-permute-start(bf16[1664,768]{1,0:T(8,128)(2,1)S(1)} %slice.169), channel_id=1, source_target_pairs={{0,1},{1,0},{2,3},{3,2},{4,5},{5,4},{6,7},{7,6},{8,9},{9,8},{10,11... | collective-permute-start | bytes 7667720 | tf_op jit(solution)/shard_map/ppermute | solution.py:534
  87.6 14.2 %collective-permute-start.10 = (bf16[448,768]{1,0:T(8,128)(2,1)S(1)}, bf16[448,768]{1,0:T(8,128)(2,1)S(1)}, u32[]{:S(2)}, u32[]{:S(2)}) collective-permute-start(bf16[448,768]{1,0:T(8,128)(2,1)S(1)} %get-tuple-element.237), channel_id=1, source_target_pairs={{0,8},{1,3},{2,10},{3,1},{4,12},{5,7},{6,14},{7,5},{8,0},{9,11},{1... | collective-permute-start | bytes 2064392 | tf_op jit(solution)/shard_map/ppermute | solution.py:534
  103.2 16.4 %collective-permute-start.13 = (bf16[384,768]{1,0:T(8,128)(2,1)S(1)}, bf16[384,768]{1,0:T(8,128)(2,1)S(1)}, u32[]{:S(2)}, u32[]{:S(2)}) collective-permute-start(bf16[384,768]{1,0:T(8,128)(2,1)S(1)} %get-tuple-element.228), channel_id=1, source_target_pairs={{0,2},{1,5},{2,0},{3,7},{4,6},{5,1},{6,4},{7,3},{8,10},{9,13},{10,... | collective-permute-start | bytes 1769480 | tf_op jit(solution)/shard_map/ppermute | solution.py:534
  104.3 22.5 %collective-permute-start.12 = (bf16[448,768]{1,0:T(8,128)(2,1)S(1)}, bf16[448,768]{1,0:T(8,128)(2,1)S(1)}, u32[]{:S(2)}, u32[]{:S(2)}) collective-permute-start(bf16[448,768]{1,0:T(8,128)(2,1)S(1)} %get-tuple-element.230), channel_id=1, source_target_pairs={{0,2},{1,9},{2,0},{3,11},{4,6},{5,13},{6,4},{7,15},{8,10},{9,1},{1... | collective-permute-start | bytes 2064392 | tf_op jit(solution)/shard_map/ppermute | solution.py:534
  105.5 14.0 %collective-permute-start.14 = (bf16[192,768]{1,0:T(8,128)(2,1)S(1)}, bf16[192,768]{1,0:T(8,128)(2,1)S(1)}, u32[]{:S(2)}, u32[]{:S(2)}) collective-permute-start(bf16[192,768]{1,0:T(8,128)(2,1)S(1)} %fusion.1), channel_id=1, source_target_pairs={{0,16},{1,17},{2,18},{3,19},{4,20},{5,21},{6,22},{7,23},{8,24},{9,... | collective-permute-start | bytes 884744 | tf_op jit(solution)/shard_map/ppermute | solution.py:534
  120.8 18.6 %collective-permute-start.17 = (bf16[192,768]{1,0:T(8,128)(2,1)S(1)}, bf16[192,768]{1,0:T(8,128)(2,1)S(1)}, u32[]{:S(2)}, u32[]{:S(2)}) collective-permute-start(bf16[192,768]{1,0:T(8,128)(2,1)S(1)} %add.160), channel_id=1, source_target_pairs={{0,4},{1,9},{2,6},{3,11},{4,0},{5,13},{6,2},{7,15},{8,12},{9,1},{1... | collective-permute-start | bytes 884744 | tf_op jit(solution)/shard_map/ppermute | solution.py:534
  121.8 16.8 %collective-permute-start.18 = (bf16[224,768]{1,0:T(8,128)(2,1)S(1)}, bf16[224,768]{1,0:T(8,128)(2,1)S(1)}, u32[]{:S(2)}, u32[]{:S(2)}) collective-permute-start(bf16[224,768]{1,0:T(8,128)(2,1)S(1)} %fusion), channel_id=1, source_target_pairs={{0,16},{1,17},{2,18},{3,19},{4,20},{5,21},{6,22},{7,23},{8,24},{9,... | collective-permute-start | bytes 1032200 | tf_op jit(solution)/shard_map/ppermute | solution.py:534
  126.8 12.8 %collective-permute-start.16 = (bf16[224,768]{1,0:T(8,128)(2,1)S(1)}, bf16[224,768]{1,0:T(8,128)(2,1)S(1)}, u32[]{:S(2)}, u32[]{:S(2)}) collective-permute-start(bf16[224,768]{1,0:T(8,128)(2,1)S(1)} %get-tuple-element.240), channel_id=1, source_target_pairs={{0,8},{1,3},{2,10},{3,1},{4,12},{5,7},{6,14},{7,5},{8,0},{9,11},{1... | collective-permute-start | bytes 1032200 | tf_op jit(solution)/shard_map/ppermute | solution.py:534
  126.9 14.2 %collective-permute-start.22 = (bf16[96,768]{1,0:T(8,128)(2,1)S(1)}, bf16[96,768]{1,0:T(8,128)(2,1)S(1)}, u32[]{:S(2)}, u32[]{:S(2)}) collective-permute-start(bf16[96,768]{1,0:T(8,128)(2,1)S(1)} %slice_add_fusion.23), channel_id=1, source_target_pairs={{0,8},{1,9},{2,10},{3,11},{4,12},{5,13},{6,14},{7,15},{8,0},{9,1},... | collective-permute-start | bytes 442376 | tf_op jit(solution)/shard_map/ppermute | solution.py:534
  149.9 27.5 %collective-permute-start.31 = (bf16[768,768]{1,0:T(8,128)(2,1)S(1)}, bf16[768,768]{1,0:T(8,128)(2,1)S(1)}, u32[]{:S(2)}, u32[]{:S(2)}) collective-permute-start(bf16[768,768]{1,0:T(8,128)(2,1)S(1)} %pad_maximum_fusion.1.refs_0_), channel_id=1, source_target_pairs={{0,2},{1,5},{2,0},{3,7},{4,6},{5,1},{6,4},{7,3},{8,10},{9,13},{10,... | collective-permute-start | bytes 3538952 | tf_op jit(solution)/shard_map/ppermute | solution.py:534
  150.9 22.7 %collective-permute-start.27 = (bf16[448,768]{1,0:T(8,128)(2,1)S(1)}, bf16[448,768]{1,0:T(8,128)(2,1)S(1)}, u32[]{:S(2)}, u32[]{:S(2)}) collective-permute-start(bf16[448,768]{1,0:T(8,128)(2,1)S(1)} %pad_maximum_fusion.2), channel_id=1, source_target_pairs={{0,8},{1,3},{2,10},{3,1},{4,12},{5,7},{6,14},{7,5},{8,0},{9,11},{1... | collective-permute-start | bytes 2064392 | tf_op jit(solution)/shard_map/ppermute | solution.py:534
  150.9 15.0 %collective-permute-start.24 = (bf16[96,768]{1,0:T(8,128)(2,1)S(1)}, bf16[96,768]{1,0:T(8,128)(2,1)S(1)}, u32[]{:S(2)}, u32[]{:S(2)}) collective-permute-start(bf16[96,768]{1,0:T(8,128)(2,1)S(1)} %fusion.3), channel_id=1, source_target_pairs={{0,16},{1,17},{2,18},{3,19},{4,20},{5,21},{6,22},{7,23},{8,24},{9,... | collective-permute-start | bytes 442376 | tf_op jit(solution)/shard_map/ppermute | solution.py:534
  152.8 14.9 %collective-permute-start.23 = (bf16[112,768]{1,0:T(8,128)(2,1)S(1)}, bf16[112,768]{1,0:T(8,128)(2,1)S(1)}, u32[]{:S(2)}, u32[]{:S(2)}) collective-permute-start(bf16[112,768]{1,0:T(8,128)(2,1)S(1)} %fusion.2), channel_id=1, source_target_pairs={{0,16},{1,17},{2,18},{3,19},{4,20},{5,21},{6,22},{7,23},{8,24},{9,... | collective-permute-start | bytes 516104 | tf_op jit(solution)/shard_map/ppermute | solution.py:534
  173.7 30.1 %collective-permute-start.38 = (bf16[896,768]{1,0:T(8,128)(2,1)S(1)}, bf16[896,768]{1,0:T(8,128)(2,1)S(1)}, u32[]{:S(2)}, u32[]{:S(2)}) collective-permute-start(bf16[896,768]{1,0:T(8,128)(2,1)S(1)} %pad_maximum_fusion.refs_0_), channel_id=1, source_target_pairs={{0,4},{1,9},{2,6},{3,11},{4,0},{5,13},{6,2},{7,15},{8,12},{9,1},{1... | collective-permute-start | bytes 4128776 | tf_op jit(solution)/shard_map/ppermute | solution.py:534
  174.7 11.1 %collective-permute-start.29 = (bf16[224,768]{1,0:T(8,128)(2,1)S(1)}, bf16[224,768]{1,0:T(8,128)(2,1)S(1)}, u32[]{:S(2)}, u32[]{:S(2)}) collective-permute-start(bf16[224,768]{1,0:T(8,128)(2,1)S(1)} %pad_maximum_fusion.6), channel_id=1, source_target_pairs={{0,8},{1,3},{2,10},{3,1},{4,12},{5,7},{6,14},{7,5},{8,0},{9,11},{1... | collective-permute-start | bytes 1032200 | tf_op jit(solution)/shard_map/ppermute | solution.py:534
  185.8 17.4 %collective-permute-start.32 = (bf16[448,768]{1,0:T(8,128)(2,1)S(1)}, bf16[448,768]{1,0:T(8,128)(2,1)S(1)}, u32[]{:S(2)}, u32[]{:S(2)}) collective-permute-start(bf16[448,768]{1,0:T(8,128)(2,1)S(1)} %pad_maximum_fusion.3.refs_0_), channel_id=1, source_target_pairs={{0,2},{1,9},{2,0},{3,11},{4,6},{5,13},{6,4},{7,15},{8,10},{9,1},{1... | collective-permute-start | bytes 2064392 | tf_op jit(solution)/shard_map/ppermute | solution.py:534
  187.4 15.9 %collective-permute-start.33 = (bf16[384,768]{1,0:T(8,128)(2,1)S(1)}, bf16[384,768]{1,0:T(8,128)(2,1)}, u32[]{:S(2)}, u32[]{:S(2)}) collective-permute-start(bf16[384,768]{1,0:T(8,128)(2,1)S(1)} %pad_maximum_fusion.5.refs_2_), channel_id=1, source_target_pairs={{0,2},{1,5},{2,0},{3,7},{4,6},{5,1},{6,4},{7,3},{8,10},{9,13},{10,... | collective-permute-start | bytes 1769480 | tf_op jit(solution)/shard_map/ppermute | solution.py:534
  187.9 20.4 %collective-permute-start.34 = (bf16[448,768]{1,0:T(8,128)(2,1)S(1)}, bf16[448,768]{1,0:T(8,128)(2,1)S(1)}, u32[]{:S(2)}, u32[]{:S(2)}) collective-permute-start(bf16[448,768]{1,0:T(8,128)(2,1)S(1)} %pad_maximum_fusion.3.refs_0_), channel_id=1, source_target_pairs={{0,1},{1,0},{2,3},{3,2},{4,5},{5,4},{6,7},{7,6},{8,9},{9,8},{10,11... | collective-permute-start | bytes 2064392 | tf_op jit(solution)/shard_map/ppermute | solution.py:534
  (43 other events, 286.6 us)

commit v3 on v2

--- a/solution.py
+++ b/solution.py
@@ -67,9 +67,9 @@
 PLANS = (FIELDS_DOWN, FIELDS_UP, FIELDS_HALF)
 HALF_ROWS = {"query": 384, "key": 384, "value": 384, "mix": 384, "low": 128}
 EVENTS = (
-    "B2", "D.core", "B3", "U.core", "turn", "p0", "p1", "D0.0", "p2", "U0.0", "D0.1", "close", "in", "D0.2",
-    "U0.1", "A.core", "U0.2", "D0.3", "A1.0", "A0.0", "A1.1", "U0.3", "D0.4", "A0.1", "A1.2", "U0.4", "A0.2",
-    "D0.5", "A1.3", "A0.3", "A1.4", "U0.5", "A0.4", "D0.6", "oD", "A1.5", "A0.5", "A1.6", "A0.6", "U0.6",
+    "B2", "D.core", "B3", "U.core", "turn", "p0", "p1", "D0.0", "U0.0", "close", "in", "D0.1", "A.core",
+    "U0.1", "D0.2", "U0.2", "A0.0", "A1.0", "D0.3", "A1.1", "A0.1", "U0.3", "A1.2", "A0.2", "U0.4", "D0.4",
+    "A1.3", "A0.3", "A1.4", "A0.4", "A1.5", "U0.5", "D0.5", "A0.5", "D0.6", "oD", "A1.6", "A0.6", "U0.6",
     "oU",
 )
 
@@ -98,7 +98,7 @@
     return jnp.stack(values)
 
 
-def place(out, sides, core, plan, field, value, start=0, shift=0, columns=slice(None)):
+def place(out, sides, core, plan, field, value, start=0, shift=0, skip=0):
     for number, base, leaf, fields in streams_of(plan):
         mask = sides[1 + 2 * number + core]
         inner = 0
@@ -107,17 +107,17 @@
                 for l in range(8):
                     at = first + l * n - start
                     if 0 <= at < value.shape[0]:
-                        row = shift + base + inner + leaf * jnp.bitwise_xor(mask, l)
+                        row = shift + base + inner + n * skip + leaf * jnp.bitwise_xor(mask, l)
                         row = pl.multiple_of(row, math.gcd(math.gcd(base + inner, leaf), 16))
-                        out[pl.ds(row, n), columns] = value[at:at + n, :]
+                        out[pl.ds(row, n), :] = value[at:at + n, :]
             inner += n
 
 
-def place_half(out, sides, field, value):
+def place_half(out, sides, field, value, skip=0):
     half = HALF_ROWS[field]
     for core in range(2):
         shift = jnp.bitwise_xor(sides[0], core) * rows_of(FIELDS_HALF)
-        place(out, sides, core, FIELDS_HALF, field, value[core * half:(core + 1) * half, :], 0, shift)
+        place(out, sides, core, FIELDS_HALF, field, value[core * half:(core + 1) * half, :], 0, shift, skip)
 
 
 def fetch(pairs, sems):
@@ -155,9 +155,14 @@
         ).astype(BF16)
         qkv_l[:, j * 256 + width_l:(j + 1) * 256] = jnp.zeros((slots, 256 - width_l), BF16)
     copies[2].wait()
-    for j, c in enumerate(columns):
-        copies[3 + j].wait()
+
+    def project(j, carry):
+        c = pl.ds(pl.multiple_of(j * width_t, width_t), width_t)
+        pltpu.make_async_copy(joint_t_any.at[:, c], joint_t.at[:, c], sems.at[3 + j]).wait()
         qkv_t[:, c] = nn(text_ref[...], joint_t[:, c]).astype(BF16)
+        return carry
+
+    lax.fori_loop(0, 3, project, 0)
     lane = lax.broadcasted_iota(jnp.int32, (slots, 128), 1)
     dead = lax.broadcasted_iota(jnp.int32, (slots, slots), 1) >= count
 
@@ -168,9 +173,9 @@
         query_l, key_l, value_l = (qkv_l[:, spot(j * 256 + at_l)] for j in range(3))
         keys = jnp.concatenate([key_t, key_l], axis=1)
         values = jnp.concatenate([value_t, value_l], axis=1)
-        for side in range(2):
-            head = 2 * pair + side
-            mask_t, mask_l = lane_masks(head, lane)
+        masks = [lane_masks(2 * pair + side, lane) for side in range(2)]
+        logits = []
+        for mask_t, mask_l in masks:
             queries = jnp.concatenate(
                 [
                     jnp.where(mask_t, query_t * 0.125, 0),
@@ -178,17 +183,20 @@
                 ],
                 axis=1,
             ).astype(BF16)
-            logits = jnp.where(dead, NEG_FILL, nt(queries, keys))
-            top = jnp.max(logits, axis=1, keepdims=True)
-            raised = jnp.exp(logits - top)
+            logits.append(jnp.where(dead, NEG_FILL, nt(queries, keys)))
+        outs = []
+        for side in range(2):
+            top = jnp.max(logits[side], axis=1, keepdims=True)
+            raised = jnp.exp(logits[side] - top)
             mass = jnp.sum(raised, axis=1, keepdims=True)
-            stats[...] = jnp.where(lane == head, top + jnp.log(mass), stats[...])
-            out = nn(raised.astype(BF16), values) * (1.0 / mass)
-            if side == 0:
-                first = out[:, :128]
-            else:
-                mixed_t[:, spot(pair * 128)] = jnp.where(mask_t, out[:, :128], first).astype(BF16)
-            mix_acc[:, spot(at_l)] = mix_acc[:, spot(at_l)] + jnp.where(mask_l, out[:, 128:], 0.0)
+            stats[...] = jnp.where(lane == 2 * pair + side, top + jnp.log(mass), stats[...])
+            outs.append(nn(raised.astype(BF16), values) * (1.0 / mass))
+        mixed_t[:, spot(pair * 128)] = jnp.where(masks[1][0], outs[1][:, :128], outs[0][:, :128]).astype(BF16)
+        mix_acc[:, spot(at_l)] = (
+            mix_acc[:, spot(at_l)]
+            + jnp.where(masks[0][1], outs[0][:, 128:], 0.0)
+            + jnp.where(masks[1][1], outs[1][:, 128:], 0.0)
+        )
         return carry
 
     lax.fori_loop(0, HEADS // 2, pair_step, 0)
@@ -210,7 +218,7 @@
 ANY_SPEC = pl.BlockSpec(memory_space=pltpu.HBM)
 
 
-def call(kernel, micros, outs, args, scratch=(), specs=None, aliases=None, limit=16, out_specs=None):
+def call(kernel, micros, outs, args, scratch=(), specs=None, aliases=None, limit=8, out_specs=None):
     moved = sum(math.prod(a.shape) * a.dtype.itemsize for a in args)
     return pl.pallas_call(
         kernel,
@@ -241,7 +249,7 @@
             pltpu.VMEM((s, 256), F32), pltpu.VMEM((wl, s), BF16), pltpu.SemaphoreType.DMA((8,)),
         ],
         [SMEM_SPEC] * 2 + [ANY_SPEC] * 6,
-        limit=56,
+        limit=48,
     )
 
 
@@ -305,15 +313,24 @@
         + [((2, wt), F32, True), ((2, wl), F32, True), ((ht, wt), BF16, False)],
         (sides, normed_t, normed_l, norms_t, norms_l, cot_t, cot_l) + tuple(weights),
         specs=[SMEM_SPEC] + [VMEM_SPEC] * 14,
-        limit=16,
+        limit=13,
     )
 
 
 def down_kernel(sides, far, act, dfeed, out):
     core = jnp.bitwise_xor(sides[0], far)
-    step = 768
-    for start in range(0, act.shape[1], step):
-        place(out, sides, core, FIELDS_DOWN, "down", tn(act[:, start:start + step], dfeed[...]).astype(BF16), start)
+    (number, _, leaf, _), = streams_of(FIELDS_DOWN)
+    mask = sides[1 + 2 * number + core]
+
+    def chunk(c, carry):
+        at = pl.ds(pl.multiple_of(c * 4 * leaf, 4 * leaf), 4 * leaf)
+        value = tn(act[:, at], dfeed[...]).astype(BF16)
+        for i in range(4):
+            row = leaf * jnp.bitwise_xor(mask, 4 * c + i)
+            out[pl.ds(pl.multiple_of(row, 16), leaf), :] = value[i * leaf:(i + 1) * leaf, :]
+        return carry
+
+    lax.fori_loop(0, 2, chunk, 0)
 
 
 def up_body(
@@ -323,11 +340,20 @@
     wt = low_t.shape[1]
     wl = low_l.shape[1]
     core = jnp.bitwise_xor(sides[0], far)
-    for start in range(0, down_t.shape[0], wt):
-        at = slice(start, start + wt)
+    (number, _, leaf, fields), = streams_of(FIELDS_UP)
+    mask = sides[1 + 2 * number + core]
+    part = fields[0][2]
+
+    def chunk(c, carry):
+        at = pl.ds(pl.multiple_of(c * wt, wt), wt)
         dhid[:, at] = (nt(dfeed_t[...], down_t[at, :]) * slope_t[:, at].astype(F32)).astype(BF16)
-        field = "right" if start else "left"
-        place(grads, sides, core, FIELDS_UP, field, tn(low_t[...], dhid[:, at]).astype(BF16))
+        value = tn(low_t[...], dhid[:, at]).astype(BF16)
+        for l in range(8):
+            row = leaf * jnp.bitwise_xor(mask, l) + part * c
+            grads[pl.ds(pl.multiple_of(row, 16), part), :] = value[l * part:(l + 1) * part, :]
+        return carry
+
+    lax.fori_loop(0, down_t.shape[0] // wt, chunk, 0)
     dfirst_t[...] = prev_t[...] + nt(dhid[...], up_t[...])
     hl = down_l.shape[1]
     dhidden = (nn(dfeed_l[...], down_l[...]) * slope_l[...].astype(F32)).astype(BF16)
@@ -488,8 +514,13 @@
 ):
     wt = text_ref.shape[2]
     wl = layout_ref.shape[1]
-    for j, field in enumerate(("query", "key", "value")):
-        place_half(grads, sides, field, tn(text_ref[0], djoint_t[:, j * wt:(j + 1) * wt]).astype(BF16))
+    def block(j, carry):
+        value = tn(text_ref[0], djoint_t[:, pl.ds(pl.multiple_of(j * wt, wt), wt)]).astype(BF16)
+        place_half(grads, sides, "query", value, j)
+        return carry
+
+    lax.fori_loop(0, 2, block, 0)
+    place_half(grads, sides, "value", tn(text_ref[0], djoint_t[:, 2 * wt:]).astype(BF16))
     for j in range(3):
         djoint_l[:, j * wl:(j + 1) * wl] = acc_l[:, j * 256:j * 256 + wl].astype(BF16)
     low = jnp.concatenate([nn(layout_ref[0], djoint_l[...]).astype(BF16), mix_low[...]], axis=1)
@@ -571,13 +602,14 @@
         return self.launch(phase + 1, self.keep)
 
 
-def unplace(parts, sides, core, plan, field, out, half=0):
+def unplace(parts, sides, core, plan, field, out, half=0, which=(0, 1)):
+    runs = []
     for i, (number, _, leaf, fields) in enumerate(streams_of(plan)):
         mask = sides[1 + 2 * number + core]
         inner = 0
         for name, first, n in fields:
             if name == field:
-                for side in range(2):
+                for side in which:
                     part = parts[2 * i + side]
 
                     def copy(r, carry, first=first, n=n, inner=inner, part=part, mask=mask, side=side, leaf=leaf):
@@ -587,7 +619,10 @@
                         return carry
 
                     lax.fori_loop(0, 4, copy, 0)
+                    start = core * half + first + 4 * n * jnp.bitwise_xor(mask // 4, side)
+                    runs.append(pl.ds(pl.multiple_of(start, 4 * n), 4 * n))
             inner += n
+    return runs
 
 
 def stage(refs, sems, fill):
@@ -618,31 +653,77 @@
     )
     fill("low", low)
     up_l[...] = low[:wl, :hl]
-    down_l[:wl, :] = low[:wl, hl:hl + wl]
-    down_l[wl:, :] = low[:wl, hl + wl:]
+    down_l[:, :wl] = low[:wl, hl:hl + wl].T
+    down_l[:, wl:] = low[:wl, hl + wl:].T
     for copy in flying:
         copy.wait()
 
 
+def send_half(own, other, sides, outs, which, sems):
+    flying = []
+    for field, out, columns, buffer in outs:
+        for parts, core in ((own, sides[0]), (other, 1 - sides[0])):
+            for run in unplace(parts, sides, core, FIELDS_HALF, field, buffer, HALF_ROWS[field], (which,)):
+                copy = pltpu.make_async_copy(buffer.at[run, :], out.at[run, columns], sems.at[len(flying)])
+                copy.start()
+                flying.append(copy)
+    return flying
+
+
+def half_outs(joint_t, mix_t, buffers):
+    wt = mix_t.shape[0]
+    names = ("query", "key", "value", "mix")
+    places = [(joint_t, slice(j * wt, (j + 1) * wt)) for j in range(3)] + [(mix_t, slice(0, wt))]
+    return [(name, *there, buffer) for name, there, buffer in zip(names, places, buffers)]
+
+
+def first_half_kernel(sides, *refs):
+    count = len(FIELDS_HALF)
+    spread = lambda refs: [ref for ref in refs for _ in range(2)]
+    own, other = spread(refs[:count]), spread(refs[count:2 * count])
+    joint_t, mix_t, mark, *buffers, sems = refs[2 * count:]
+    mark[...] = jnp.zeros_like(mark)
+    for copy in send_half(own, other, sides, half_outs(joint_t, mix_t, buffers), 0, sems):
+        copy.wait()
+
+
 def open_half_kernel(sides, *refs):
     count = 2 * len(FIELDS_HALF)
-    own, other, refs = refs[:count], refs[count:2 * count], refs[2 * count:]
+    own, other, refs = refs[:count], refs[count:2 * count], refs[2 * count + 2:]
     joint_t, mix_t, joint_l, mix_l, norm_t, norm_l, *buffers, low, sems = refs
-    wt, wl = mix_t.shape[0], mix_l.shape[0]
-
-    def fill(field, out):
-        for parts, core in ((own, sides[0]), (other, 1 - sides[0])):
-            unplace(parts, sides, core, FIELDS_HALF, field, out, HALF_ROWS[field])
-
-    outs = [(field, joint_t, slice(j * wt, (j + 1) * wt)) for j, field in enumerate(("query", "key", "value"))]
-    flying = stage([(*o, b) for o, b in zip(outs + [("mix", mix_t, slice(0, wt))], buffers)], sems, fill)
-    fill("low", low)
+    wl = mix_l.shape[0]
+    flying = send_half(own, other, sides, half_outs(joint_t, mix_t, buffers), 1, sems)
+    for parts, core in ((own, sides[0]), (other, 1 - sides[0])):
+        unplace(parts, sides, core, FIELDS_HALF, "low", low, HALF_ROWS["low"])
     joint_l[...] = low[:wl, :3 * wl]
     mix_l[...] = low[:wl, 3 * wl:]
     norm_t[...] = low[wl:wl + 4, :]
     norm_l[...] = low[wl + 16:wl + 20, :wl]
     for copy in flying:
         copy.wait()
+
+
+def open_half(sides, own_parts, to_far, wt, wl):
+    buffers = [pltpu.VMEM((wt, wt), F32)] * 4
+    sems = pltpu.SemaphoreType.DMA((4 * len(own_parts),))
+    big = [((wt, 3 * wt), F32, False), ((wt, wt), F32, False)]
+    keeps, gots = own_parts[0::2], own_parts[1::2]
+    far_keeps = to_far(keeps, 0)
+    *begun, mark = call(
+        first_half_kernel, 3, big + [((8, 128), F32, False)], (sides, *keeps, *far_keeps), buffers + [sems],
+        [SMEM_SPEC] + [VMEM_SPEC] * 2 * len(keeps), limit=24, out_specs=[ANY_SPEC] * 2 + [VMEM_SPEC],
+    )
+    gots = [tie([got], mark)[0] for got in gots]
+    both = lambda one, two: [part for pair in zip(one, two) for part in pair]
+    args = (sides, *both(keeps, gots), *both(far_keeps, to_far(gots, 1)), *begun)
+    return call(
+        open_half_kernel, 3,
+        big + [(shape, F32, False) for shape in ((wl, 3 * wl), (wl, wl), (4, wt), (4, wl))],
+        args, buffers + [pltpu.VMEM((256, wt), F32), sems],
+        [SMEM_SPEC] + [VMEM_SPEC] * (len(args) - 3) + [ANY_SPEC] * 2,
+        aliases={len(args) - 2: 0, len(args) - 1: 1}, limit=24,
+        out_specs=[ANY_SPEC] * 2 + [VMEM_SPEC] * 4,
+    )
 
 
 def open_up(kernel, micros, direct, outs, buffers, sides, token, parts):
@@ -755,18 +836,18 @@
         return [part for i in range(len(plan)) for part in streams["%s%d" % (name, i)].keep]
 
     def open_down():
-        run["down"] = open_up(open_down_kernel, 3, 1, [(ht, wt)], [(ht, wt)], sides, run["token"], parts_of("D", FIELDS_DOWN))
-        run["token"] = list(run["down"])
+        run["down"], = open_up(open_down_kernel, 3, 1, [(ht, wt)], [(ht, wt)], sides, run["token"], parts_of("D", FIELDS_DOWN))
+        run["token"] = [run["down"]]
 
     def open_upper():
         run["up"] = open_up(
-            open_up_kernel, 3, 1, [(wt, ht), (wl, hl), (hl, wl)], [(wt, wt)] * 2 + [(256, wt)], sides, run["token"], parts_of("U", FIELDS_UP)
-        )
-        run["token"] = list(run["up"])
+            open_up_kernel, 3, 1, [(wt, ht), (wl, hl), (wl, hl)], [(wt, wt)] * 2 + [(256, wt)], sides, run["token"], parts_of("U", FIELDS_UP)
+        )
+        run["token"] = [run["up"][1]]
 
     kernels = {
-        "B2": far_grads, "B3": own_grads, "turn": turn_back, "p0": lambda: pair_grads(0, 2),
-        "p1": lambda: pair_grads(2, 4), "p2": lambda: pair_grads(4, 6), "close": close_up, "in": inputs_up,
+        "B2": far_grads, "B3": own_grads, "turn": turn_back, "p0": lambda: pair_grads(0, 3),
+        "p1": lambda: pair_grads(3, 6), "close": close_up, "in": inputs_up,
     }
     opens = {"oD": open_down, "oU": open_upper}
     owns = {"D": ("down_own", FIELDS_DOWN), "U": ("up_own", FIELDS_UP), "A": ("half_own", FIELDS_HALF)}
@@ -791,12 +872,11 @@
 
     if halves:
         own_parts = parts_of("A", FIELDS_HALF)
-        far_parts = [swap(part, -1, many) for part in own_parts]
-        down_grad_t, = run["down"]
+        down_grad_t = run["down"]
         up_grad_t, up_grad_l, down_grad_l = run["up"]
-        joint_t, mix_t, joint_l, mix_l, norm_t, norm_l = open_up(
-            open_half_kernel, 4, 2, [(wt, 3 * wt), (wt, wt), (wl, 3 * wl), (wl, wl), (4, wt), (4, wl)],
-            [(wt, wt)] * 4 + [(256, wt)], sides, [], own_parts + far_parts,
+        down_grad_l = down_grad_l.T
+        joint_t, mix_t, joint_l, mix_l, norm_t, norm_l = open_half(
+            sides, own_parts, lambda parts, side: [swap(part, -1, many) for part in parts], wt, wl
         )
     else:
         def parts(packed, plan, shift=0):
@@ -812,7 +892,7 @@
         ]
         ups = [
             open_up(
-                open_up_kernel, 3, 1, [(wt, hidden), (wl, wide), (wide, wl)], [(wt, wt)] * 2 + [(256, wt)], sides, [],
+                open_up_kernel, 3, 1, [(wt, hidden), (wl, wide), (wl, wide)], [(wt, wt)] * 2 + [(256, wt)], sides, [],
                 parts(p, FIELDS_UP),
             )
             for p in (up_own, up_far)
@@ -821,18 +901,17 @@
             jnp.concatenate([ups[0][0], ups[1][0]], axis=1),
             jnp.concatenate(downs, axis=0),
             jnp.concatenate([ups[0][1], ups[1][1]], axis=1),
-            jnp.concatenate([ups[0][2], ups[1][2]], axis=0),
+            jnp.concatenate([ups[0][2].T, ups[1][2].T], axis=0),
         ]
         up_grad_t, down_grad_t, up_grad_l, down_grad_l = (
             lax.psum(lax.psum_scatter(g, "tensor", scatter_dimension=axis, tiled=True), "dp")
             for g, axis in zip(joined, (1, 0, 1, 0))
         )
         rows = grads.shape[0] // 2
-        joint_t, mix_t, joint_l, mix_l, norm_t, norm_l = lax.psum(open_up(
-            open_half_kernel, 4, 2, [(wt, 3 * wt), (wt, wt), (wl, 3 * wl), (wl, wl), (4, wt), (4, wl)],
-            [(wt, wt)] * 4 + [(256, wt)], sides, [],
-            parts(grads, FIELDS_HALF) + parts(grads, FIELDS_HALF, rows),
-        ), AXES)
+        far_parts = parts(grads, FIELDS_HALF, rows)
+        joint_t, mix_t, joint_l, mix_l, norm_t, norm_l = lax.psum(
+            open_half(sides, parts(grads, FIELDS_HALF), lambda parts, side: far_parts[side::2], wt, wl), AXES
+        )
     return (
         result_t[None],
         result_l.T[None],

time: 219 us -> 204 us (0.932); the launches traced: 215 us -> 203 us
  waiting for transfers between devices: 83.8 us -> 76.3 us
  local copies, waits for them, and re-layouts: 9.19 us -> 2.71 us
  starting transfers between devices: 34.4 us -> 36.9 us
    ppermute x39, waiting for transfers between devices: 83.8 us -> 76.3 us  [swap(): return lax.ppermute(value, AXES, pairs)]
    unnamed x57 -> x36, local copies, waits for them, and re-layouts: 8.42 us -> 1.94 us
    ppermute x39, starting transfers between devices: 34.4 us -> 36.9 us  [swap(): return lax.ppermute(value, AXES, pairs)]
  transfers between devices with their start and end apart: 39 -> 39, of which waited for: 16 -> 17; matrix products, arithmetic and copies ran while one was open for 2% -> 2% of each run, Pallas kernels for 28% -> 31%
where the time goes in v3:
time: 204 us; the launch traced here: 203 us
  Pallas kernels  82 us (40%)
  waiting for transfers between devices  76.3 us (37%)
  starting transfers between devices  36.9 us (18%)
  other arithmetic  3.46 us (2%)
  local copies, waits for them, and re-layouts  2.71 us (1%)
    pallas_call x13, Pallas kernels, call(): pl.pallas_call(kernel, out_shape=[pltpu.VMEM(s, d) if kept else jax.Shape...  82 us
    ppermute x39, waiting for transfers between devices, swap(): return lax.ppermute(value, AXES, pairs)  76.3 us
    ppermute x39, starting transfers between devices, swap(): return lax.ppermute(value, AXES, pairs)  36.9 us
  transfers between devices with their start and end apart: 39, of which 17 were waited for; matrix products, arithmetic and copies ran while one was open for 2% of the time, Pallas kernels for 31%

profile of v3, /device:TPU:0, one launch (start us, length us, event | category | flops | bytes accessed | tf_op | source)
XLA Modules:
  0.0 203.3 jit_solution(4766568705252563447)
XLA Ops:
  3.1 13.3 %shard_map.272 = (bf16[512,2304]{1,0:T(8,128)(2,1)S(1)}, bf16[512,768]{1,0:T(8,128)(2,1)S(1)}, bf16[512,768]{1,0:T(8,128)(2,1)S(1)}, bf16[512,192]{1,0:T(8,128)(...) custom-call(s32[1]{0:T(128)S(6)} %copy.45.count_ref, s32[9]{0:T(128)} %stack.30.sides.refs_0_, ...), custom_call_target="tpu_custom_call" | custom-call | flops 13200000000 | bytes 5996584 | tf_op jit(solution)/shard_map/pallas_call | solution.py:223
  17.4 12.3 %shard_map.273 = (bf16[512,768]{1,0:T(8,128)(2,1)}, bf16[192,512]{1,0:T(8,128)(2,1)}, f32[512,768]{1,0:T(8,128)S(1)}, f32[512,192]{1,0:T(8,128)S(1)}, bf16[512,7...) custom-call(s32[9]{0:T(128)S(1)} %copy-done, ...), custom_call_target="tpu_custom_call" | custom-call | flops 17600000000 | bytes 12991524 | tf_op jit(solution)/shard_map/pallas_call | solution.py:223
  30.2 8.4 %shard_map.274 = (bf16[1536,768]{1,0:T(8,128)(2,1)S(1)}, bf16[1792,768]{1,0:T(8,128)(2,1)S(1)}, f32[512,768]{1,0:T(8,128)S(1)}, f32[512,192]{1,0:T(8,128)S(1)}) custom-call(s32[9]{0:T(128)S(1)} %copy-done, bf16[512,1536]{1,0:T(8,128)(2,1)S(1)} %get-tuple-element.126.refs_1_, bf16[512,768]{1,0:T(8,128)(2,1)S(1)} %get-tuple-element.140.refs_2_.refs_0_, ...), custom_call_target="tpu_custom_call" | custom-call | flops 8800000000 | bytes 12877860 | tf_op jit(solution)/shard_map/pallas_call | solution.py:223
  40.0 2.9 %collective-permute-start.7 = (bf16[768,768]{1,0:T(8,128)(2,1)}, bf16[768,768]{1,0:T(8,128)(2,1)S(1)}, u32[]{:S(2)}, u32[]{:S(2)}) collective-permute-start(bf16[768,768]{1,0:T(8,128)(2,1)} %get-tuple-element.225), channel_id=1, source_target_pairs={{0,2},{1,5},{2,0},{3,7},{4,6},{5,1},{6,4},{7,3},{8,10},{9,13},{10,... | collective-permute-start | bytes 3538952 | tf_op jit(solution)/shard_map/ppermute | solution.py:565
  42.9 5.4 %shard_map.275 = (bf16[1792,768]{1,0:T(8,128)(2,1)S(1)}, f32[512,768]{1,0:T(8,128)S(1)}, f32[512,192]{1,0:T(8,128)S(1)}) custom-call(s32[9]{0:T(128)S(1)} %copy-done, bf16[512,768]{1,0:T(8,128)(2,1)S(1)} %get-tuple-element.140.refs_2_.refs_0_, bf16[512,192]{1,0:T(8,128)(2,1)S(1)} %get-tuple-element.128.refs_3_.refs_1_, ...), custom_call_target="tpu_custom_call" | custom-call | flops 5500000256 | bytes 11304996 | tf_op jit(solution)/shard_map/pallas_call | solution.py:223
  50.4 2.9 %shard_map.276 = (bf16[3328,768]{1,0:T(8,128)(2,1)S(1)}, f32[512,768]{1,0:T(8,128)S(1)}, f32[512,192]{1,0:T(8,128)S(1)}, bf16[512,768]{1,0:T(8,128)(2,1)S(1)}, b...) custom-call(s32[9]{0:T(128)S(1)} %copy-done, ...), custom_call_target="tpu_custom_call" | custom-call | flops 4400000000 | bytes 6453796 | tf_op jit(solution)/shard_map/pallas_call | solution.py:223
  53.3 9.2 %shard_map.277 = (bf16[512,2304]{1,0:T(8,128)(2,1)S(1)}, f32[512,768]{1,0:T(8,128)S(1)}) custom-call(s32[2]{0:T(128)S(1)} %iota_multiply_fusion.span_ref, s32[1]{0:T(128)S(6)} %copy.45.count_ref, bf16[512,2304]{1,0:T(8,128)(2,1)S(1)} %get-tuple-element.120.qkv_t, bf16[512,768]{1,0:T(8,128)(2,1)S(1)} %copy-done.17, ...), custom_call_target="tpu_custom_call", output_to_operand_aliasing={{0}: (7, {}), {1}: (8, {})} | custom-call | flops 9900000256 | bytes 8388620 | tf_op jit(solution)/shard_map/pallas_call | solution.py:223
  62.6 9.4 %shard_map.278 = (bf16[512,2304]{1,0:T(8,128)(2,1)S(1)}, f32[512,768]{1,0:T(8,128)S(1)}) custom-call(s32[2]{0:T(128)S(1)} %copy-done.15, s32[1]{0:T(128)S(6)} %copy.45.count_ref, bf16[512,2304]{1,0:T(8,128)(2,1)S(1)} %get-tuple-element.120.qkv_t, bf16[512,768]{1,0:T(8,128)(2,1)S(1)} %copy-done.17, ...), custom_call_target="tpu_custom_call", output_to_operand_aliasing={{0}: (7, {}), {1}: (8, {})} | custom-call | flops 9900000256 | bytes 8388620 | tf_op jit(solution)/shard_map/pallas_call | solution.py:223
  73.3 3.2 %shard_map.279 = (bf16[3328,768]{1,0:T(8,128)(2,1)S(1)}, bf16[512,576]{1,0:T(8,128)(2,1)S(1)}) custom-call(s32[9]{0:T(128)S(1)} %copy-done, bf16[1,512,768]{2,1,0:T(8,128)(2,1)S(1)} %copy-done.6, bf16[1,192,512]{2,1,0:T(8,128)(2,1)S(1)} %bitcast.20, bf16[512,2304]{1,0:T(8,128)(2,1)S(1)} %get-tuple-element.161.djoint_t, ...), custom_call_target="tpu_custom_call", output_to_operand_aliasing={{0}: (7, {})} | custom-call | flops 3300000000 | bytes 10199076 | tf_op jit(solution)/shard_map/pallas_call | solution.py:223
  79.0 3.5 %shard_map.280 = (f32[512,768]{1,0:T(8,128)}, f32[192,512]{1,0:T(8,128)}) custom-call(bf16[512,2304]{1,0:T(8,128)(2,1)S(1)} %get-tuple-element.161.djoint_t, bf16[512,576]{1,0:T(8,128)(2,1)S(1)} %get-tuple-element.169.djoint_l, bf16[768,2304]{1,0:T(8,128)(2,1)S(1)} %copy-done.1, bf16[192,576]{1,0:T(8,128)(2,1)S(1)} %copy-done.7, ...), custom_call_target="tpu_custom_call" | custom-call | flops 3300000000 | bytes 8675328 | tf_op jit(solution)/shard_map/pallas_call | solution.py:223
  82.5 4.3 %collective-permute-done.9 = bf16[384,768]{1,0:T(8,128)(2,1)S(1)} collective-permute-done((bf16[384,768]{1,0:T(8,128)(2,1)S(1)}, bf16[384,768]{1,0:T(8,128)(2,1)S(1)}, u32[]{:S(2)}, u32[]{:S(2)}) %collective-permute-start.9) | collective-permute-done | bytes 589856 | tf_op jit(solution)/shard_map/ppermute | solution.py:565
  89.9 9.3 %collective-permute-done.11 = bf16[448,768]{1,0:T(8,128)(2,1)S(1)} collective-permute-done((bf16[448,768]{1,0:T(8,128)(2,1)S(1)}, bf16[448,768]{1,0:T(8,128)(2,1)S(1)}, u32[]{:S(2)}, u32[]{:S(2)}) %collective-permute-start.11) | collective-permute-done | bytes 688160 | tf_op jit(solution)/shard_map/ppermute | solution.py:565
  106.8 7.2 %collective-permute-done.15 = bf16[384,768]{1,0:T(8,128)(2,1)S(1)} collective-permute-done((bf16[384,768]{1,0:T(8,128)(2,1)S(1)}, bf16[384,768]{1,0:T(8,128)(2,1)S(1)}, u32[]{:S(2)}, u32[]{:S(2)}) %collective-permute-start.15) | collective-permute-done | bytes 589856 | tf_op jit(solution)/shard_map/ppermute | solution.py:565
  123.1 8.6 %collective-permute-done.14 = bf16[224,768]{1,0:T(8,128)(2,1)S(1)} collective-permute-done((bf16[224,768]{1,0:T(8,128)(2,1)S(1)}, bf16[224,768]{1,0:T(8,128)(2,1)S(1)}, u32[]{:S(2)}, u32[]{:S(2)}) %collective-permute-start.14) | collective-permute-done | bytes 344096 | tf_op jit(solution)/shard_map/ppermute | solution.py:565
  140.4 4.2 %collective-permute-done.22 = bf16[96,768]{1,0:T(8,128)(2,1)S(1)} collective-permute-done((bf16[96,768]{1,0:T(8,128)(2,1)S(1)}, bf16[96,768]{1,0:T(8,128)(2,1)S(1)}, u32[]{:S(2)}, u32[]{:S(2)}) %collective-permute-start.22) | collective-permute-done | bytes 147488 | tf_op jit(solution)/shard_map/ppermute | solution.py:565
  146.9 3.0 %collective-permute-done.26 = bf16[96,768]{1,0:T(8,128)(2,1)S(1)} collective-permute-done((bf16[96,768]{1,0:T(8,128)(2,1)S(1)}, bf16[96,768]{1,0:T(8,128)(2,1)S(1)}, u32[]{:S(2)}, u32[]{:S(2)}) %collective-permute-start.26) | collective-permute-done | bytes 147488 | tf_op jit(solution)/shard_map/ppermute | solution.py:565
  152.0 6.5 %collective-permute-done.25 = bf16[112,768]{1,0:T(8,128)(2,1)S(1)} collective-permute-done((bf16[112,768]{1,0:T(8,128)(2,1)S(1)}, bf16[112,768]{1,0:T(8,128)(2,1)S(1)}, u32[]{:S(2)}, u32[]{:S(2)}) %collective-permute-start.25) | collective-permute-done | bytes 172064 | tf_op jit(solution)/shard_map/ppermute | solution.py:565
  158.8 4.8 %collective-permute-done.28 = bf16[384,768]{1,0:T(8,128)(2,1)S(1)} collective-permute-done((bf16[384,768]{1,0:T(8,128)(2,1)S(1)}, bf16[384,768]{1,0:T(8,128)(2,1)S(1)}, u32[]{:S(2)}, u32[]{:S(2)}) %collective-permute-start.28) | collective-permute-done | bytes 589856 | tf_op jit(solution)/shard_map/ppermute | solution.py:565
  171.4 3.5 %shard_map.282 = (f32[768,2304]{1,0:T(8,128)}, f32[768,768]{1,0:T(8,128)}, f32[8,128]{1,0:T(8,128)}) custom-call(s32[9]{0:T(128)S(1)} %copy-done, bf16[448,768]{1,0:T(8,128)(2,1)S(1)} %pad_maximum_fusion.3.refs_0_, bf16[384,768]{1,0:T(8,128)(2,1)S(1)} %pad_maximum_fusion.5.refs_1_.refs_2_, bf16[448,768]{1,0:T(8,128)(2,1)S(1)} %collective-permute-done.34.refs_2_.refs_4_, ...), custom_call_target="tpu_custom_call" | custom-call | flops 3300000000 | bytes 2555940 | tf_op jit(solution)/shard_map/pallas_call | solution.py:223
  174.9 5.1 %collective-permute-done.33.refs_1_ = bf16[768,768]{1,0:T(8,128)(2,1)S(1)} collective-permute-done((bf16[768,768]{1,0:T(8,128)(2,1)S(1)}, bf16[768,768]{1,0:T(8,128)(2,1)S(1)}, u32[]{:S(2)}, u32[]{:S(2)}) %collective-permute-start.33) | collective-permute-done | bytes 1179680 | tf_op jit(solution)/shard_map/ppermute | solution.py:565
  180.0 3.1 %shard_map.281 = f32[1536,768]{1,0:T(8,128)} custom-call(s32[9]{0:T(128)S(1)} %copy-done, bf16[768,768]{1,0:T(8,128)(2,1)S(1)} %pad_maximum_fusion.1.refs_0_, bf16[768,768]{1,0:T(8,128)(2,1)S(1)} %collective-permute-done.33.refs_1_), custom_call_target="tpu_custom_call" | custom-call | flops 3300000000 | bytes 2359332 | tf_op jit(solution)/shard_map/pallas_call | solution.py:223
  183.1 10.6 %collective-permute-done.32.refs_3_ = bf16[384,768]{1,0:T(8,128)(2,1)S(1)} collective-permute-done((bf16[384,768]{1,0:T(8,128)(2,1)S(1)}, bf16[384,768]{1,0:T(8,128)(2,1)S(1)}, u32[]{:S(2)}, u32[]{:S(2)}) %collective-permute-start.32) | collective-permute-done | bytes 589856 | tf_op jit(solution)/shard_map/ppermute | solution.py:565
  195.6 3.8 %shard_map.284 = (f32[768,1536]{1,0:T(8,128)}, f32[192,384]{1,0:T(8,128)}, f32[192,384]{1,0:T(8,128)}) custom-call(s32[9]{0:T(128)S(1)} %copy-done, bf16[896,768]{1,0:T(8,128)(2,1)S(1)} %pad_maximum_fusion.refs_0_, bf16[896,768]{1,0:T(8,128)(2,1)S(1)} %collective-permute-done.38.refs_1_), custom_call_target="tpu_custom_call" | custom-call | flops 3300000000 | bytes 2752548 | tf_op jit(solution)/shard_map/pallas_call | solution.py:223
  199.4 3.8 %shard_map.283 = (f32[768,2304]{1,0:T(8,128)}, f32[768,768]{1,0:T(8,128)}, f32[192,576]{1,0:T(8,128)}, f32[192,192]{1,0:T(8,128)}, f32[4,768]{1,0:T(4,128)}, /*index=5*/f32[4,192]{1,0:T(4,128)}) custom-call(s32[9]{0:T(128)S(1)} %copy-done, bf16[448,768]{1,0:T(8,128)(2,1)S(1)} %pad_maximum_fusion.3.refs_0_, ...), custom_call_target="tpu_custom_call", output_to_operand_aliasing={{0}: (9, {}), {1}: (10, {})} | custom-call | flops 3300000000 | bytes 14549028 | tf_op jit(solution)/shard_map/pallas_call | solution.py:223
  (134 shorter events, 52.8 us)
Async XLA Ops:
  0.6 16.7 %collective-permute-start = (bf16[768,1536]{1,0:T(8,128)(2,1)}, bf16[768,1536]{1,0:T(8,128)(2,1)S(1)}, u32[]{:S(2)}, u32[]{:S(2)}) collective-permute-start(bf16[768,1536]{1,0:T(8,128)(2,1)} %refs_9_.1), channel_id=1, source_target_pairs={{0,1},{1,0},{2,3},{3,2},{4,5},{5,4},{6,7},{7,6},{8,9},{9,8},{10,11... | collective-permute-start | bytes 7077896 | tf_op jit(solution)/shard_map/ppermute | solution.py:565
  1.2 16.2 %collective-permute-start.1 = (bf16[1536,768]{1,0:T(8,128)(2,1)}, bf16[1536,768]{1,0:T(8,128)(2,1)}, u32[]{:S(2)}, u32[]{:S(2)}) collective-permute-start(bf16[1536,768]{1,0:T(8,128)(2,1)} %refs_4_.3), channel_id=1, source_target_pairs={{0,1},{1,0},{2,3},{3,2},{4,5},{5,4},{6,7},{7,6},{8,9},{9,8},{10,11... | collective-permute-start | bytes 7077896 | tf_op jit(solution)/shard_map/ppermute | solution.py:565
  1.2 16.1 %collective-permute-start.2 = (bf16[192,384]{1,0:T(8,128)(2,1)}, bf16[192,384]{1,0:T(8,128)(2,1)S(1)}, u32[]{:S(2)}, u32[]{:S(2)}) collective-permute-start(bf16[192,384]{1,0:T(8,128)(2,1)} %refs_10_.1), channel_id=1, source_target_pairs={{0,1},{1,0},{2,3},{3,2},{4,5},{5,4},{6,7},{7,6},{8,9},{9,8},{10,11... | collective-permute-start | bytes 442376 | tf_op jit(solution)/shard_map/ppermute | solution.py:565
  1.7 15.6 %collective-permute-start.3 = (bf16[192,384]{1,0:T(8,128)(2,1)}, bf16[192,384]{1,0:T(8,128)(2,1)S(1)}, u32[]{:S(2)}, u32[]{:S(2)}) collective-permute-start(bf16[192,384]{1,0:T(8,128)(2,1)} %bitcast.21), channel_id=1, source_target_pairs={{0,1},{1,0},{2,3},{3,2},{4,5},{5,4},{6,7},{7,6},{8,9},{9,8},{10,11... | collective-permute-start | bytes 442376 | tf_op jit(solution)/shard_map/ppermute | solution.py:565
  40.0 32.0 %collective-permute-start.7 = (bf16[768,768]{1,0:T(8,128)(2,1)}, bf16[768,768]{1,0:T(8,128)(2,1)S(1)}, u32[]{:S(2)}, u32[]{:S(2)}) collective-permute-start(bf16[768,768]{1,0:T(8,128)(2,1)} %get-tuple-element.225), channel_id=1, source_target_pairs={{0,2},{1,5},{2,0},{3,7},{4,6},{5,1},{6,4},{7,3},{8,10},{9,13},{10,... | collective-permute-start | bytes 3538952 | tf_op jit(solution)/shard_map/ppermute | solution.py:565
  48.8 23.3 %collective-permute-start.6 = (bf16[896,768]{1,0:T(8,128)(2,1)S(1)}, bf16[896,768]{1,0:T(8,128)(2,1)S(1)}, u32[]{:S(2)}, u32[]{:S(2)}) collective-permute-start(bf16[896,768]{1,0:T(8,128)(2,1)S(1)} %get-tuple-element.223), channel_id=1, source_target_pairs={{0,4},{1,9},{2,6},{3,11},{4,0},{5,13},{6,2},{7,15},{8,12},{9,1},{1... | collective-permute-start | bytes 4128776 | tf_op jit(solution)/shard_map/ppermute | solution.py:565
  76.8 11.2 %collective-permute-start.8 = (bf16[1664,768]{1,0:T(8,128)(2,1)S(1)}, bf16[1664,768]{1,0:T(8,128)(2,1)S(1)}, u32[]{:S(2)}, u32[]{:S(2)}) collective-permute-start(bf16[1664,768]{1,0:T(8,128)(2,1)S(1)} %slice.165), channel_id=1, source_target_pairs={{0,1},{1,0},{2,3},{3,2},{4,5},{5,4},{6,7},{7,6},{8,9},{9,8},{10,11... | collective-permute-start | bytes 7667720 | tf_op jit(solution)/shard_map/ppermute | solution.py:565
  76.9 9.9 %collective-permute-start.9 = (bf16[384,768]{1,0:T(8,128)(2,1)S(1)}, bf16[384,768]{1,0:T(8,128)(2,1)S(1)}, u32[]{:S(2)}, u32[]{:S(2)}) collective-permute-start(bf16[384,768]{1,0:T(8,128)(2,1)S(1)} %get-tuple-element.229), channel_id=1, source_target_pairs={{0,8},{1,3},{2,10},{3,1},{4,12},{5,7},{6,14},{7,5},{8,0},{9,11},{1... | collective-permute-start | bytes 1769480 | tf_op jit(solution)/shard_map/ppermute | solution.py:565
  78.5 20.7 %collective-permute-start.11 = (bf16[448,768]{1,0:T(8,128)(2,1)S(1)}, bf16[448,768]{1,0:T(8,128)(2,1)S(1)}, u32[]{:S(2)}, u32[]{:S(2)}) collective-permute-start(bf16[448,768]{1,0:T(8,128)(2,1)S(1)} %get-tuple-element.227), channel_id=1, source_target_pairs={{0,8},{1,3},{2,10},{3,1},{4,12},{5,7},{6,14},{7,5},{8,0},{9,11},{1... | collective-permute-start | bytes 2064392 | tf_op jit(solution)/shard_map/ppermute | solution.py:565
  86.9 14.5 %collective-permute-start.13 = (bf16[192,768]{1,0:T(8,128)(2,1)S(1)}, bf16[192,768]{1,0:T(8,128)(2,1)S(1)}, u32[]{:S(2)}, u32[]{:S(2)}) collective-permute-start(bf16[192,768]{1,0:T(8,128)(2,1)S(1)} %slice_add_fusion.19), channel_id=1, source_target_pairs={{0,4},{1,9},{2,6},{3,11},{4,0},{5,13},{6,2},{7,15},{8,12},{9,1},{1... | collective-permute-start | bytes 884744 | tf_op jit(solution)/shard_map/ppermute | solution.py:565
  88.2 18.5 %collective-permute-start.10 = (bf16[448,768]{1,0:T(8,128)(2,1)S(1)}, bf16[448,768]{1,0:T(8,128)(2,1)S(1)}, u32[]{:S(2)}, u32[]{:S(2)}) collective-permute-start(bf16[448,768]{1,0:T(8,128)(2,1)S(1)} %get-tuple-element.220), channel_id=1, source_target_pairs={{0,2},{1,9},{2,0},{3,11},{4,6},{5,13},{6,4},{7,15},{8,10},{9,1},{1... | collective-permute-start | bytes 2064392 | tf_op jit(solution)/shard_map/ppermute | solution.py:565
  100.4 13.6 %collective-permute-start.15 = (bf16[384,768]{1,0:T(8,128)(2,1)S(1)}, bf16[384,768]{1,0:T(8,128)(2,1)S(1)}, u32[]{:S(2)}, u32[]{:S(2)}) collective-permute-start(bf16[384,768]{1,0:T(8,128)(2,1)S(1)} %get-tuple-element.219), channel_id=1, source_target_pairs={{0,2},{1,5},{2,0},{3,7},{4,6},{5,1},{6,4},{7,3},{8,10},{9,13},{10,... | collective-permute-start | bytes 1769480 | tf_op jit(solution)/shard_map/ppermute | solution.py:565
  101.4 19.0 %collective-permute-start.17 = (bf16[192,768]{1,0:T(8,128)(2,1)S(1)}, bf16[192,768]{1,0:T(8,128)(2,1)S(1)}, u32[]{:S(2)}, u32[]{:S(2)}) collective-permute-start(bf16[192,768]{1,0:T(8,128)(2,1)S(1)} %fusion.1), channel_id=1, source_target_pairs={{0,16},{1,17},{2,18},{3,19},{4,20},{5,21},{6,22},{7,23},{8,24},{9,... | collective-permute-start | bytes 884744 | tf_op jit(solution)/shard_map/ppermute | solution.py:565
  115.2 16.6 %collective-permute-start.14 = (bf16[224,768]{1,0:T(8,128)(2,1)S(1)}, bf16[224,768]{1,0:T(8,128)(2,1)S(1)}, u32[]{:S(2)}, u32[]{:S(2)}) collective-permute-start(bf16[224,768]{1,0:T(8,128)(2,1)S(1)} %get-tuple-element.230), channel_id=1, source_target_pairs={{0,8},{1,3},{2,10},{3,1},{4,12},{5,7},{6,14},{7,5},{8,0},{9,11},{1... | collective-permute-start | bytes 1032200 | tf_op jit(solution)/shard_map/ppermute | solution.py:565
  117.1 15.8 %collective-permute-start.20 = (bf16[224,768]{1,0:T(8,128)(2,1)S(1)}, bf16[224,768]{1,0:T(8,128)(2,1)S(1)}, u32[]{:S(2)}, u32[]{:S(2)}) collective-permute-start(bf16[224,768]{1,0:T(8,128)(2,1)S(1)} %fusion), channel_id=1, source_target_pairs={{0,16},{1,17},{2,18},{3,19},{4,20},{5,21},{6,22},{7,23},{8,24},{9,... | collective-permute-start | bytes 1032200 | tf_op jit(solution)/shard_map/ppermute | solution.py:565
  120.5 19.8 %collective-permute-start.23 = (bf16[192,768]{1,0:T(8,128)(2,1)S(1)}, bf16[192,768]{1,0:T(8,128)(2,1)S(1)}, u32[]{:S(2)}, u32[]{:S(2)}) collective-permute-start(bf16[192,768]{1,0:T(8,128)(2,1)S(1)} %add.164), channel_id=1, source_target_pairs={{0,4},{1,9},{2,6},{3,11},{4,0},{5,13},{6,2},{7,15},{8,12},{9,1},{1... | collective-permute-start | bytes 884744 | tf_op jit(solution)/shard_map/ppermute | solution.py:565
  121.7 12.8 %collective-permute-start.19 = (bf16[96,768]{1,0:T(8,128)(2,1)S(1)}, bf16[96,768]{1,0:T(8,128)(2,1)S(1)}, u32[]{:S(2)}, u32[]{:S(2)}) collective-permute-start(bf16[96,768]{1,0:T(8,128)(2,1)S(1)} %slice_add_fusion.23), channel_id=1, source_target_pairs={{0,8},{1,9},{2,10},{3,11},{4,12},{5,13},{6,14},{7,15},{8,0},{9,1},... | collective-permute-start | bytes 442376 | tf_op jit(solution)/shard_map/ppermute | solution.py:565
  134.5 10.1 %collective-permute-start.22 = (bf16[96,768]{1,0:T(8,128)(2,1)S(1)}, bf16[96,768]{1,0:T(8,128)(2,1)S(1)}, u32[]{:S(2)}, u32[]{:S(2)}) collective-permute-start(bf16[96,768]{1,0:T(8,128)(2,1)S(1)} %fusion.3), channel_id=1, source_target_pairs={{0,16},{1,17},{2,18},{3,19},{4,20},{5,21},{6,22},{7,23},{8,24},{9,... | collective-permute-start | bytes 442376 | tf_op jit(solution)/shard_map/ppermute | solution.py:565
  144.8 14.0 %collective-permute-start.29 = (bf16[448,768]{1,0:T(8,128)(2,1)S(1)}, bf16[448,768]{1,0:T(8,128)(2,1)S(1)}, u32[]{:S(2)}, u32[]{:S(2)}) collective-permute-start(bf16[448,768]{1,0:T(8,128)(2,1)S(1)} %pad_maximum_fusion.2), channel_id=1, source_target_pairs={{0,8},{1,3},{2,10},{3,1},{4,12},{5,7},{6,14},{7,5},{8,0},{9,11},{1... | collective-permute-start | bytes 2064392 | tf_op jit(solution)/shard_map/ppermute | solution.py:565
  146.8 16.8 %collective-permute-start.28 = (bf16[384,768]{1,0:T(8,128)(2,1)S(1)}, bf16[384,768]{1,0:T(8,128)(2,1)S(1)}, u32[]{:S(2)}, u32[]{:S(2)}) collective-permute-start(bf16[384,768]{1,0:T(8,128)(2,1)S(1)} %pad_maximum_fusion.4), channel_id=1, source_target_pairs={{0,8},{1,3},{2,10},{3,1},{4,12},{5,7},{6,14},{7,5},{8,0},{9,11},{1... | collective-permute-start | bytes 1769480 | tf_op jit(solution)/shard_map/ppermute | solution.py:565
  163.7 16.3 %collective-permute-start.33 = (bf16[768,768]{1,0:T(8,128)(2,1)S(1)}, bf16[768,768]{1,0:T(8,128)(2,1)S(1)}, u32[]{:S(2)}, u32[]{:S(2)}) collective-permute-start(bf16[768,768]{1,0:T(8,128)(2,1)S(1)} %pad_maximum_fusion.1.refs_0_), channel_id=1, source_target_pairs={{0,2},{1,5},{2,0},{3,7},{4,6},{5,1},{6,4},{7,3},{8,10},{9,13},{10,... | collective-permute-start | bytes 3538952 | tf_op jit(solution)/shard_map/ppermute | solution.py:565
  167.9 27.6 %collective-permute-start.38 = (bf16[896,768]{1,0:T(8,128)(2,1)S(1)}, bf16[896,768]{1,0:T(8,128)(2,1)S(1)}, u32[]{:S(2)}, u32[]{:S(2)}) collective-permute-start(bf16[896,768]{1,0:T(8,128)(2,1)S(1)} %pad_maximum_fusion.refs_0_), channel_id=1, source_target_pairs={{0,4},{1,9},{2,6},{3,11},{4,0},{5,13},{6,2},{7,15},{8,12},{9,1},{1... | collective-permute-start | bytes 4128776 | tf_op jit(solution)/shard_map/ppermute | solution.py:565
  168.8 24.8 %collective-permute-start.31 = (bf16[448,768]{1,0:T(8,128)(2,1)S(1)}, bf16[448,768]{1,0:T(8,128)(2,1)S(1)}, u32[]{:S(2)}, u32[]{:S(2)}) collective-permute-start(bf16[448,768]{1,0:T(8,128)(2,1)S(1)} %pad_maximum_fusion.3.refs_0_), channel_id=1, source_target_pairs={{0,2},{1,9},{2,0},{3,11},{4,6},{5,13},{6,4},{7,15},{8,10},{9,1},{1... | collective-permute-start | bytes 2064392 | tf_op jit(solution)/shard_map/ppermute | solution.py:565
  170.4 23.3 %collective-permute-start.32 = (bf16[384,768]{1,0:T(8,128)(2,1)S(1)}, bf16[384,768]{1,0:T(8,128)(2,1)S(1)}, u32[]{:S(2)}, u32[]{:S(2)}) collective-permute-start(bf16[384,768]{1,0:T(8,128)(2,1)S(1)} %pad_maximum_fusion.5.refs_1_.refs_2_), channel_id=1, source_target_pairs={{0,2},{1,5},{2,0},{3,7},{4,6},{5,1},{6,4},{7,3},{8,10},{9,13},{10,... | collective-permute-start | bytes 1769480 | tf_op jit(solution)/shard_map/ppermute | solution.py:565
  (33 other events, 257.9 us)

commit v4 on v3

--- a/solution.py
+++ b/solution.py
@@ -625,16 +625,6 @@
     return runs
 
 
-def stage(refs, sems, fill):
-    flying = []
-    for i, (field, out, columns, buffer) in enumerate(refs):
-        fill(field, buffer)
-        copy = pltpu.make_async_copy(buffer, out.at[:, columns], sems.at[i])
-        copy.start()
-        flying.append(copy)
-    return flying
-
-
 def open_down_kernel(sides, *refs):
     parts, (out, buffer, sems) = refs[:-3], refs[-3:]
     unplace(parts, sides, sides[0], FIELDS_DOWN, "down", buffer)
@@ -648,9 +638,13 @@
     wt = up_t.shape[0]
     wl, hl = up_l.shape
     fill = functools.partial(unplace, parts, sides, sides[0], FIELDS_UP)
-    flying = stage(
-        [("left", up_t, slice(0, wt), left), ("right", up_t, slice(wt, 2 * wt), right)], sems, fill
-    )
+    flying = []
+    for side in range(2):
+        for field, columns, buffer in (("left", slice(0, wt), left), ("right", slice(wt, 2 * wt), right)):
+            run, = fill(field, buffer, which=(side,))
+            copy = pltpu.make_async_copy(buffer.at[run, :], up_t.at[run, columns], sems.at[len(flying)])
+            copy.start()
+            flying.append(copy)
     fill("low", low)
     up_l[...] = low[:wl, :hl]
     down_l[:, :wl] = low[:wl, hl:hl + wl].T

time: 204 us -> 203 us (level)
  no operation moved by 1% of the time
where the time goes in v4:
time: 203 us
  Pallas kernels  81.9 us (40%)
  waiting for transfers between devices  76.3 us (38%)
  starting transfers between devices  36.9 us (18%)
  other arithmetic  3.46 us (2%)
  local copies, waits for them, and re-layouts  2.71 us (1%)
    pallas_call x13, Pallas kernels, call(): pl.pallas_call(kernel, out_shape=[pltpu.VMEM(s, d) if kept else jax.Shape...  81.9 us
    ppermute x39, waiting for transfers between devices, swap(): return lax.ppermute(value, AXES, pairs)  76.3 us
    ppermute x39, starting transfers between devices, swap(): return lax.ppermute(value, AXES, pairs)  36.9 us
  transfers between devices with their start and end apart: 39, of which 17 were waited for; matrix products, arithmetic and copies ran while one was open for 2% of the time, Pallas kernels for 31%

profile of v4, /device:TPU:0, one launch (start us, length us, event | category | flops | bytes accessed | tf_op | source)
XLA Modules:
  0.0 203.2 jit_solution(5423602277412269897)
XLA Ops:
  3.1 13.3 %shard_map.272 = (bf16[512,2304]{1,0:T(8,128)(2,1)S(1)}, bf16[512,768]{1,0:T(8,128)(2,1)S(1)}, bf16[512,768]{1,0:T(8,128)(2,1)S(1)}, bf16[512,192]{1,0:T(8,128)(...) custom-call(s32[1]{0:T(128)S(6)} %copy.45.count_ref, s32[9]{0:T(128)} %stack.30.sides.refs_0_, ...), custom_call_target="tpu_custom_call" | custom-call | flops 13200000000 | bytes 5996584 | tf_op jit(solution)/shard_map/pallas_call | solution.py:223
  17.4 12.3 %shard_map.273 = (bf16[512,768]{1,0:T(8,128)(2,1)}, bf16[192,512]{1,0:T(8,128)(2,1)}, f32[512,768]{1,0:T(8,128)S(1)}, f32[512,192]{1,0:T(8,128)S(1)}, bf16[512,7...) custom-call(s32[9]{0:T(128)S(1)} %copy-done, ...), custom_call_target="tpu_custom_call" | custom-call | flops 17600000000 | bytes 12991524 | tf_op jit(solution)/shard_map/pallas_call | solution.py:223
  30.2 8.4 %shard_map.274 = (bf16[1536,768]{1,0:T(8,128)(2,1)S(1)}, bf16[1792,768]{1,0:T(8,128)(2,1)S(1)}, f32[512,768]{1,0:T(8,128)S(1)}, f32[512,192]{1,0:T(8,128)S(1)}) custom-call(s32[9]{0:T(128)S(1)} %copy-done, bf16[512,1536]{1,0:T(8,128)(2,1)S(1)} %get-tuple-element.126.refs_1_, bf16[512,768]{1,0:T(8,128)(2,1)S(1)} %get-tuple-element.140.refs_2_.refs_0_, ...), custom_call_target="tpu_custom_call" | custom-call | flops 8800000000 | bytes 12877860 | tf_op jit(solution)/shard_map/pallas_call | solution.py:223
  40.0 2.9 %collective-permute-start.7 = (bf16[768,768]{1,0:T(8,128)(2,1)}, bf16[768,768]{1,0:T(8,128)(2,1)S(1)}, u32[]{:S(2)}, u32[]{:S(2)}) collective-permute-start(bf16[768,768]{1,0:T(8,128)(2,1)} %get-tuple-element.225), channel_id=1, source_target_pairs={{0,2},{1,5},{2,0},{3,7},{4,6},{5,1},{6,4},{7,3},{8,10},{9,13},{10,... | collective-permute-start | bytes 3538952 | tf_op jit(solution)/shard_map/ppermute | solution.py:565
  42.9 5.4 %shard_map.275 = (bf16[1792,768]{1,0:T(8,128)(2,1)S(1)}, f32[512,768]{1,0:T(8,128)S(1)}, f32[512,192]{1,0:T(8,128)S(1)}) custom-call(s32[9]{0:T(128)S(1)} %copy-done, bf16[512,768]{1,0:T(8,128)(2,1)S(1)} %get-tuple-element.140.refs_2_.refs_0_, bf16[512,192]{1,0:T(8,128)(2,1)S(1)} %get-tuple-element.128.refs_3_.refs_1_, ...), custom_call_target="tpu_custom_call" | custom-call | flops 5500000256 | bytes 11304996 | tf_op jit(solution)/shard_map/pallas_call | solution.py:223
  50.4 2.9 %shard_map.276 = (bf16[3328,768]{1,0:T(8,128)(2,1)S(1)}, f32[512,768]{1,0:T(8,128)S(1)}, f32[512,192]{1,0:T(8,128)S(1)}, bf16[512,768]{1,0:T(8,128)(2,1)S(1)}, b...) custom-call(s32[9]{0:T(128)S(1)} %copy-done, ...), custom_call_target="tpu_custom_call" | custom-call | flops 4400000000 | bytes 6453796 | tf_op jit(solution)/shard_map/pallas_call | solution.py:223
  53.3 9.2 %shard_map.277 = (bf16[512,2304]{1,0:T(8,128)(2,1)S(1)}, f32[512,768]{1,0:T(8,128)S(1)}) custom-call(s32[2]{0:T(128)S(1)} %iota_multiply_fusion.span_ref, s32[1]{0:T(128)S(6)} %copy.45.count_ref, bf16[512,2304]{1,0:T(8,128)(2,1)S(1)} %get-tuple-element.120.qkv_t, bf16[512,768]{1,0:T(8,128)(2,1)S(1)} %copy-done.17, ...), custom_call_target="tpu_custom_call", output_to_operand_aliasing={{0}: (7, {}), {1}: (8, {})} | custom-call | flops 9900000256 | bytes 8388620 | tf_op jit(solution)/shard_map/pallas_call | solution.py:223
  62.6 9.4 %shard_map.278 = (bf16[512,2304]{1,0:T(8,128)(2,1)S(1)}, f32[512,768]{1,0:T(8,128)S(1)}) custom-call(s32[2]{0:T(128)S(1)} %copy-done.15, s32[1]{0:T(128)S(6)} %copy.45.count_ref, bf16[512,2304]{1,0:T(8,128)(2,1)S(1)} %get-tuple-element.120.qkv_t, bf16[512,768]{1,0:T(8,128)(2,1)S(1)} %copy-done.17, ...), custom_call_target="tpu_custom_call", output_to_operand_aliasing={{0}: (7, {}), {1}: (8, {})} | custom-call | flops 9900000256 | bytes 8388620 | tf_op jit(solution)/shard_map/pallas_call | solution.py:223
  73.3 3.2 %shard_map.279 = (bf16[3328,768]{1,0:T(8,128)(2,1)S(1)}, bf16[512,576]{1,0:T(8,128)(2,1)S(1)}) custom-call(s32[9]{0:T(128)S(1)} %copy-done, bf16[1,512,768]{2,1,0:T(8,128)(2,1)S(1)} %copy-done.6, bf16[1,192,512]{2,1,0:T(8,128)(2,1)S(1)} %bitcast.20, bf16[512,2304]{1,0:T(8,128)(2,1)S(1)} %get-tuple-element.161.djoint_t, ...), custom_call_target="tpu_custom_call", output_to_operand_aliasing={{0}: (7, {})} | custom-call | flops 3300000000 | bytes 10199076 | tf_op jit(solution)/shard_map/pallas_call | solution.py:223
  79.0 3.5 %shard_map.280 = (f32[512,768]{1,0:T(8,128)}, f32[192,512]{1,0:T(8,128)}) custom-call(bf16[512,2304]{1,0:T(8,128)(2,1)S(1)} %get-tuple-element.161.djoint_t, bf16[512,576]{1,0:T(8,128)(2,1)S(1)} %get-tuple-element.169.djoint_l, bf16[768,2304]{1,0:T(8,128)(2,1)S(1)} %copy-done.1, bf16[192,576]{1,0:T(8,128)(2,1)S(1)} %copy-done.7, ...), custom_call_target="tpu_custom_call" | custom-call | flops 3300000000 | bytes 8675328 | tf_op jit(solution)/shard_map/pallas_call | solution.py:223
  82.5 4.3 %collective-permute-done.9 = bf16[384,768]{1,0:T(8,128)(2,1)S(1)} collective-permute-done((bf16[384,768]{1,0:T(8,128)(2,1)S(1)}, bf16[384,768]{1,0:T(8,128)(2,1)S(1)}, u32[]{:S(2)}, u32[]{:S(2)}) %collective-permute-start.9) | collective-permute-done | bytes 589856 | tf_op jit(solution)/shard_map/ppermute | solution.py:565
  89.9 9.3 %collective-permute-done.11 = bf16[448,768]{1,0:T(8,128)(2,1)S(1)} collective-permute-done((bf16[448,768]{1,0:T(8,128)(2,1)S(1)}, bf16[448,768]{1,0:T(8,128)(2,1)S(1)}, u32[]{:S(2)}, u32[]{:S(2)}) %collective-permute-start.11) | collective-permute-done | bytes 688160 | tf_op jit(solution)/shard_map/ppermute | solution.py:565
  106.8 7.2 %collective-permute-done.15 = bf16[384,768]{1,0:T(8,128)(2,1)S(1)} collective-permute-done((bf16[384,768]{1,0:T(8,128)(2,1)S(1)}, bf16[384,768]{1,0:T(8,128)(2,1)S(1)}, u32[]{:S(2)}, u32[]{:S(2)}) %collective-permute-start.15) | collective-permute-done | bytes 589856 | tf_op jit(solution)/shard_map/ppermute | solution.py:565
  123.1 8.6 %collective-permute-done.14 = bf16[224,768]{1,0:T(8,128)(2,1)S(1)} collective-permute-done((bf16[224,768]{1,0:T(8,128)(2,1)S(1)}, bf16[224,768]{1,0:T(8,128)(2,1)S(1)}, u32[]{:S(2)}, u32[]{:S(2)}) %collective-permute-start.14) | collective-permute-done | bytes 344096 | tf_op jit(solution)/shard_map/ppermute | solution.py:565
  140.4 4.2 %collective-permute-done.22 = bf16[96,768]{1,0:T(8,128)(2,1)S(1)} collective-permute-done((bf16[96,768]{1,0:T(8,128)(2,1)S(1)}, bf16[96,768]{1,0:T(8,128)(2,1)S(1)}, u32[]{:S(2)}, u32[]{:S(2)}) %collective-permute-start.22) | collective-permute-done | bytes 147488 | tf_op jit(solution)/shard_map/ppermute | solution.py:565
  146.9 3.0 %collective-permute-done.26 = bf16[96,768]{1,0:T(8,128)(2,1)S(1)} collective-permute-done((bf16[96,768]{1,0:T(8,128)(2,1)S(1)}, bf16[96,768]{1,0:T(8,128)(2,1)S(1)}, u32[]{:S(2)}, u32[]{:S(2)}) %collective-permute-start.26) | collective-permute-done | bytes 147488 | tf_op jit(solution)/shard_map/ppermute | solution.py:565
  152.0 6.5 %collective-permute-done.25 = bf16[112,768]{1,0:T(8,128)(2,1)S(1)} collective-permute-done((bf16[112,768]{1,0:T(8,128)(2,1)S(1)}, bf16[112,768]{1,0:T(8,128)(2,1)S(1)}, u32[]{:S(2)}, u32[]{:S(2)}) %collective-permute-start.25) | collective-permute-done | bytes 172064 | tf_op jit(solution)/shard_map/ppermute | solution.py:565
  158.8 4.8 %collective-permute-done.28 = bf16[384,768]{1,0:T(8,128)(2,1)S(1)} collective-permute-done((bf16[384,768]{1,0:T(8,128)(2,1)S(1)}, bf16[384,768]{1,0:T(8,128)(2,1)S(1)}, u32[]{:S(2)}, u32[]{:S(2)}) %collective-permute-start.28) | collective-permute-done | bytes 589856 | tf_op jit(solution)/shard_map/ppermute | solution.py:565
  171.4 3.5 %shard_map.282 = (f32[768,2304]{1,0:T(8,128)}, f32[768,768]{1,0:T(8,128)}, f32[8,128]{1,0:T(8,128)}) custom-call(s32[9]{0:T(128)S(1)} %copy-done, bf16[448,768]{1,0:T(8,128)(2,1)S(1)} %pad_maximum_fusion.3.refs_0_, bf16[384,768]{1,0:T(8,128)(2,1)S(1)} %pad_maximum_fusion.5.refs_1_.refs_2_, bf16[448,768]{1,0:T(8,128)(2,1)S(1)} %collective-permute-done.34.refs_2_.refs_4_, ...), custom_call_target="tpu_custom_call" | custom-call | flops 3300000000 | bytes 2555940 | tf_op jit(solution)/shard_map/pallas_call | solution.py:223
  174.9 5.1 %collective-permute-done.33.refs_1_ = bf16[768,768]{1,0:T(8,128)(2,1)S(1)} collective-permute-done((bf16[768,768]{1,0:T(8,128)(2,1)S(1)}, bf16[768,768]{1,0:T(8,128)(2,1)S(1)}, u32[]{:S(2)}, u32[]{:S(2)}) %collective-permute-start.33) | collective-permute-done | bytes 1179680 | tf_op jit(solution)/shard_map/ppermute | solution.py:565
  180.0 3.1 %shard_map.281 = f32[1536,768]{1,0:T(8,128)} custom-call(s32[9]{0:T(128)S(1)} %copy-done, bf16[768,768]{1,0:T(8,128)(2,1)S(1)} %pad_maximum_fusion.1.refs_0_, bf16[768,768]{1,0:T(8,128)(2,1)S(1)} %collective-permute-done.33.refs_1_), custom_call_target="tpu_custom_call" | custom-call | flops 3300000000 | bytes 2359332 | tf_op jit(solution)/shard_map/pallas_call | solution.py:223
  183.1 10.6 %collective-permute-done.32.refs_3_ = bf16[384,768]{1,0:T(8,128)(2,1)S(1)} collective-permute-done((bf16[384,768]{1,0:T(8,128)(2,1)S(1)}, bf16[384,768]{1,0:T(8,128)(2,1)S(1)}, u32[]{:S(2)}, u32[]{:S(2)}) %collective-permute-start.32) | collective-permute-done | bytes 589856 | tf_op jit(solution)/shard_map/ppermute | solution.py:565
  195.6 3.7 %shard_map.284 = (f32[768,1536]{1,0:T(8,128)}, f32[192,384]{1,0:T(8,128)}, f32[192,384]{1,0:T(8,128)}) custom-call(s32[9]{0:T(128)S(1)} %copy-done, bf16[896,768]{1,0:T(8,128)(2,1)S(1)} %pad_maximum_fusion.refs_0_, bf16[896,768]{1,0:T(8,128)(2,1)S(1)} %collective-permute-done.38.refs_1_), custom_call_target="tpu_custom_call" | custom-call | flops 3300000000 | bytes 2752548 | tf_op jit(solution)/shard_map/pallas_call | solution.py:223
  199.3 3.8 %shard_map.283 = (f32[768,2304]{1,0:T(8,128)}, f32[768,768]{1,0:T(8,128)}, f32[192,576]{1,0:T(8,128)}, f32[192,192]{1,0:T(8,128)}, f32[4,768]{1,0:T(4,128)}, /*index=5*/f32[4,192]{1,0:T(4,128)}) custom-call(s32[9]{0:T(128)S(1)} %copy-done, bf16[448,768]{1,0:T(8,128)(2,1)S(1)} %pad_maximum_fusion.3.refs_0_, ...), custom_call_target="tpu_custom_call", output_to_operand_aliasing={{0}: (9, {}), {1}: (10, {})} | custom-call | flops 3300000000 | bytes 14549028 | tf_op jit(solution)/shard_map/pallas_call | solution.py:223
  (134 shorter events, 52.8 us)
Async XLA Ops:
  0.6 16.7 %collective-permute-start = (bf16[768,1536]{1,0:T(8,128)(2,1)}, bf16[768,1536]{1,0:T(8,128)(2,1)S(1)}, u32[]{:S(2)}, u32[]{:S(2)}) collective-permute-start(bf16[768,1536]{1,0:T(8,128)(2,1)} %refs_9_.1), channel_id=1, source_target_pairs={{0,1},{1,0},{2,3},{3,2},{4,5},{5,4},{6,7},{7,6},{8,9},{9,8},{10,11... | collective-permute-start | bytes 7077896 | tf_op jit(solution)/shard_map/ppermute | solution.py:565
  1.2 16.2 %collective-permute-start.1 = (bf16[1536,768]{1,0:T(8,128)(2,1)}, bf16[1536,768]{1,0:T(8,128)(2,1)}, u32[]{:S(2)}, u32[]{:S(2)}) collective-permute-start(bf16[1536,768]{1,0:T(8,128)(2,1)} %refs_4_.3), channel_id=1, source_target_pairs={{0,1},{1,0},{2,3},{3,2},{4,5},{5,4},{6,7},{7,6},{8,9},{9,8},{10,11... | collective-permute-start | bytes 7077896 | tf_op jit(solution)/shard_map/ppermute | solution.py:565
  1.2 16.1 %collective-permute-start.2 = (bf16[192,384]{1,0:T(8,128)(2,1)}, bf16[192,384]{1,0:T(8,128)(2,1)S(1)}, u32[]{:S(2)}, u32[]{:S(2)}) collective-permute-start(bf16[192,384]{1,0:T(8,128)(2,1)} %refs_10_.1), channel_id=1, source_target_pairs={{0,1},{1,0},{2,3},{3,2},{4,5},{5,4},{6,7},{7,6},{8,9},{9,8},{10,11... | collective-permute-start | bytes 442376 | tf_op jit(solution)/shard_map/ppermute | solution.py:565
  1.7 15.6 %collective-permute-start.3 = (bf16[192,384]{1,0:T(8,128)(2,1)}, bf16[192,384]{1,0:T(8,128)(2,1)S(1)}, u32[]{:S(2)}, u32[]{:S(2)}) collective-permute-start(bf16[192,384]{1,0:T(8,128)(2,1)} %bitcast.21), channel_id=1, source_target_pairs={{0,1},{1,0},{2,3},{3,2},{4,5},{5,4},{6,7},{7,6},{8,9},{9,8},{10,11... | collective-permute-start | bytes 442376 | tf_op jit(solution)/shard_map/ppermute | solution.py:565
  40.0 32.0 %collective-permute-start.7 = (bf16[768,768]{1,0:T(8,128)(2,1)}, bf16[768,768]{1,0:T(8,128)(2,1)S(1)}, u32[]{:S(2)}, u32[]{:S(2)}) collective-permute-start(bf16[768,768]{1,0:T(8,128)(2,1)} %get-tuple-element.225), channel_id=1, source_target_pairs={{0,2},{1,5},{2,0},{3,7},{4,6},{5,1},{6,4},{7,3},{8,10},{9,13},{10,... | collective-permute-start | bytes 3538952 | tf_op jit(solution)/shard_map/ppermute | solution.py:565
  48.8 23.3 %collective-permute-start.6 = (bf16[896,768]{1,0:T(8,128)(2,1)S(1)}, bf16[896,768]{1,0:T(8,128)(2,1)S(1)}, u32[]{:S(2)}, u32[]{:S(2)}) collective-permute-start(bf16[896,768]{1,0:T(8,128)(2,1)S(1)} %get-tuple-element.223), channel_id=1, source_target_pairs={{0,4},{1,9},{2,6},{3,11},{4,0},{5,13},{6,2},{7,15},{8,12},{9,1},{1... | collective-permute-start | bytes 4128776 | tf_op jit(solution)/shard_map/ppermute | solution.py:565
  76.8 11.2 %collective-permute-start.8 = (bf16[1664,768]{1,0:T(8,128)(2,1)S(1)}, bf16[1664,768]{1,0:T(8,128)(2,1)S(1)}, u32[]{:S(2)}, u32[]{:S(2)}) collective-permute-start(bf16[1664,768]{1,0:T(8,128)(2,1)S(1)} %slice.165), channel_id=1, source_target_pairs={{0,1},{1,0},{2,3},{3,2},{4,5},{5,4},{6,7},{7,6},{8,9},{9,8},{10,11... | collective-permute-start | bytes 7667720 | tf_op jit(solution)/shard_map/ppermute | solution.py:565
  76.9 9.9 %collective-permute-start.9 = (bf16[384,768]{1,0:T(8,128)(2,1)S(1)}, bf16[384,768]{1,0:T(8,128)(2,1)S(1)}, u32[]{:S(2)}, u32[]{:S(2)}) collective-permute-start(bf16[384,768]{1,0:T(8,128)(2,1)S(1)} %get-tuple-element.229), channel_id=1, source_target_pairs={{0,8},{1,3},{2,10},{3,1},{4,12},{5,7},{6,14},{7,5},{8,0},{9,11},{1... | collective-permute-start | bytes 1769480 | tf_op jit(solution)/shard_map/ppermute | solution.py:565
  78.5 20.7 %collective-permute-start.11 = (bf16[448,768]{1,0:T(8,128)(2,1)S(1)}, bf16[448,768]{1,0:T(8,128)(2,1)S(1)}, u32[]{:S(2)}, u32[]{:S(2)}) collective-permute-start(bf16[448,768]{1,0:T(8,128)(2,1)S(1)} %get-tuple-element.227), channel_id=1, source_target_pairs={{0,8},{1,3},{2,10},{3,1},{4,12},{5,7},{6,14},{7,5},{8,0},{9,11},{1... | collective-permute-start | bytes 2064392 | tf_op jit(solution)/shard_map/ppermute | solution.py:565
  86.9 14.5 %collective-permute-start.13 = (bf16[192,768]{1,0:T(8,128)(2,1)S(1)}, bf16[192,768]{1,0:T(8,128)(2,1)S(1)}, u32[]{:S(2)}, u32[]{:S(2)}) collective-permute-start(bf16[192,768]{1,0:T(8,128)(2,1)S(1)} %slice_add_fusion.19), channel_id=1, source_target_pairs={{0,4},{1,9},{2,6},{3,11},{4,0},{5,13},{6,2},{7,15},{8,12},{9,1},{1... | collective-permute-start | bytes 884744 | tf_op jit(solution)/shard_map/ppermute | solution.py:565
  88.2 18.5 %collective-permute-start.10 = (bf16[448,768]{1,0:T(8,128)(2,1)S(1)}, bf16[448,768]{1,0:T(8,128)(2,1)S(1)}, u32[]{:S(2)}, u32[]{:S(2)}) collective-permute-start(bf16[448,768]{1,0:T(8,128)(2,1)S(1)} %get-tuple-element.220), channel_id=1, source_target_pairs={{0,2},{1,9},{2,0},{3,11},{4,6},{5,13},{6,4},{7,15},{8,10},{9,1},{1... | collective-permute-start | bytes 2064392 | tf_op jit(solution)/shard_map/ppermute | solution.py:565
  100.4 13.6 %collective-permute-start.15 = (bf16[384,768]{1,0:T(8,128)(2,1)S(1)}, bf16[384,768]{1,0:T(8,128)(2,1)S(1)}, u32[]{:S(2)}, u32[]{:S(2)}) collective-permute-start(bf16[384,768]{1,0:T(8,128)(2,1)S(1)} %get-tuple-element.219), channel_id=1, source_target_pairs={{0,2},{1,5},{2,0},{3,7},{4,6},{5,1},{6,4},{7,3},{8,10},{9,13},{10,... | collective-permute-start | bytes 1769480 | tf_op jit(solution)/shard_map/ppermute | solution.py:565
  101.4 19.0 %collective-permute-start.17 = (bf16[192,768]{1,0:T(8,128)(2,1)S(1)}, bf16[192,768]{1,0:T(8,128)(2,1)S(1)}, u32[]{:S(2)}, u32[]{:S(2)}) collective-permute-start(bf16[192,768]{1,0:T(8,128)(2,1)S(1)} %fusion.1), channel_id=1, source_target_pairs={{0,16},{1,17},{2,18},{3,19},{4,20},{5,21},{6,22},{7,23},{8,24},{9,... | collective-permute-start | bytes 884744 | tf_op jit(solution)/shard_map/ppermute | solution.py:565
  115.2 16.6 %collective-permute-start.14 = (bf16[224,768]{1,0:T(8,128)(2,1)S(1)}, bf16[224,768]{1,0:T(8,128)(2,1)S(1)}, u32[]{:S(2)}, u32[]{:S(2)}) collective-permute-start(bf16[224,768]{1,0:T(8,128)(2,1)S(1)} %get-tuple-element.230), channel_id=1, source_target_pairs={{0,8},{1,3},{2,10},{3,1},{4,12},{5,7},{6,14},{7,5},{8,0},{9,11},{1... | collective-permute-start | bytes 1032200 | tf_op jit(solution)/shard_map/ppermute | solution.py:565
  117.1 15.8 %collective-permute-start.20 = (bf16[224,768]{1,0:T(8,128)(2,1)S(1)}, bf16[224,768]{1,0:T(8,128)(2,1)S(1)}, u32[]{:S(2)}, u32[]{:S(2)}) collective-permute-start(bf16[224,768]{1,0:T(8,128)(2,1)S(1)} %fusion), channel_id=1, source_target_pairs={{0,16},{1,17},{2,18},{3,19},{4,20},{5,21},{6,22},{7,23},{8,24},{9,... | collective-permute-start | bytes 1032200 | tf_op jit(solution)/shard_map/ppermute | solution.py:565
  120.5 19.8 %collective-permute-start.23 = (bf16[192,768]{1,0:T(8,128)(2,1)S(1)}, bf16[192,768]{1,0:T(8,128)(2,1)S(1)}, u32[]{:S(2)}, u32[]{:S(2)}) collective-permute-start(bf16[192,768]{1,0:T(8,128)(2,1)S(1)} %add.164), channel_id=1, source_target_pairs={{0,4},{1,9},{2,6},{3,11},{4,0},{5,13},{6,2},{7,15},{8,12},{9,1},{1... | collective-permute-start | bytes 884744 | tf_op jit(solution)/shard_map/ppermute | solution.py:565
  121.7 12.8 %collective-permute-start.19 = (bf16[96,768]{1,0:T(8,128)(2,1)S(1)}, bf16[96,768]{1,0:T(8,128)(2,1)S(1)}, u32[]{:S(2)}, u32[]{:S(2)}) collective-permute-start(bf16[96,768]{1,0:T(8,128)(2,1)S(1)} %slice_add_fusion.23), channel_id=1, source_target_pairs={{0,8},{1,9},{2,10},{3,11},{4,12},{5,13},{6,14},{7,15},{8,0},{9,1},... | collective-permute-start | bytes 442376 | tf_op jit(solution)/shard_map/ppermute | solution.py:565
  134.5 10.1 %collective-permute-start.22 = (bf16[96,768]{1,0:T(8,128)(2,1)S(1)}, bf16[96,768]{1,0:T(8,128)(2,1)S(1)}, u32[]{:S(2)}, u32[]{:S(2)}) collective-permute-start(bf16[96,768]{1,0:T(8,128)(2,1)S(1)} %fusion.3), channel_id=1, source_target_pairs={{0,16},{1,17},{2,18},{3,19},{4,20},{5,21},{6,22},{7,23},{8,24},{9,... | collective-permute-start | bytes 442376 | tf_op jit(solution)/shard_map/ppermute | solution.py:565
  144.8 14.0 %collective-permute-start.29 = (bf16[448,768]{1,0:T(8,128)(2,1)S(1)}, bf16[448,768]{1,0:T(8,128)(2,1)S(1)}, u32[]{:S(2)}, u32[]{:S(2)}) collective-permute-start(bf16[448,768]{1,0:T(8,128)(2,1)S(1)} %pad_maximum_fusion.2), channel_id=1, source_target_pairs={{0,8},{1,3},{2,10},{3,1},{4,12},{5,7},{6,14},{7,5},{8,0},{9,11},{1... | collective-permute-start | bytes 2064392 | tf_op jit(solution)/shard_map/ppermute | solution.py:565
  146.8 16.8 %collective-permute-start.28 = (bf16[384,768]{1,0:T(8,128)(2,1)S(1)}, bf16[384,768]{1,0:T(8,128)(2,1)S(1)}, u32[]{:S(2)}, u32[]{:S(2)}) collective-permute-start(bf16[384,768]{1,0:T(8,128)(2,1)S(1)} %pad_maximum_fusion.4), channel_id=1, source_target_pairs={{0,8},{1,3},{2,10},{3,1},{4,12},{5,7},{6,14},{7,5},{8,0},{9,11},{1... | collective-permute-start | bytes 1769480 | tf_op jit(solution)/shard_map/ppermute | solution.py:565
  163.7 16.3 %collective-permute-start.33 = (bf16[768,768]{1,0:T(8,128)(2,1)S(1)}, bf16[768,768]{1,0:T(8,128)(2,1)S(1)}, u32[]{:S(2)}, u32[]{:S(2)}) collective-permute-start(bf16[768,768]{1,0:T(8,128)(2,1)S(1)} %pad_maximum_fusion.1.refs_0_), channel_id=1, source_target_pairs={{0,2},{1,5},{2,0},{3,7},{4,6},{5,1},{6,4},{7,3},{8,10},{9,13},{10,... | collective-permute-start | bytes 3538952 | tf_op jit(solution)/shard_map/ppermute | solution.py:565
  167.9 27.6 %collective-permute-start.38 = (bf16[896,768]{1,0:T(8,128)(2,1)S(1)}, bf16[896,768]{1,0:T(8,128)(2,1)S(1)}, u32[]{:S(2)}, u32[]{:S(2)}) collective-permute-start(bf16[896,768]{1,0:T(8,128)(2,1)S(1)} %pad_maximum_fusion.refs_0_), channel_id=1, source_target_pairs={{0,4},{1,9},{2,6},{3,11},{4,0},{5,13},{6,2},{7,15},{8,12},{9,1},{1... | collective-permute-start | bytes 4128776 | tf_op jit(solution)/shard_map/ppermute | solution.py:565
  168.8 24.8 %collective-permute-start.31 = (bf16[448,768]{1,0:T(8,128)(2,1)S(1)}, bf16[448,768]{1,0:T(8,128)(2,1)S(1)}, u32[]{:S(2)}, u32[]{:S(2)}) collective-permute-start(bf16[448,768]{1,0:T(8,128)(2,1)S(1)} %pad_maximum_fusion.3.refs_0_), channel_id=1, source_target_pairs={{0,2},{1,9},{2,0},{3,11},{4,6},{5,13},{6,4},{7,15},{8,10},{9,1},{1... | collective-permute-start | bytes 2064392 | tf_op jit(solution)/shard_map/ppermute | solution.py:565
  170.4 23.3 %collective-permute-start.32 = (bf16[384,768]{1,0:T(8,128)(2,1)S(1)}, bf16[384,768]{1,0:T(8,128)(2,1)S(1)}, u32[]{:S(2)}, u32[]{:S(2)}) collective-permute-start(bf16[384,768]{1,0:T(8,128)(2,1)S(1)} %pad_maximum_fusion.5.refs_1_.refs_2_), channel_id=1, source_target_pairs={{0,2},{1,5},{2,0},{3,7},{4,6},{5,1},{6,4},{7,3},{8,10},{9,13},{10,... | collective-permute-start | bytes 1769480 | tf_op jit(solution)/shard_map/ppermute | solution.py:565
  (33 other events, 257.7 us)
